TPU v7x, 128 devices: a whole 4x4x4 slice. The times are simulated.
128 devices in a mesh: pipe: 2 (over core), dom: 64 (over y, z, x).
Axes of the slice: x: 4, y: 4, z: 4, core: 2. Of those that a mesh axis runs over, the one named last changes fastest.
Arguments:
- node_in: bfloat16 [2, 2, 12288, 512], P('pipe', None, 'dom'), may hold values from -6 to 6
- edge_in: bfloat16 [2, 2, 49152, 512], P('pipe', None, 'dom'), may hold values from -6 to 6
- cot_node: bfloat16 [2, 12288, 512], P(None, 'dom'), may hold values from -6 to 6
- cot_edge: bfloat16 [2, 49152, 512], P(None, 'dom'), may hold values from -6 to 6
- node_count: int32 [64], P('dom'), may hold values from 96 to 192, as said below
- edge_count: int32 [64], P('dom'), may hold values from 1 to 768, as said below
- edge_source: int32 [49152], P('dom'), may hold values from 0 to 319, as said below
- edge_target: int32 [49152], P('dom'), may hold values from 0 to 191, as said below
- halo_send: int32 [64, 64, 2], P('dom'), may hold values from 0 to 191, as said below
- hang_send: int32 [64, 64, 2], P('dom'), may hold values from 0 to 192, as said below
- parent_rows: int32 [64, 64, 2], P('dom'), may hold values from 0 to 192, as said below
- w_edge_in: bfloat16 [2, 1536, 512], P('pipe'), may hold values from -0.15625 to 0.15625
- w_edge_mid: bfloat16 [2, 2, 512, 512], P('pipe'), may hold values from -0.25 to 0.25
- edge_bias: float32 [2, 4, 512], P('pipe'), may hold values from -1.8 to 1.8
- edge_gain: float32 [2, 512], P('pipe'), may hold values from 0.5 to 1.5
- w_node_in: bfloat16 [2, 1024, 512], P('pipe'), may hold values from -0.1875 to 0.1875
- w_node_mid: bfloat16 [2, 2, 512, 512], P('pipe'), may hold values from -0.25 to 0.25
- node_bias: float32 [2, 4, 512], P('pipe'), may hold values from -1.8 to 1.8
- node_gain: float32 [2, 512], P('pipe'), may hold values from 0.5 to 1.5
Outputs:
- grad_node_in: bfloat16 [2, 2, 12288, 512], P('pipe', None, 'dom')
- grad_edge_in: bfloat16 [2, 2, 49152, 512], P('pipe', None, 'dom')
- grad_w_edge_in: float32 [2, 1536, 512], P('pipe', 'dom')
- grad_w_edge_mid: float32 [2, 2, 512, 512], P('pipe', None, 'dom')
- grad_edge_bias: float32 [2, 4, 512], P('pipe', None, 'dom')
- grad_edge_gain: float32 [2, 512], P('pipe', 'dom')
- grad_w_node_in: float32 [2, 1024, 512], P('pipe', 'dom')
- grad_w_node_mid: float32 [2, 2, 512, 512], P('pipe', None, 'dom')
- grad_node_bias: float32 [2, 4, 512], P('pipe', None, 'dom')
- grad_node_gain: float32 [2, 512], P('pipe', 'dom')
Inputs may be any that keep to these rules, and one draw needn't show every extreme that they name: Partition p has node_count[p] live node rows; some partition is full. Partition p has edge_count[p] live edge rows; some partition is full. `edge_source`: each edge's source is a live node row of its partition or 192 + k, the k-th received row of its partition. `edge_target`: each edge's target is a live node row of its partition. halo_send[p, q, :] are live rows of partition p. hang_send[p, q, 0] == hang_send[p, q, 1]: a live row of partition p hanging on an edge of partition q, or 192 for none; a row hangs for at most one q, and no hanging row is a parent. parent_rows[q, p, :] are two different live rows of partition q, or both 192 where hang_send[p, q, 0] is 192.
All inputs are finite; a program needn't handle non-finite values.
Results may differ from a plain program's by a relative error of at most 0.015.
Values may be sent and summed in bfloat16 or wider, within the bound.
No kernel may reach another device: no remote copies, remote signals or barrier semaphores. Data moves between devices by JAX's collectives and lax.ppermute only.
A program may use at most 192 MiB of HBM per device.

v0:
```python
import functools

import jax
import jax.numpy as jnp
from jax import lax
from jax.experimental import pallas as pl
from jax.experimental.pallas import tpu as pltpu
from jax.sharding import PartitionSpec as P

EPS = 1e-05
BF = jnp.bfloat16
F32 = jnp.float32
BLOCK = 256


def dot(a, b):
    return lax.dot_general(a, b, (((1,), (0,)), ((), ())), preferred_element_type=F32)


def dot_t0(a, b):
    return lax.dot_general(a, b, (((0,), (0,)), ((), ())), preferred_element_type=F32)


def dot_t1(a, b):
    return lax.dot_general(a, b, (((1,), (1,)), ((), ())), preferred_element_type=F32)


def hot_rows(index_row, rows):
    grid = lax.broadcasted_iota(jnp.int32, (rows, index_row.shape[1]), 0)
    return jnp.where(grid == index_row, 1.0, 0.0)


def spread_rows(per):
    row = lax.broadcasted_iota(jnp.int32, (8 * per, 4 * per), 0)
    col = lax.broadcasted_iota(jnp.int32, (8 * per, 4 * per), 1)
    return jnp.where(col == (row & 7) * per + (row >> 3), 1.0, 0.0).astype(BF)


def act(value):
    sig = 0.5 * jnp.tanh(0.5 * value) + 0.5
    out = value * sig
    return out.astype(BF), sig + out * (1.0 - sig)


def norm_rows(value):
    centred = value - jnp.mean(value, axis=-1, keepdims=True)
    inv = lax.rsqrt(jnp.mean(centred * centred, axis=-1, keepdims=True) + EPS)
    return centred * inv, inv


def norm_back(grad, gain, normed, inv):
    scaled = grad * gain
    return inv * (
        scaled
        - jnp.mean(scaled, axis=-1, keepdims=True)
        - normed * jnp.mean(scaled * normed, axis=-1, keepdims=True)
    )


def col_sum(value):
    return jnp.sum(value, axis=0, keepdims=True)


def pre_kernel(core, idx, own_all, rec_all, cot_all, out, ownb, recv, cotb, sems):
    c = core[0]
    cp = [
        pltpu.make_async_copy(own_all.at[0, c], ownb, sems.at[0]),
        pltpu.make_async_copy(cot_all.at[c], cotb, sems.at[1]),
        pltpu.make_async_copy(rec_all.at[0, c], recv, sems.at[2]),
    ]
    for one in cp:
        one.start()
    rows = ownb.shape[0]
    h0 = hot_rows(idx[0:1, :], rows).astype(BF)
    h1 = hot_rows(idx[1:2, :], rows).astype(BF)
    hg = hot_rows(idx[2:3, :], rows).astype(BF)
    for one in cp:
        one.wait()
    own, other = ownb[...], recv[...]
    low = jnp.where(c == 0, own.astype(F32), other.astype(F32)).astype(BF)
    top = jnp.where(c == 0, other.astype(F32), own.astype(F32)).astype(BF)
    for k, (hot, rows_of) in enumerate(((h0, low), (h1, low), (h0, top), (h1, top), (hg, cotb[...]))):
        out[k] = dot_t0(hot, rows_of).astype(BF)


def post_kernel(idx, local, back, node_out, hang_out):
    rows = local.shape[0]
    total = local[...]
    for s in range(2):
        total = total + dot(hot_rows(idx[s : s + 1, :], rows).astype(BF), back[s])
    low = total.astype(BF)
    node_out[...] = low
    hang = dot_t0(hot_rows(idx[2:3, :], rows).astype(BF), low).astype(BF)
    half = hang.shape[1] // 2
    hang_out[0] = hang[:, :half]
    hang_out[1] = hang[:, half:]


def sum_kernel(idx, local, came, part_out, node_out):
    per = came.shape[0]
    part_out[...] = jnp.sum(came[:, 0:80, :].astype(F32), axis=0)
    tail = came[:, 80:88, :].astype(F32).reshape(per * 8, came.shape[2]).astype(BF)
    quarters = dot_t0(spread_rows(per), tail).astype(BF)
    rows = local.shape[0]
    total = local[...]
    for s in range(2):
        back = jnp.concatenate(
            [quarters[(s + 2 * k) * per : (s + 2 * k + 1) * per, :] for k in range(2)], axis=1
        )
        total = total + dot(hot_rows(idx[s : s + 1, :], rows).astype(BF), back)
    node_out[...] = total.astype(BF)


def end_kernel(core, p0, p1, r0, r1, n0, n1, m0, m1, node_out, we, wem, wn, wnm):
    def write(left, right, first, second):
        full = jnp.concatenate([left[0:80, :], right[0:80, :]], axis=1)
        node_out[0, 0] = first[...]
        node_out[0, 1] = second[...]
        we[0] = full[0:24, :]
        wem[0, 0] = full[32:40, :]
        wem[0, 1] = full[40:48, :]
        wn[0] = full[48:64, :]
        wnm[0, 0] = full[64:72, :]
        wnm[0, 1] = full[72:80, :]

    @pl.when(core[0] == 0)
    def _():
        write(p0, r0, n0, m0)

    @pl.when(core[0] == 1)
    def _():
        write(r1, p1, m1, n1)


SAVED = 14


def unit_kernel(mode, layer, *refs):
    take = iter(refs)

    def some(n):
        return [next(take) for _ in range(n)]

    forward_part, backward_part = "F" in mode, "B" in mode
    scal, idx, erow, ecol, got = some(5)
    per = got.shape[1]
    inc_of = lambda: jnp.concatenate([got[2 * layer], got[2 * layer + 1]], axis=0)
    hang_in = next(take) if mode == "B" else None
    own_nodes, own_edges, *own_rest = some(7)
    recs = some(7)
    gout_all, gedge_all = some(2) if backward_part else (None, None)
    kept_in = some(SAVED) if mode == "B" else None
    saved = some(SAVED) if mode == "F" else None
    if backward_part:
        local_ref, edge_ref, keep_ref, send_ref = some(4)
        back_ref = next(take) if mode == "FB" else None
    dsts = some(7)
    nodes, edges, w1, wm, n1, nm, vec = dsts
    if mode != "F":
        saved = some(SAVED)
    oh, a1, a2, s1, s2, nrm, inv, _, _, _, _, _, _, _ = saved
    q, msg, gout, gedge, l1, l2, l3, gag, bsum, sems = some(10)

    is_own, c, node_count, edge_count, gi = (scal[i] for i in range(5))
    owns = [own_nodes.at[0, c], own_edges.at[0, c]] + [r.at[0] for r in own_rest[:4]]
    owns = owns + [own_rest[4]]
    recs = [recs[0].at[0, c], recs[1].at[0, c]] + recs[2:]
    order = [6, 0, 2, 1, 3, 4, 5] if forward_part else [6, 0, 5, 4, 3, 2, 1]
    if backward_part:
        cg = pltpu.make_async_copy(gout_all.at[gi], gout, sems.at[7])
        ce = pltpu.make_async_copy(gedge_all.at[gi], gedge, sems.at[8])
    loads = []
    if mode == "B":
        loads = [
            pltpu.make_async_copy(kept_in[k], saved[k], sems.at[9 + k]) for k in range(SAVED)
        ]
        cg.start()
        for k in range(7, SAVED):
            loads[k].start()

    @pl.when(is_own == 1)
    def _():
        for k in order:
            pltpu.make_async_copy(owns[k], dsts[k], sems.at[k]).start()

    @pl.when(is_own == 0)
    def _():
        for k in order:
            pltpu.make_async_copy(recs[k], dsts[k], sems.at[k]).start()

    if mode == "B":
        for k in range(7):
            loads[k].start()
    else:
        if backward_part:
            cg.start()
    if backward_part:
        ce.start()

    def ready(k):
        pltpu.make_async_copy(recs[k], dsts[k], sems.at[k]).wait()

    n_rows = nodes.shape[0]
    e_rows = edges.shape[0]
    width = nodes.shape[1]
    blocks = e_rows // BLOCK

    def live_of(start, size, count):
        return (lax.broadcasted_iota(jnp.int32, (size, 1), 0) + start < count).astype(F32)

    ready(6)
    eb = [vec[i : i + 1, :] for i in range(4)]
    eg = vec[4:5, :]
    nb = [vec[i : i + 1, :] for i in range(5, 9)]
    ng = vec[9:10, :]
    to_target = hot_rows(erow[1:2, :], n_rows).astype(BF)

    if forward_part:
        def build(i, _):
            rows = pl.ds(pl.multiple_of(i * BLOCK, BLOCK), BLOCK)
            grid = lax.broadcasted_iota(jnp.int32, (BLOCK, width), 1)
            hit = (grid == ecol[rows, 0:1]) | (grid == ecol[rows, 1:2])
            oh[rows, :] = jnp.where(hit, 1.0, 0.0).astype(BF)
            return 0

        lax.fori_loop(0, blocks, build, 0)
        ready(0)
        ready(2)
        q[0:n_rows, :] = dot(nodes[...], w1[width : 2 * width, :]).astype(BF)
        q[n_rows : 2 * n_rows, :] = dot(nodes[...], w1[0:width, :]).astype(BF)
        q[2 * n_rows :, :] = dot(inc_of(), w1[0:width, :]).astype(BF)
        ready(1)
        ready(3)

        def forward(i, _):
            start = pl.multiple_of(i * BLOCK, BLOCK)
            rows = pl.ds(start, BLOCK)
            z = dot(oh[rows, :], q[...]) + dot(edges[rows, :], w1[2 * width :, :]) + eb[0]
            low, slope = act(z)
            a1[rows, :] = low
            s1[rows, :] = slope
            low, slope = act(dot(low, wm[0]) + eb[1])
            a2[rows, :] = low
            s2[rows, :] = slope
            normed, rstd = norm_rows(dot(low, wm[1]) + eb[2])
            nrm[rows, :] = normed
            inv[rows, :] = rstd
            msg[rows, :] = ((normed * eg + eb[3]) * live_of(start, BLOCK, edge_count)).astype(BF)
            return 0

        lax.fori_loop(0, blocks, forward, 0)

        agg = dot(to_target, msg[...]).astype(BF)
        ready(4)
        ready(5)
        x_n = nodes[...]
        na1, ns1 = act(dot(x_n, n1[0:width, :]) + dot(agg, n1[width:, :]) + nb[0])
        na2, ns2 = act(dot(na1, nm[0]) + nb[1])
        nn, nr = norm_rows(dot(na2, nm[1]) + nb[2])
        for ref, value in zip(saved[7:], (agg, na1, na2, ns1, ns2, nn, nr)):
            ref[...] = value

    if not backward_part:
        return
    if not forward_part:
        ready(0)
        ready(4)
        ready(5)
        for one in loads[7:]:
            one.wait()
    x_n = nodes[...]
    agg, na1, na2, ns1, ns2, nn, nr = (ref[...] for ref in saved[7:])

    def halves(low):
        half = width // 2
        f = low.astype(F32)
        swapped = jnp.concatenate([f[:, half:], f[:, :half]], axis=1)
        return jnp.where(c == 0, f, swapped).astype(BF)

    def put(first, pieces):
        half = width // 2
        tile = jnp.concatenate([x.reshape(64, -1, x.shape[-1]) for x in pieces], axis=1)
        n = tile.shape[1]
        keep_ref[:, first : first + n, :] = tile[:, :, :half].astype(BF)
        send_ref[:, first : first + n, :] = tile[:, :, half:].astype(BF)

    cg.wait()
    hung = jnp.max(
        jnp.where(
            lax.broadcasted_iota(jnp.int32, (n_rows, idx.shape[1]), 0) == idx[2:3, :], 1.0, 0.0
        ),
        axis=1,
        keepdims=True,
    )
    spread = 0.5 * (hot_rows(idx[3:4, :], n_rows) + hot_rows(idx[4:5, :], n_rows))
    if mode == "B":
        from_hanging = jnp.concatenate([hang_in[0], hang_in[1]], axis=1)
    else:
        from_hanging = got[4]
    grad_new = gout[...].astype(F32) * (1.0 - hung) + dot(spread.astype(BF), from_hanging)
    gy = grad_new * live_of(0, n_rows, node_count)
    bsum[8:9, :] = col_sum(gy)
    bsum[9:10, :] = col_sum(gy * nn)
    g3 = norm_back(gy, ng, nn, nr)
    bsum[7:8, :] = col_sum(g3)
    low3 = g3.astype(BF)
    g2 = dot_t1(low3, nm[1]) * ns2
    bsum[6:7, :] = col_sum(g2)
    low2 = g2.astype(BF)
    g1 = dot_t1(low2, nm[0]) * ns1
    bsum[5:6, :] = col_sum(g1)
    low1 = g1.astype(BF)
    direct = grad_new + dot_t1(low1, n1[0:width, :])
    gag[0:n_rows, :] = dot_t1(low1, n1[width:, :]).astype(BF)
    gag[n_rows:, :] = jnp.zeros((gag.shape[0] - n_rows, width), BF)
    low1p = halves(low1)
    put(48, [jnp.concatenate([dot_t0(x_n, low1p), dot_t0(agg, low1p)], axis=0)])
    put(64, [dot_t0(na1, halves(low2)), dot_t0(na2, halves(low3))])

    if not forward_part:
        ready(1)
        ready(2)
        ready(3)
        for one in loads[:7]:
            one.wait()
    ce.wait()
    gk = gag.shape[0]

    def backward(i, carry):
        start = pl.multiple_of(i * BLOCK, BLOCK)
        rows = pl.ds(start, BLOCK)
        c1, c2, c3, c4, c5 = carry
        ge = gedge[rows, :].astype(F32)
        gy = (dot(oh[rows, 0:gk], gag[...]) + ge) * live_of(start, BLOCK, edge_count)
        normed = nrm[rows, :]
        g3 = norm_back(gy, eg, normed, inv[rows, :])
        low = g3.astype(BF)
        l3[rows, :] = halves(low)
        g2 = dot_t1(low, wm[1]) * s2[rows, :]
        low = g2.astype(BF)
        l2[rows, :] = halves(low)
        g1 = dot_t1(low, wm[0]) * s1[rows, :]
        low = g1.astype(BF)
        l1[rows, :] = low
        edge_ref[rows, :] = (ge + dot_t1(low, w1[2 * width :, :])).astype(BF)
        return (
            c1 + col_sum(g1),
            c2 + col_sum(g2),
            c3 + col_sum(g3),
            c4 + col_sum(gy),
            c5 + col_sum(gy * normed),
        )

    zero = jnp.zeros((1, width), F32)
    sums = lax.fori_loop(0, blocks, backward, (zero,) * 5)
    for k in range(5):
        bsum[k : k + 1, :] = sums[k]
    bsum[10:16, :] = jnp.zeros((6, width), F32)

    lowv = l1[...]
    t_sum = dot(to_target, lowv).astype(BF)
    from_source = hot_rows(erow[0:1, :] - n_rows, width - n_rows).astype(BF)
    s_sum = dot(from_source, lowv).astype(BF)
    d_ext = dot_t1(s_sum, w1[0:width, :])
    local_ref[...] = direct + d_ext[0:n_rows, :] + dot_t1(t_sum, w1[width : 2 * width, :])
    d_inc = d_ext[n_rows:, :].astype(BF)
    if mode == "FB":
        for s in range(back_ref.shape[0]):
            back_ref[s] = d_inc[s * per : (s + 1) * per, :]
    else:
        half = width // 2
        quarters = jnp.concatenate([d_inc[:, :half], d_inc[:, half:]], axis=0)
        rows = dot(spread_rows(per), quarters).reshape(per, 8, half)
        keep_ref[:, 80:88, :] = rows.astype(BF)
        send_ref[:, 80:88, :] = jnp.zeros((per, 8, half), BF)
    sp, tp = halves(s_sum), halves(t_sum)
    grad_w1 = jnp.concatenate(
        [
            dot_t0(x_n, sp[0:n_rows, :]) + dot_t0(inc_of(), sp[n_rows:, :]),
            dot_t0(x_n, tp),
            dot_t0(edges[...], halves(lowv)),
        ],
        axis=0,
    )
    groups = []
    for b in range(width // 128):
        cols = slice(b * 128, (b + 1) * 128)
        pair = jnp.concatenate([bsum[0:8, cols], bsum[8:16, cols]], axis=1)
        pair = jnp.concatenate([pair, pair], axis=1)
        groups.append(jnp.broadcast_to(pair[None], (16, 8, width)))
    put(0, [grad_w1, jnp.concatenate(groups, axis=0)])
    put(32, [dot_t0(a1[...], l2[...]), dot_t0(a2[...], l3[...])])


VM = pl.BlockSpec(memory_space=pltpu.VMEM)
SM = pl.BlockSpec(memory_space=pltpu.SMEM)
HB = pl.BlockSpec(memory_space=pl.ANY)


def swap(x):
    return lax.ppermute(x, "pipe", [(0, 1), (1, 0)])


def exchange(x):
    return lax.all_to_all(x, "dom", split_axis=0, concat_axis=0, tiled=True)


def body(
    node_in, edge_in, cot_node, cot_edge, node_count, edge_count, edge_source, edge_target,
    halo_send, hang_send, parent_rows,
    w_edge_in, w_edge_mid, edge_bias, edge_gain, w_node_in, w_node_mid, node_bias, node_gain,
):
    n_rows, width = node_in.shape[2:]
    e_rows = edge_in.shape[2]
    peers = lax.axis_size("dom")
    slots = halo_send.shape[2]
    c = lax.axis_index("pipe")
    p = lax.axis_index("dom")
    half = width // 2

    vec = jnp.concatenate(
        [edge_bias[0], edge_gain, node_bias[0], node_gain, jnp.zeros((6, width), F32)], axis=0
    )
    rec_nodes = swap(node_in)
    rec_edges = swap(edge_in)
    rec_vec = swap(vec)
    rec_w1, rec_wm, rec_n1, rec_nm = (
        swap(w[0]) for w in (w_edge_in, w_edge_mid, w_node_in, w_node_mid)
    )

    hs, gs, ps = halo_send[0], hang_send[0], parent_rows[0]
    idx = jnp.stack([hs[:, 0], hs[:, 1], gs[:, 0], ps[:, 0], ps[:, 1]] + [hs[:, 0]] * 3)
    k = edge_source - n_rows
    source = jnp.where(k < 0, edge_source, n_rows + (k % slots) * peers + k // slots)
    ecol = jnp.stack([edge_target, n_rows + source] + [edge_target] * 6, axis=1)
    erow = jnp.stack([n_rows + source, edge_target] + [edge_target] * 6, axis=0)

    outs = pl.pallas_call(
        pre_kernel,
        out_shape=jax.ShapeDtypeStruct((5, peers, width), BF),
        in_specs=[SM, VM, HB, HB, HB],
        out_specs=VM,
        scratch_shapes=[
            pltpu.VMEM((n_rows, width), BF),
            pltpu.VMEM((n_rows, width), BF),
            pltpu.VMEM((n_rows, width), BF),
            pltpu.SemaphoreType.DMA((3,)),
        ],
        name="pre",
    )(c.reshape(1), idx, node_in, rec_nodes, cot_node)
    got = exchange(jnp.swapaxes(outs, 0, 1))
    got = jnp.swapaxes(got, 0, 1)

    shape = jax.ShapeDtypeStruct
    saved = [shape((e_rows, width), BF)] * 3 + [shape((e_rows, width), F32)] * 3
    saved += [shape((e_rows, 1), F32)]
    saved += [shape((n_rows, width), BF)] * 3 + [shape((n_rows, width), F32)] * 3
    saved += [shape((n_rows, 1), F32)]

    def results(mode):
        chunk = shape((peers, 80 if mode == "FB" else 88, half), BF)
        some = [shape((n_rows, width), F32), shape((e_rows, width), BF), chunk, chunk]
        return some + ([shape((slots, peers, width), BF)] if mode == "FB" else [])

    stages = [
        shape((n_rows, width), BF),
        shape((e_rows, width), BF),
        shape(w_edge_in.shape[1:], BF),
        shape(w_edge_mid.shape[1:], BF),
        shape(w_node_in.shape[1:], BF),
        shape(w_node_mid.shape[1:], BF),
        shape((16, width), F32),
    ]
    work = [
        shape((width, width), BF),
        shape((e_rows, width), BF),
        shape((n_rows, width), BF),
        shape((e_rows, width), BF),
        shape((e_rows, width), BF),
        shape((e_rows, width), BF),
        shape((e_rows, width), BF),
        shape((256, width), BF),
        shape((16, width), F32),
    ]

    def run(mode, layer, hang_l=None, gout=None, gedge=None, gi=0, kept=()):
        own = (c == layer).astype(jnp.int32)
        scal = jnp.stack([own, c, node_count[0], edge_count[0], jnp.int32(gi)]).astype(jnp.int32)
        back = "B" in mode
        arrays = [scal, idx, erow, ecol, got] + ([hang_l] if mode == "B" else [])
        near = len(arrays) - 1
        arrays += [node_in, edge_in, w_edge_in, w_edge_mid, w_node_in, w_node_mid, vec]
        arrays += [rec_nodes, rec_edges, rec_w1, rec_wm, rec_n1, rec_nm, rec_vec]
        arrays += ([gout, gedge] if back else []) + list(kept)
        outs = (saved if mode == "F" else []) + (results(mode) if back else [])
        scratch = stages + ([] if mode == "F" else saved) + work
        return pl.pallas_call(
            functools.partial(unit_kernel, mode, layer),
            out_shape=outs,
            in_specs=[SM] + [VM] * near + [HB] * (len(arrays) - near - 1),
            out_specs=[VM] * len(outs),
            scratch_shapes=[pltpu.VMEM(x.shape, x.dtype) for x in scratch]
            + [pltpu.SemaphoreType.DMA((9 + SAVED,))],
            compiler_params=pltpu.CompilerParams(vmem_limit_bytes=56 * 1024 * 1024),
        )(*arrays)

    post = pl.pallas_call(
        post_kernel,
        out_shape=[shape((n_rows, width), BF), shape((2, peers, half), BF)],
        in_specs=[VM] * 3,
        out_specs=[VM] * 2,
        name="post",
    )

    def give_back(local, back):
        came = exchange(jnp.swapaxes(back, 0, 1))
        return post(idx, local, jnp.swapaxes(came, 0, 1))

    def paired(keep, send):
        return (keep.astype(F32) + swap(send).astype(F32)).astype(BF)

    local1, edge1, keep1, send1, back1 = run("FB", 1, None, cot_node, cot_edge, c)
    kept0 = run("F", 0)
    node1, hang1 = give_back(local1, back1)
    hang_in0 = exchange(jnp.swapaxes(hang1, 0, 1))
    mine1, hang_in0 = lax.optimization_barrier((paired(keep1, send1), hang_in0))
    part1 = jnp.sum(exchange(mine1).astype(F32), axis=0)
    local0, edge0, keep0, send0 = run(
        "B", 0, jnp.swapaxes(hang_in0, 0, 1), node1[None], edge1[None], 0, kept0
    )
    up = [(0, 1)]
    down = [(1, 0)]
    first = c == 0
    came = exchange(paired(keep0, send0))
    part0, node0 = pl.pallas_call(
        sum_kernel,
        out_shape=[shape((80, half), F32), shape((n_rows, width), BF)],
        in_specs=[VM] * 3,
        out_specs=[VM] * 2,
        name="sums",
    )(idx, local0, came)
    lower = lax.ppermute(edge0, "pipe", down)
    upper = lax.ppermute(edge1, "pipe", up)
    edge_final = jnp.where(first, jnp.stack([edge0, lower]), jnp.stack([upper, edge1]))[None]
    r0, m0 = lax.ppermute((part0, node0), "pipe", down)
    r1, m1 = lax.ppermute((part1, node1), "pipe", up)
    node_final, we, wem, wn, wnm = pl.pallas_call(
        end_kernel,
        out_shape=[
            shape((1, 2, n_rows, width), BF),
            shape((1, 24, width), F32),
            shape((1, 2, 8, width), F32),
            shape((1, 16, width), F32),
            shape((1, 2, 8, width), F32),
        ],
        in_specs=[SM] + [VM] * 8,
        out_specs=[VM] * 5,
        name="end",
    )(c.reshape(1), part0, part1, r0, r1, node0, node1, m0, m1)
    mine = jnp.where(first, part0[24:32], part1[24:32])
    bias = jnp.concatenate([mine[:, 0:128], mine[:, 128:256]], axis=0)
    bias = lax.dynamic_slice_in_dim(bias, (p % 16) * 8, 8, axis=1)
    return (
        node_final,
        edge_final,
        we,
        wem,
        bias[None, 0:4],
        bias[4:5],
        wn,
        wnm,
        bias[None, 5:9],
        bias[9:10],
    )


def solution(mesh):
    dom3 = P("dom", None, None)
    in_specs = (
        P("pipe", None, "dom", None),
        P("pipe", None, "dom", None),
        P(None, "dom", None),
        P(None, "dom", None),
        P("dom"),
        P("dom"),
        P("dom"),
        P("dom"),
        dom3,
        dom3,
        dom3,
        P("pipe", None, None),
        P("pipe", None, None, None),
        P("pipe", None, None),
        P("pipe", None),
        P("pipe", None, None),
        P("pipe", None, None, None),
        P("pipe", None, None),
        P("pipe", None),
    )
    out_specs = (
        P("pipe", None, "dom", None),
        P("pipe", None, "dom", None),
        P("pipe", "dom", None),
        P("pipe", None, "dom", None),
        P("pipe", None, "dom"),
        P("pipe", "dom"),
        P("pipe", "dom", None),
        P("pipe", None, "dom", None),
        P("pipe", None, "dom"),
        P("pipe", "dom"),
    )
    return jax.shard_map(body, mesh=mesh, in_specs=in_specs, out_specs=out_specs, check_vma=False)
```

profile of v0, /device:TPU:0, one launch (start us, length us, event | category | flops | bytes accessed | tf_op | source)
XLA Modules:
  0.0 226.6 jit_solution(17535108111906619531)
XLA Ops:
  0.6 0.1 collective-permute-start.2
  0.7 0.5 collective-permute-start.1
  1.2 0.1 collective-permute-start
  1.3 4.1 %concatenate.20.refs_11_.refs_12_ = f32[16,512]{1,0:T(8,128)} concatenate(f32[4,512]{1,0:T(4,128)} %bitcast.60, f32[1,512]{1,0:T(1,128)} %param.33, f32[4,512]{1,0:T(4,128)} %bitcast.61, f32[1,512]{1,0:T(1,128)} %param.37, f32[6,512]{1,0:T(8,128)S(1)} %broadcast_in_dim.16), dimensions={0} | concatenate | bytes 65536 | tf_op jit(solution)/shard_map/concatenate | solution.py:421
  5.4 0.4 collective-permute-start.6
  5.8 0.1 collective-permute-start.5
  5.9 1.3 collective-permute-done.6.refs_18_.refs_19_
  7.2 0.1 collective-permute-start.4
  7.3 0.5 copy-done.9
  7.8 0.1 collective-permute-start.3
  8.0 1.2 slice_bitcast_fusion.4
  9.2 1.3 slice_bitcast_fusion.2
  10.4 1.3 stack.75.idx.refs_1_
  11.7 2.9 %pre.1 = bf16[5,64,512]{2,1,0:T(8,128)(2,1)} custom-call(s32[1]{0:T(128)} %bitcast.core, s32[8,64]{1,0:T(8,128)} %stack.75.idx.refs_1_, bf16[1,2,192,512]{3,2,1,0:T(8,128)(2,1)} %refs_6_.5, bf16[1,2,192,512]{3,2,1,0:T(8,128)(2,1)} %copy-done.5, bf16[2,192,512]{2,1,0:T(8,128)(2,1)} %refs_19_.1), custom_call_target="tpu_custom_call" | custom-call | tf_op jit(solution)/shard_map/pre/pallas_call | solution.py:438
  14.6 2.0 copy.37
  16.6 11.8 %all-to-all-start = ((bf16[64,5,512]{2,1,0:T(8,128)(2,1)}), bf16[64,5,512]{2,1,0:T(8,128)(2,1)}, u32[]{:S(2)}, u32[]{:S(2)}) async-start(bf16[64,5,512]{2,1,0:T(8,128)(2,1)} %copy.37), calls=%async_computation | async-start | bytes 1048576 | tf_op jit(solution)/shard_map/all_to_all | solution.py:405
  29.8 0.1 stack.84
  29.8 0.9 copy.45.refs_3_
  30.7 0.6 stack.81.refs_2_
  31.4 0.6 stack.87.refs_0_
  32.0 10.2 %all-to-all-done = bf16[64,5,512]{2,1,0:T(8,128)(2,1)} async-done(((bf16[64,5,512]{2,1,0:T(8,128)(2,1)}), bf16[64,5,512]{2,1,0:T(8,128)(2,1)}, u32[]{:S(2)}, u32[]{:S(2)}) %all-to-all-start) | async-done | bytes 327712 | tf_op jit(solution)/shard_map/all_to_all | solution.py:405
  42.2 1.9 copy.49
  44.1 0.0 copy-start.1
  44.1 1.1 copy-done
  45.3 0.5 copy-done.1
  45.8 18.9 %shard_map.258 = (f32[192,512]{1,0:T(8,128)}, bf16[768,512]{1,0:T(8,128)(2,1)}, bf16[64,80,256]{2,1,0:T(8,128)(2,1)}, bf16[64,80,256]{2,1,0:T(8,128)(2,1)}, bf16[2,64,512]{2,1,0:T(8,128)(2,1)}) custom-call(s32[5]{0:T(128)} %stack.87.refs_0_, s32[8,64]{1,0:T(8,128)} %stack.75.idx.refs_1_, s32[8,768]{1,0:T(8,128)} %stack.81.refs_2_, s32[768,8]{1,0:T(8,128)} %copy.45.refs_3_, ...), custom_call_target="tpu_custom_call" | custom-call | tf_op jit(solution)/shard_map/pallas_call | solution.py:497
  64.7 0.1 collective-permute-start.7
  64.8 1.7 copy.40
  66.4 4.8 %all-to-all-start.1 = ((bf16[64,2,512]{2,1,0:T(2,128)(2,1)}), bf16[64,2,512]{2,1,0:T(2,128)(2,1)S(1)}, u32[]{:S(2)}, u32[]{:S(2)}) async-start(bf16[64,2,512]{2,1,0:T(2,128)(2,1)} %copy.40), calls=%async_computation.1 | async-start | bytes 262144 | tf_op jit(solution)/shard_map/all_to_all | solution.py:405
  71.2 0.6 stack.78.refs_0_
  71.8 11.2 %shard_map.259 = (bf16[768,512]{1,0:T(8,128)(2,1)}, bf16[768,512]{1,0:T(8,128)(2,1)}, bf16[768,512]{1,0:T(8,128)(2,1)}, f32[768,512]{1,0:T(8,128)}, f32[768,512]...) custom-call(s32[5]{0:T(128)} %stack.78.refs_0_, ...), custom_call_target="tpu_custom_call" | custom-call | tf_op jit(solution)/shard_map/pallas_call | solution.py:497
  83.0 0.7 copy.50
  83.7 2.0 post.1
  85.7 1.5 copy.42
  87.2 10.3 %all-to-all-start.2 = ((bf16[64,2,256]{2,1,0:T(2,128)(2,1)}), bf16[64,2,256]{2,1,0:T(2,128)(2,1)S(1)}, u32[]{:S(2)}, u32[]{:S(2)}) async-start(bf16[64,2,256]{2,1,0:T(2,128)(2,1)} %copy.42), calls=%async_computation.2 | async-start | bytes 131072 | tf_op jit(solution)/shard_map/all_to_all | solution.py:405
  97.6 4.0 %add_convert_fusion.1 = bf16[64,80,256]{2,1,0:T(8,128)(2,1)} fusion(bf16[64,80,256]{2,1,0:T(8,128)(2,1)} %collective-permute-done.7, bf16[64,80,256]{2,1,0:T(8,128)(2,1)S(1)} %copy-done.6), kind=kLoop, calls=%fused_computation.2 | loop fusion | flops 5242880 | bytes 7864320 | tf_op jit(solution)/shard_map/convert_element_type | solution.py:520
  101.6 5.6 %all-to-all-done.2 = bf16[64,2,256]{2,1,0:T(2,128)(2,1)S(1)} async-done(((bf16[64,2,256]{2,1,0:T(2,128)(2,1)}), bf16[64,2,256]{2,1,0:T(2,128)(2,1)S(1)}, u32[]{:S(2)}, u32[]{:S(2)}) %all-to-all-start.2) | async-done | bytes 65568 | tf_op jit(solution)/shard_map/all_to_all | solution.py:405
  107.2 0.6 copy.51
  107.8 15.7 %shard_map.260 = (f32[192,512]{1,0:T(8,128)}, bf16[768,512]{1,0:T(8,128)(2,1)}, bf16[64,88,256]{2,1,0:T(8,128)(2,1)}, bf16[64,88,256]{2,1,0:T(8,128)(2,1)}) custom-call(s32[5]{0:T(128)} %stack.78.refs_0_, s32[8,64]{1,0:T(8,128)} %stack.75.idx.refs_1_, s32[8,768]{1,0:T(8,128)} %stack.81.refs_2_, s32[768,8]{1,0:T(8,128)} %copy.45.refs_3_, ...), custom_call_target="tpu_custom_call" | custom-call | tf_op jit(solution)/shard_map/pallas_call | solution.py:497
  123.6 0.1 collective-permute-start.8
  123.7 5.0 %all-to-all-start.4 = ((bf16[64,80,256]{2,1,0:T(8,128)(2,1)}), bf16[64,80,256]{2,1,0:T(8,128)(2,1)S(1)}, u32[]{:S(2)}, u32[]{:S(2)}) async-start(bf16[64,80,256]{2,1,0:T(8,128)(2,1)} %add_convert_fusion.1), calls=%async_computation.4 | async-start | bytes 5242880 | tf_op jit(solution)/shard_map/all_to_all | solution.py:405
  128.6 0.6 collective-permute-done.8
  129.3 5.0 %add_convert_fusion = bf16[64,88,256]{2,1,0:T(8,128)(2,1)} fusion(bf16[64,88,256]{2,1,0:T(8,128)(2,1)} %collective-permute-done.8, bf16[64,88,256]{2,1,0:T(8,128)(2,1)} %get-tuple-element.67), kind=kLoop, calls=%fused_computation | loop fusion | flops 5767168 | bytes 8650752 | tf_op jit(solution)/shard_map/convert_element_type | solution.py:520
  134.2 31.8 %all-to-all-done.4 = bf16[64,80,256]{2,1,0:T(8,128)(2,1)S(1)} async-done(((bf16[64,80,256]{2,1,0:T(8,128)(2,1)}), bf16[64,80,256]{2,1,0:T(8,128)(2,1)S(1)}, u32[]{:S(2)}, u32[]{:S(2)}) %all-to-all-start.4) | async-done | bytes 2621472 | tf_op jit(solution)/shard_map/all_to_all | solution.py:405
  166.0 1.6 copy-done.3
  167.6 5.3 %all-to-all-start.3 = ((bf16[64,88,256]{2,1,0:T(8,128)(2,1)}), bf16[64,88,256]{2,1,0:T(8,128)(2,1)S(1)}, u32[]{:S(2)}, u32[]{:S(2)}) async-start(bf16[64,88,256]{2,1,0:T(8,128)(2,1)} %add_convert_fusion), calls=%async_computation.3 | async-start | bytes 5767168 | tf_op jit(solution)/shard_map/all_to_all | solution.py:405
  172.9 2.5 %collective-permute-start.14 = (bf16[768,512]{1,0:T(8,128)(2,1)}, bf16[768,512]{1,0:T(8,128)(2,1)}, u32[]{:S(2)}, u32[]{:S(2)}) collective-permute-start(bf16[768,512]{1,0:T(8,128)(2,1)} %get-tuple-element.51), channel_id=1, source_target_pairs={{0,64},{1,65},{2,66},{3,67},{4,68},{5,69},{6,70},{7,71},{8,72},{9,... | collective-permute-start | bytes 2359304 | tf_op jit(solution)/shard_map/ppermute | solution.py:543
  175.3 1.3 collective-permute-start.13
  176.6 4.1 %collective-permute-start.12 = (bf16[192,512]{1,0:T(8,128)(2,1)S(1)}, bf16[192,512]{1,0:T(8,128)(2,1)S(1)}, u32[]{:S(2)}, u32[]{:S(2)}) collective-permute-start(bf16[192,512]{1,0:T(8,128)(2,1)S(1)} %copy-done.7), channel_id=1, source_target_pairs={{0,64},{1,65},{2,66},{3,67},{4,68},{5,69},{6,70},{7,71},{8,72},{9,... | collective-permute-start | bytes 589832 | tf_op jit(solution)/shard_map/ppermute | solution.py:546
  180.8 3.3 %maximum_select_fusion = bf16[1,2,768,512]{3,2,1,0:T(8,128)(2,1)} fusion(bf16[1,1,768,512]{3,2,1,0:T(8,128)(2,1)} %bitcast.26, bf16[1,1,768,512]{3,2,1,0:T(8,128)(2,1)} %bitcast.55, bf16[1,1,768,512]{3,2,1,0:T(8,128)(2,1)} %bitcast.52, bf16[1,1,768,512]{3,2,1,0:T(8,128)(2,1)} %bitcast.27, pred[]{:T(512)S(6)} %eq.12), kind=kLoop, calls=%fused_computation.3 | loop fusion | flops 2359296 | bytes 4718593 | tf_op jit(solution)/shard_map/jit(_where)/select_n | solution.py:544
  184.1 0.4 convert_reduce_fusion.p1
  184.5 1.3 collective-permute-start.10
  185.8 26.7 %all-to-all-done.3.came = bf16[64,88,256]{2,1,0:T(8,128)(2,1)S(1)} async-done(((bf16[64,88,256]{2,1,0:T(8,128)(2,1)}), bf16[64,88,256]{2,1,0:T(8,128)(2,1)S(1)}, u32[]{:S(2)}, u32[]{:S(2)}) %all-to-all-start.3) | async-done | bytes 2883616 | tf_op jit(solution)/shard_map/all_to_all | solution.py:405
  212.5 1.5 copy-done.2
  214.0 3.6 %sums.1 = (f32[80,256]{1,0:T(8,128)}, bf16[192,512]{1,0:T(8,128)(2,1)}) custom-call(s32[8,64]{1,0:T(8,128)} %stack.75.idx.refs_1_, f32[192,512]{1,0:T(8,128)} %get-tuple-element.66.local, bf16[64,88,256]{2,1,0:T(8,128)(2,1)} %copy-done.2), custom_call_target="tpu_custom_call" | custom-call | tf_op jit(solution)/shard_map/sums/pallas_call | solution.py:535
  217.6 0.7 slice_select_fusion
  218.3 1.3 collective-permute-start.9
  219.6 0.1 dynamic-slice_maximum_fusion
  219.7 0.6 slice_bitcast_fusion
  220.2 1.3 collective-permute-start.11
  221.5 0.5 fusion.9
  222.1 1.7 collective-permute-done.11.m0
  223.8 0.7 copy-done.11
  224.5 2.1 end.1
  (45 shorter events, 0.1 us)
Async XLA Ops:
  0.6 43.5 %collective-permute-start.2 = (bf16[1536,512]{1,0:T(8,128)(2,1)}, bf16[1536,512]{1,0:T(8,128)(2,1)S(1)}, u32[]{:S(2)}, u32[]{:S(2)}) collective-permute-start(bf16[1536,512]{1,0:T(8,128)(2,1)} %bitcast.44), channel_id=1, source_target_pairs={{0,64},{64,0},{1,65},{65,1},{2,66},{66,2},{3,67},{67,3},{4,68},{68... | collective-permute-start | bytes 4718600 | tf_op jit(solution)/shard_map/ppermute | solution.py:401
  0.7 43.4 %collective-permute-start.1 = (bf16[1,2,768,512]{3,2,1,0:T(8,128)(2,1)}, bf16[1,2,768,512]{3,2,1,0:T(8,128)(2,1)S(1)}, u32[]{:S(2)}, u32[]{:S(2)}) collective-permute-start(bf16[1,2,768,512]{3,2,1,0:T(8,128)(2,1)} %refs_7_.5), channel_id=1, source_target_pairs={{0,64},{64,0},{1,65},{65,1},{2,66},{66,2},{3,67},{67,3},{4,68},{68... | collective-permute-start | bytes 4718600 | tf_op jit(solution)/shard_map/ppermute | solution.py:401
  1.2 6.1 %collective-permute-start = (bf16[1,2,192,512]{3,2,1,0:T(8,128)(2,1)}, bf16[1,2,192,512]{3,2,1,0:T(8,128)(2,1)S(1)}, u32[]{:S(2)}, u32[]{:S(2)}) collective-permute-start(bf16[1,2,192,512]{3,2,1,0:T(8,128)(2,1)} %refs_6_.5), channel_id=1, source_target_pairs={{0,64},{64,0},{1,65},{65,1},{2,66},{66,2},{3,67},{67,3},{4,68},{68... | collective-permute-start | bytes 1179656 | tf_op jit(solution)/shard_map/ppermute | solution.py:401
  5.4 23.0 %copy-start.14 = (s32[768]{0:T(1024)S(1)}, s32[768]{0:T(1024)}, u32[]{:S(2)}) copy-start(s32[768]{0:T(1024)} %param.26) | copy-start | bytes 9220
  5.4 23.0 %copy-start.15 = (s32[768]{0:T(1024)S(1)}, s32[768]{0:T(1024)}, u32[]{:S(2)}) copy-start(s32[768]{0:T(1024)} %param.25) | copy-start | bytes 9220
  5.4 1.8 collective-permute-start.6
  5.8 38.3 %collective-permute-start.5 = (bf16[2,512,512]{2,1,0:T(8,128)(2,1)}, bf16[2,512,512]{2,1,0:T(8,128)(2,1)}, u32[]{:S(2)}, u32[]{:S(2)}) collective-permute-start(bf16[2,512,512]{2,1,0:T(8,128)(2,1)} %bitcast.47), channel_id=1, source_target_pairs={{0,64},{64,0},{1,65},{65,1},{2,66},{66,2},{3,67},{67,3},{4,68},{68... | collective-permute-start | bytes 3145736 | tf_op jit(solution)/shard_map/ppermute | solution.py:401
  7.2 0.6 copy-start.9
  7.2 36.9 %collective-permute-start.4 = (bf16[1024,512]{1,0:T(8,128)(2,1)}, bf16[1024,512]{1,0:T(8,128)(2,1)}, u32[]{:S(2)}, u32[]{:S(2)}) collective-permute-start(bf16[1024,512]{1,0:T(8,128)(2,1)} %bitcast.46), channel_id=1, source_target_pairs={{0,64},{64,0},{1,65},{65,1},{2,66},{66,2},{3,67},{67,3},{4,68},{68... | collective-permute-start | bytes 3145736 | tf_op jit(solution)/shard_map/ppermute | solution.py:401
  7.8 3.9 %copy-start.5 = (bf16[1,2,192,512]{3,2,1,0:T(8,128)(2,1)}, bf16[1,2,192,512]{3,2,1,0:T(8,128)(2,1)S(1)}, u32[]{:S(2)}) copy-start(bf16[1,2,192,512]{3,2,1,0:T(8,128)(2,1)S(1)} %collective-permute-done.rec_all.refs_12_.refs_13_) | copy-start | bytes 1179652
  7.8 36.3 %collective-permute-start.3 = (bf16[2,512,512]{2,1,0:T(8,128)(2,1)}, bf16[2,512,512]{2,1,0:T(8,128)(2,1)}, u32[]{:S(2)}, u32[]{:S(2)}) collective-permute-start(bf16[2,512,512]{2,1,0:T(8,128)(2,1)} %bitcast.45), channel_id=1, source_target_pairs={{0,64},{64,0},{1,65},{65,1},{2,66},{66,2},{3,67},{67,3},{4,68},{68... | collective-permute-start | bytes 3145736 | tf_op jit(solution)/shard_map/ppermute | solution.py:401
  16.6 25.6 %all-to-all-start = ((bf16[64,5,512]{2,1,0:T(8,128)(2,1)}), bf16[64,5,512]{2,1,0:T(8,128)(2,1)}, u32[]{:S(2)}, u32[]{:S(2)}) async-start(bf16[64,5,512]{2,1,0:T(8,128)(2,1)} %copy.37), calls=%async_computation | async-start | bytes 1048576 | tf_op jit(solution)/shard_map/all_to_all | solution.py:405
  44.1 1.2 copy-start
  44.1 1.6 copy-start.1
  64.7 32.9 %collective-permute-start.7 = (bf16[64,80,256]{2,1,0:T(8,128)(2,1)}, bf16[64,80,256]{2,1,0:T(8,128)(2,1)}, u32[]{:S(2)}, u32[]{:S(2)}) collective-permute-start(bf16[64,80,256]{2,1,0:T(8,128)(2,1)} %get-tuple-element.45), channel_id=1, source_target_pairs={{0,64},{64,0},{1,65},{65,1},{2,66},{66,2},{3,67},{67,3},{4,68},{68... | collective-permute-start | bytes 7864328 | tf_op jit(solution)/shard_map/ppermute | solution.py:401
  66.4 16.6 %all-to-all-start.1 = ((bf16[64,2,512]{2,1,0:T(2,128)(2,1)}), bf16[64,2,512]{2,1,0:T(2,128)(2,1)S(1)}, u32[]{:S(2)}, u32[]{:S(2)}) async-start(bf16[64,2,512]{2,1,0:T(2,128)(2,1)} %copy.40), calls=%async_computation.1 | async-start | bytes 262144 | tf_op jit(solution)/shard_map/all_to_all | solution.py:405
  71.8 25.8 %copy-start.6 = (bf16[64,80,256]{2,1,0:T(8,128)(2,1)S(1)}, bf16[64,80,256]{2,1,0:T(8,128)(2,1)}, u32[]{:S(2)}) copy-start(bf16[64,80,256]{2,1,0:T(8,128)(2,1)} %get-tuple-element.44) | copy-start | bytes 7864324
  87.2 19.9 %all-to-all-start.2 = ((bf16[64,2,256]{2,1,0:T(2,128)(2,1)}), bf16[64,2,256]{2,1,0:T(2,128)(2,1)S(1)}, u32[]{:S(2)}, u32[]{:S(2)}) async-start(bf16[64,2,256]{2,1,0:T(2,128)(2,1)} %copy.42), calls=%async_computation.2 | async-start | bytes 131072 | tf_op jit(solution)/shard_map/all_to_all | solution.py:405
  123.6 5.7 %collective-permute-start.8 = (bf16[64,88,256]{2,1,0:T(8,128)(2,1)}, bf16[64,88,256]{2,1,0:T(8,128)(2,1)}, u32[]{:S(2)}, u32[]{:S(2)}) collective-permute-start(bf16[64,88,256]{2,1,0:T(8,128)(2,1)} %get-tuple-element.68), channel_id=1, source_target_pairs={{0,64},{64,0},{1,65},{65,1},{2,66},{66,2},{3,67},{67,3},{4,68},{68... | collective-permute-start | bytes 8650760 | tf_op jit(solution)/shard_map/ppermute | solution.py:401
  123.7 42.4 %all-to-all-start.4 = ((bf16[64,80,256]{2,1,0:T(8,128)(2,1)}), bf16[64,80,256]{2,1,0:T(8,128)(2,1)S(1)}, u32[]{:S(2)}, u32[]{:S(2)}) async-start(bf16[64,80,256]{2,1,0:T(8,128)(2,1)} %add_convert_fusion.1), calls=%async_computation.4 | async-start | bytes 5242880 | tf_op jit(solution)/shard_map/all_to_all | solution.py:405
  134.2 42.4 %copy-start.7 = (bf16[192,512]{1,0:T(8,128)(2,1)S(1)}, bf16[192,512]{1,0:T(8,128)(2,1)}, u32[]{:S(2)}) copy-start(bf16[192,512]{1,0:T(8,128)(2,1)} %get-tuple-element.50.n1) | copy-start | bytes 589828
  166.0 1.6 copy-start.3
  167.6 44.9 %all-to-all-start.3 = ((bf16[64,88,256]{2,1,0:T(8,128)(2,1)}), bf16[64,88,256]{2,1,0:T(8,128)(2,1)S(1)}, u32[]{:S(2)}, u32[]{:S(2)}) async-start(bf16[64,88,256]{2,1,0:T(8,128)(2,1)} %add_convert_fusion), calls=%async_computation.3 | async-start | bytes 5767168 | tf_op jit(solution)/shard_map/all_to_all | solution.py:405
  172.9 7.9 %collective-permute-start.14 = (bf16[768,512]{1,0:T(8,128)(2,1)}, bf16[768,512]{1,0:T(8,128)(2,1)}, u32[]{:S(2)}, u32[]{:S(2)}) collective-permute-start(bf16[768,512]{1,0:T(8,128)(2,1)} %get-tuple-element.51), channel_id=1, source_target_pairs={{0,64},{1,65},{2,66},{3,67},{4,68},{5,69},{6,70},{7,71},{8,72},{9,... | collective-permute-start | bytes 2359304 | tf_op jit(solution)/shard_map/ppermute | solution.py:543
  175.3 5.5 %collective-permute-start.13 = (bf16[768,512]{1,0:T(8,128)(2,1)}, bf16[768,512]{1,0:T(8,128)(2,1)}, u32[]{:S(2)}, u32[]{:S(2)}) collective-permute-start(bf16[768,512]{1,0:T(8,128)(2,1)} %get-tuple-element.73), channel_id=1, source_target_pairs={{64,0},{65,1},{66,2},{67,3},{68,4},{69,5},{70,6},{71,7},{72,8},{73... | collective-permute-start | bytes 2359304 | tf_op jit(solution)/shard_map/ppermute | solution.py:542
  176.6 7.4 %copy-start.4 = (bf16[64,80,256]{2,1,0:T(8,128)(2,1)S(1)}, bf16[64,80,256]{2,1,0:T(8,128)(2,1)}, u32[]{:S(2)}) copy-start(bf16[64,80,256]{2,1,0:T(8,128)(2,1)} %copy-done.3) | copy-start | bytes 7864324
  176.6 45.4 %collective-permute-start.12 = (bf16[192,512]{1,0:T(8,128)(2,1)S(1)}, bf16[192,512]{1,0:T(8,128)(2,1)S(1)}, u32[]{:S(2)}, u32[]{:S(2)}) collective-permute-start(bf16[192,512]{1,0:T(8,128)(2,1)S(1)} %copy-done.7), channel_id=1, source_target_pairs={{0,64},{1,65},{2,66},{3,67},{4,68},{5,69},{6,70},{7,71},{8,72},{9,... | collective-permute-start | bytes 589832 | tf_op jit(solution)/shard_map/ppermute | solution.py:546
  184.5 39.3 %copy-start.8 = (f32[80,256]{1,0:T(8,128)}, f32[80,256]{1,0:T(8,128)S(1)}, u32[]{:S(2)}) copy-start(f32[80,256]{1,0:T(8,128)S(1)} %convert_reduce_fusion.p1) | copy-start | bytes 245764
  184.5 37.6 %collective-permute-start.10 = (f32[80,256]{1,0:T(8,128)S(1)}, f32[80,256]{1,0:T(8,128)S(1)}, u32[]{:S(2)}, u32[]{:S(2)}) collective-permute-start(f32[80,256]{1,0:T(8,128)S(1)} %convert_reduce_fusion.p1), channel_id=1, source_target_pairs={{0,64},{1,65},{2,66},{3,67},{4,68},{5,69},{6,70},{7,71},{8,72},{9,... | collective-permute-start | bytes 245768 | tf_op jit(solution)/shard_map/ppermute | solution.py:546
  212.5 1.5 copy-start.2
  218.3 3.8 %collective-permute-start.9 = (f32[80,256]{1,0:T(8,128)}, f32[80,256]{1,0:T(8,128)S(1)}, u32[]{:S(2)}, u32[]{:S(2)}) collective-permute-start(f32[80,256]{1,0:T(8,128)} %get-tuple-element.69.p0), channel_id=1, source_target_pairs={{64,0},{65,1},{66,2},{67,3},{68,4},{69,5},{70,6},{71,7},{72,8},{73... | collective-permute-start | bytes 245768 | tf_op jit(solution)/shard_map/ppermute | solution.py:545
  220.2 3.5 %collective-permute-start.11 = (bf16[192,512]{1,0:T(8,128)(2,1)}, bf16[192,512]{1,0:T(8,128)(2,1)S(1)}, u32[]{:S(2)}, u32[]{:S(2)}) collective-permute-start(bf16[192,512]{1,0:T(8,128)(2,1)} %get-tuple-element.71.n0), channel_id=1, source_target_pairs={{64,0},{65,1},{66,2},{67,3},{68,4},{69,5},{70,6},{71,7},{72,8},{73... | collective-permute-start | bytes 589832 | tf_op jit(solution)/shard_map/ppermute | solution.py:545
  222.1 1.7 copy-start.10
  222.1 1.7 copy-start.12
  222.1 1.7 copy-start.13
  223.8 0.7 copy-start.11
where the time goes:
time: 229 us; the launch traced here: 227 us
  waiting for transfers between devices  77.9 us (34%)
  Pallas kernels  56.4 us (25%)
  starting transfers between devices  50.5 us (22%)
  local copies, waits for them, and re-layouts  26 us (11%)
  other arithmetic  13.4 us (6%)
  between operations  2.32 us (1%)
    all_to_all x5, waiting for transfers between devices, exchange(): return lax.all_to_all(x, 'dom', split_axis=0, concat_axis=0, tiled=True)  74.3 us
    pallas_call x3, Pallas kernels, run(): pl.pallas_call(functools.partial(unit_kernel, mode, layer), out_shape=out...  45.8 us
    all_to_all x5, starting transfers between devices, exchange(): return lax.all_to_all(x, 'dom', split_axis=0, concat_axis=0, tiled=True)  37.1 us
    convert_element_type x2, other arithmetic, paired(): return (keep.astype(F32) + swap(send).astype(F32)).astype(BF)  8.93 us
    unnamed x32, local copies, waits for them, and re-layouts  5.91 us
    ppermute x2, starting transfers between devices, body(): r1, m1 = lax.ppermute((part1, node1), 'pipe', up)  5.44 us
  transfers between devices with their start and end apart: 20, of which 7 were waited for; matrix products, arithmetic and copies ran while one was open for 15% of the time, Pallas kernels for 9%

commit v1 on v0

--- a/solution.py
+++ b/solution.py
@@ -30,10 +30,48 @@
     return jnp.where(grid == index_row, 1.0, 0.0)
 
 
-def spread_rows(per):
-    row = lax.broadcasted_iota(jnp.int32, (8 * per, 4 * per), 0)
-    col = lax.broadcasted_iota(jnp.int32, (8 * per, 4 * per), 1)
+def spread_rows(per, count):
+    shape = (8 * per, count * per)
+    row = lax.broadcasted_iota(jnp.int32, shape, 0)
+    col = lax.broadcasted_iota(jnp.int32, shape, 1)
     return jnp.where(col == (row & 7) * per + (row >> 3), 1.0, 0.0).astype(BF)
+
+
+def to_chunks(pieces, per):
+    count = pieces.shape[0] // per
+    rows = dot(spread_rows(per, count), pieces)
+    return rows.reshape(per, 8, pieces.shape[1]).astype(BF)
+
+
+def from_chunks(chunks, count):
+    per, _, n = chunks.shape
+    rows = chunks.astype(F32).reshape(per * 8, n).astype(BF)
+    return dot_t0(spread_rows(per, count), rows).astype(BF)
+
+
+def fold(rows, per):
+    parts = []
+    for s in range(rows.shape[0] // per):
+        for b in range(rows.shape[1] // 128):
+            parts.append(rows[s * per : (s + 1) * per, b * 128 : (b + 1) * 128])
+    return jnp.concatenate(parts, axis=0)
+
+
+def unfold(rows, per):
+    return jnp.concatenate([rows[b * per : (b + 1) * per] for b in range(4)], axis=1)
+
+
+def per_chunk(sums, chunks):
+    n = sums.shape[1]
+    take = lax.broadcasted_iota(jnp.int32, (128, 16), 0) >> 3
+    take = jnp.where(take == lax.broadcasted_iota(jnp.int32, (128, 16), 1), 1.0, 0.0)
+    lane = lax.broadcasted_iota(jnp.int32, (128, n), 0)
+    col = lax.broadcasted_iota(jnp.int32, (128, n), 1)
+    spaced = dot(take.astype(BF), sums.astype(BF))
+    spaced = jnp.where((lane & 7) == (col & 7), spaced, 0.0).astype(BF)
+    home = lax.broadcasted_iota(jnp.int32, (chunks, n), 1) >> 3
+    home = jnp.where(home == lax.broadcasted_iota(jnp.int32, (chunks, n), 0), 1.0, 0.0)
+    return dot_t1(home.astype(BF), spaced)
 
 
 def act(value):
@@ -61,7 +99,9 @@
     return jnp.sum(value, axis=0, keepdims=True)
 
 
-def pre_kernel(core, idx, own_all, rec_all, cot_all, out, ownb, recv, cotb, sems):
+def pre_kernel(
+    core, idx, eb, eg, nb, ng, own_all, rec_all, cot_all, out, vec, ownb, recv, cotb, sems
+):
     c = core[0]
     cp = [
         pltpu.make_async_copy(own_all.at[0, c], ownb, sems.at[0]),
@@ -70,37 +110,44 @@
     ]
     for one in cp:
         one.start()
+    vec[0:4, :] = eb[0]
+    vec[4:5, :] = eg[...]
+    vec[5:9, :] = nb[0]
+    vec[9:10, :] = ng[...]
+    vec[10:16, :] = jnp.zeros((6, vec.shape[1]), F32)
     rows = ownb.shape[0]
-    h0 = hot_rows(idx[0:1, :], rows).astype(BF)
-    h1 = hot_rows(idx[1:2, :], rows).astype(BF)
-    hg = hot_rows(idx[2:3, :], rows).astype(BF)
+    h0, h1, hg = (hot_rows(idx[k : k + 1, :], rows).astype(BF) for k in range(3))
     for one in cp:
         one.wait()
     own, other = ownb[...], recv[...]
     low = jnp.where(c == 0, own.astype(F32), other.astype(F32)).astype(BF)
     top = jnp.where(c == 0, other.astype(F32), own.astype(F32)).astype(BF)
-    for k, (hot, rows_of) in enumerate(((h0, low), (h1, low), (h0, top), (h1, top), (hg, cotb[...]))):
-        out[k] = dot_t0(hot, rows_of).astype(BF)
-
-
-def post_kernel(idx, local, back, node_out, hang_out):
+    pairs = ((h0, low), (h1, low), (h0, top), (h1, top), (hg, cotb[...]))
+    pieces = jnp.concatenate([dot_t0(hot, src).astype(BF) for hot, src in pairs], axis=0)
+    out[...] = to_chunks(pieces, idx.shape[1])
+
+
+def post_kernel(idx, local, came, node_out, hang_out):
     rows = local.shape[0]
+    per = came.shape[0]
     total = local[...]
+    back = from_chunks(came[...], 8)
     for s in range(2):
-        total = total + dot(hot_rows(idx[s : s + 1, :], rows).astype(BF), back[s])
+        part = unfold(back[s * 4 * per : (s + 1) * 4 * per], per)
+        total = total + dot(hot_rows(idx[s : s + 1, :], rows).astype(BF), part)
     low = total.astype(BF)
     node_out[...] = low
     hang = dot_t0(hot_rows(idx[2:3, :], rows).astype(BF), low).astype(BF)
-    half = hang.shape[1] // 2
-    hang_out[0] = hang[:, :half]
-    hang_out[1] = hang[:, half:]
-
-
-def sum_kernel(idx, local, came, part_out, node_out):
+    hang_out[...] = to_chunks(fold(hang, per), per)
+
+
+def sum_kernel(idx, local, came, part_out, ship):
     per = came.shape[0]
-    part_out[...] = jnp.sum(came[:, 0:80, :].astype(F32), axis=0)
-    tail = came[:, 80:88, :].astype(F32).reshape(per * 8, came.shape[2]).astype(BF)
-    quarters = dot_t0(spread_rows(per), tail).astype(BF)
+    half = came.shape[2]
+    part = jnp.sum(came[...].astype(F32), axis=0)
+    part_out[...] = part
+    tail = came[:, 72:80, :].astype(F32).reshape(per * 8, half).astype(BF)
+    quarters = dot_t0(spread_rows(per, 5), tail).astype(BF)
     rows = local.shape[0]
     total = local[...]
     for s in range(2):
@@ -108,34 +155,56 @@
             [quarters[(s + 2 * k) * per : (s + 2 * k + 1) * per, :] for k in range(2)], axis=1
         )
         total = total + dot(hot_rows(idx[s : s + 1, :], rows).astype(BF), back)
-    node_out[...] = total.astype(BF)
-
-
-def end_kernel(core, p0, p1, r0, r1, n0, n1, m0, m1, node_out, we, wem, wn, wnm):
+    ship[0:rows, :] = total.astype(BF)
+    split_part(part, ship, rows)
+
+
+def split_part(part, ship, rows):
+    high = part.astype(BF)
+    low = (part - high.astype(F32)).astype(BF)
+    ship[rows:, :] = jnp.concatenate([high, low], axis=1)
+
+
+def first_kernel(came, node, part_out, ship):
+    rows = node.shape[0]
+    part = jnp.sum(came[...].astype(F32), axis=0)
+    part = jnp.concatenate([part, jnp.zeros((8, part.shape[1]), F32)], axis=0)
+    part_out[...] = part
+    ship[0:rows, :] = node[...]
+    split_part(part, ship, rows)
+
+
+def end_kernel(core, p0, p1, s0, s1, r0, r1, node_out, we, wem, wn, wnm):
+    def part_of(ship):
+        rows = node_out.shape[2]
+        half = p0.shape[1]
+        return ship[rows:, :half].astype(F32) + ship[rows:, half:].astype(F32)
+
     def write(left, right, first, second):
-        full = jnp.concatenate([left[0:80, :], right[0:80, :]], axis=1)
-        node_out[0, 0] = first[...]
-        node_out[0, 1] = second[...]
+        full = jnp.concatenate([left, right], axis=1)
+        rows = node_out.shape[2]
+        node_out[0, 0] = first[0:rows, :]
+        node_out[0, 1] = second[0:rows, :]
         we[0] = full[0:24, :]
-        wem[0, 0] = full[32:40, :]
-        wem[0, 1] = full[40:48, :]
-        wn[0] = full[48:64, :]
-        wnm[0, 0] = full[64:72, :]
-        wnm[0, 1] = full[72:80, :]
+        wem[0, 0] = full[24:32, :]
+        wem[0, 1] = full[64:72, :]
+        wn[0] = full[32:48, :]
+        wnm[0, 0] = full[48:56, :]
+        wnm[0, 1] = full[56:64, :]
 
     @pl.when(core[0] == 0)
     def _():
-        write(p0, r0, n0, m0)
+        write(p0[...], part_of(r0), s0, r0)
 
     @pl.when(core[0] == 1)
     def _():
-        write(r1, p1, m1, n1)
+        write(part_of(r1), p1[...], r1, s1)
 
 
 SAVED = 14
 
 
-def unit_kernel(mode, layer, *refs):
+def unit_kernel(mode, *refs):
     take = iter(refs)
 
     def some(n):
@@ -143,29 +212,34 @@
 
     forward_part, backward_part = "F" in mode, "B" in mode
     scal, idx, erow, ecol, got = some(5)
-    per = got.shape[1]
-    inc_of = lambda: jnp.concatenate([got[2 * layer], got[2 * layer + 1]], axis=0)
+    per = idx.shape[1]
     hang_in = next(take) if mode == "B" else None
     own_nodes, own_edges, *own_rest = some(7)
     recs = some(7)
     gout_all, gedge_all = some(2) if backward_part else (None, None)
     kept_in = some(SAVED) if mode == "B" else None
-    saved = some(SAVED) if mode == "F" else None
+    bias_in = next(take) if mode == "B" else None
+    saved_out = some(SAVED) if mode == "F" else None
     if backward_part:
-        local_ref, edge_ref, keep_ref, send_ref = some(4)
-        back_ref = next(take) if mode == "FB" else None
+        local_ref, edge_out, keep_out, send_out = some(4)
+        back_ref, bias_ref, inc_out = some(3) if mode == "FB" else (None, None, None)
     dsts = some(7)
     nodes, edges, w1, wm, n1, nm, vec = dsts
-    if mode != "F":
-        saved = some(SAVED)
+    saved = some(SAVED)
     oh, a1, a2, s1, s2, nrm, inv, _, _, _, _, _, _, _ = saved
-    q, msg, gout, gedge, l1, l2, l3, gag, bsum, sems = some(10)
+    q, msg, gout, gedge, l1, l2, l3, gag, bsum, inc = some(10)
+    if backward_part:
+        edge_ref, keep_ref, send_ref = some(3)
+    sems = next(take)
+    sent = []
+
+    def leave(src, dst, sem):
+        pltpu.make_async_copy(src, dst, sems.at[sem]).start()
 
     is_own, c, node_count, edge_count, gi = (scal[i] for i in range(5))
     owns = [own_nodes.at[0, c], own_edges.at[0, c]] + [r.at[0] for r in own_rest[:4]]
     owns = owns + [own_rest[4]]
     recs = [recs[0].at[0, c], recs[1].at[0, c]] + recs[2:]
-    order = [6, 0, 2, 1, 3, 4, 5] if forward_part else [6, 0, 5, 4, 3, 2, 1]
     if backward_part:
         cg = pltpu.make_async_copy(gout_all.at[gi], gout, sems.at[7])
         ce = pltpu.make_async_copy(gedge_all.at[gi], gedge, sems.at[8])
@@ -174,28 +248,25 @@
         loads = [
             pltpu.make_async_copy(kept_in[k], saved[k], sems.at[9 + k]) for k in range(SAVED)
         ]
+
+    def fetch(order):
+        @pl.when(is_own == 1)
+        def _():
+            for k in order:
+                pltpu.make_async_copy(owns[k], dsts[k], sems.at[k]).start()
+
+        @pl.when(is_own == 0)
+        def _():
+            for k in order:
+                pltpu.make_async_copy(recs[k], dsts[k], sems.at[k]).start()
+
+    if mode == "B":
         cg.start()
         for k in range(7, SAVED):
             loads[k].start()
-
-    @pl.when(is_own == 1)
-    def _():
-        for k in order:
-            pltpu.make_async_copy(owns[k], dsts[k], sems.at[k]).start()
-
-    @pl.when(is_own == 0)
-    def _():
-        for k in order:
-            pltpu.make_async_copy(recs[k], dsts[k], sems.at[k]).start()
-
-    if mode == "B":
-        for k in range(7):
-            loads[k].start()
+        fetch([6, 0, 5, 4])
     else:
-        if backward_part:
-            cg.start()
-    if backward_part:
-        ce.start()
+        fetch([6, 0, 2, 1, 3])
 
     def ready(k):
         pltpu.make_async_copy(recs[k], dsts[k], sems.at[k]).wait()
@@ -214,6 +285,16 @@
     nb = [vec[i : i + 1, :] for i in range(5, 9)]
     ng = vec[9:10, :]
     to_target = hot_rows(erow[1:2, :], n_rows).astype(BF)
+
+    if mode == "FB":
+        pieces = from_chunks(got[...], 5)
+        inc_out[...] = pieces[0 : 2 * per]
+        inc[...] = pieces[2 * per : 4 * per]
+        from_hanging = pieces[4 * per :]
+    else:
+        inc[...] = got[...]
+        if backward_part:
+            from_hanging = unfold(from_chunks(hang_in[...], 4), per)
 
     if forward_part:
         def build(i, _):
@@ -228,9 +309,13 @@
         ready(2)
         q[0:n_rows, :] = dot(nodes[...], w1[width : 2 * width, :]).astype(BF)
         q[n_rows : 2 * n_rows, :] = dot(nodes[...], w1[0:width, :]).astype(BF)
-        q[2 * n_rows :, :] = dot(inc_of(), w1[0:width, :]).astype(BF)
+        q[2 * n_rows :, :] = dot(inc[...], w1[0:width, :]).astype(BF)
         ready(1)
         ready(3)
+        fetch([4, 5])
+        if backward_part:
+            cg.start()
+            ce.start()
 
         def forward(i, _):
             start = pl.multiple_of(i * BLOCK, BLOCK)
@@ -246,6 +331,9 @@
             nrm[rows, :] = normed
             inv[rows, :] = rstd
             msg[rows, :] = ((normed * eg + eb[3]) * live_of(start, BLOCK, edge_count)).astype(BF)
+            if mode == "F":
+                for k in range(7):
+                    leave(saved[k].at[rows, :], saved_out[k].at[rows, :], 9 + k)
             return 0
 
         lax.fori_loop(0, blocks, forward, 0)
@@ -261,6 +349,10 @@
             ref[...] = value
 
     if not backward_part:
+        for k in range(7, SAVED):
+            leave(saved[k], saved_out[k], 9 + k)
+        for k in range(SAVED):
+            pltpu.make_async_copy(saved[k], saved_out[k], sems.at[9 + k]).wait()
         return
     if not forward_part:
         ready(0)
@@ -268,6 +360,10 @@
         ready(5)
         for one in loads[7:]:
             one.wait()
+        for one in loads[:7]:
+            one.start()
+        fetch([3, 2, 1])
+        ce.start()
     x_n = nodes[...]
     agg, na1, na2, ns1, ns2, nn, nr = (ref[...] for ref in saved[7:])
 
@@ -283,6 +379,11 @@
         n = tile.shape[1]
         keep_ref[:, first : first + n, :] = tile[:, :, :half].astype(BF)
         send_ref[:, first : first + n, :] = tile[:, :, half:].astype(BF)
+        for ref, dst in ((send_ref, send_out), (keep_ref, keep_out)):
+            part = (slice(None), pl.ds(first, n), slice(None))
+            copy = pltpu.make_async_copy(ref.at[part], dst.at[part], sems.at[24 + len(sent)])
+            copy.start()
+            sent.append(copy)
 
     cg.wait()
     hung = jnp.max(
@@ -293,10 +394,6 @@
         keepdims=True,
     )
     spread = 0.5 * (hot_rows(idx[3:4, :], n_rows) + hot_rows(idx[4:5, :], n_rows))
-    if mode == "B":
-        from_hanging = jnp.concatenate([hang_in[0], hang_in[1]], axis=1)
-    else:
-        from_hanging = got[4]
     grad_new = gout[...].astype(F32) * (1.0 - hung) + dot(spread.astype(BF), from_hanging)
     gy = grad_new * live_of(0, n_rows, node_count)
     bsum[8:9, :] = col_sum(gy)
@@ -314,8 +411,8 @@
     gag[0:n_rows, :] = dot_t1(low1, n1[width:, :]).astype(BF)
     gag[n_rows:, :] = jnp.zeros((gag.shape[0] - n_rows, width), BF)
     low1p = halves(low1)
-    put(48, [jnp.concatenate([dot_t0(x_n, low1p), dot_t0(agg, low1p)], axis=0)])
-    put(64, [dot_t0(na1, halves(low2)), dot_t0(na2, halves(low3))])
+    put(32, [jnp.concatenate([dot_t0(x_n, low1p), dot_t0(agg, low1p)], axis=0)])
+    put(48, [dot_t0(na1, halves(low2)), dot_t0(na2, halves(low3))])
 
     if not forward_part:
         ready(1)
@@ -343,6 +440,7 @@
         low = g1.astype(BF)
         l1[rows, :] = low
         edge_ref[rows, :] = (ge + dot_t1(low, w1[2 * width :, :])).astype(BF)
+        leave(edge_ref.at[rows, :], edge_out.at[rows, :], 23)
         return (
             c1 + col_sum(g1),
             c2 + col_sum(g2),
@@ -364,32 +462,32 @@
     d_ext = dot_t1(s_sum, w1[0:width, :])
     local_ref[...] = direct + d_ext[0:n_rows, :] + dot_t1(t_sum, w1[width : 2 * width, :])
     d_inc = d_ext[n_rows:, :].astype(BF)
+    bias_row = per_chunk(bsum[...], per)
+    half = width // 2
+    extra = []
     if mode == "FB":
-        for s in range(back_ref.shape[0]):
-            back_ref[s] = d_inc[s * per : (s + 1) * per, :]
+        back_ref[...] = to_chunks(fold(d_inc, per), per)
+        bias_ref[...] = bias_row
     else:
-        half = width // 2
-        quarters = jnp.concatenate([d_inc[:, :half], d_inc[:, half:]], axis=0)
-        rows = dot(spread_rows(per), quarters).reshape(per, 8, half)
-        keep_ref[:, 80:88, :] = rows.astype(BF)
-        send_ref[:, 80:88, :] = jnp.zeros((per, 8, half), BF)
+        bias_row = jnp.concatenate([bias_row, bias_in[...]], axis=1).astype(BF)
+        kept = jnp.concatenate([d_inc[:, :half], d_inc[:, half:], bias_row], axis=0)
+        given = jnp.concatenate([jnp.zeros((4 * per, half), BF), bias_row], axis=0)
+        place = spread_rows(per, 5)
+        extra = [jnp.concatenate([dot(place, kept), dot(place, given)], axis=1)]
+    put(64, [dot_t0(a2[...], l3[...])] + extra)
     sp, tp = halves(s_sum), halves(t_sum)
     grad_w1 = jnp.concatenate(
         [
-            dot_t0(x_n, sp[0:n_rows, :]) + dot_t0(inc_of(), sp[n_rows:, :]),
+            dot_t0(x_n, sp[0:n_rows, :]) + dot_t0(inc[...], sp[n_rows:, :]),
             dot_t0(x_n, tp),
             dot_t0(edges[...], halves(lowv)),
         ],
         axis=0,
     )
-    groups = []
-    for b in range(width // 128):
-        cols = slice(b * 128, (b + 1) * 128)
-        pair = jnp.concatenate([bsum[0:8, cols], bsum[8:16, cols]], axis=1)
-        pair = jnp.concatenate([pair, pair], axis=1)
-        groups.append(jnp.broadcast_to(pair[None], (16, 8, width)))
-    put(0, [grad_w1, jnp.concatenate(groups, axis=0)])
-    put(32, [dot_t0(a1[...], l2[...]), dot_t0(a2[...], l3[...])])
+    put(0, [grad_w1, dot_t0(a1[...], l2[...])])
+    for copy in sent:
+        copy.wait()
+    pltpu.make_async_copy(edge_ref, edge_out, sems.at[23]).wait()
 
 
 VM = pl.BlockSpec(memory_space=pltpu.VMEM)
@@ -415,18 +513,9 @@
     peers = lax.axis_size("dom")
     slots = halo_send.shape[2]
     c = lax.axis_index("pipe")
-    p = lax.axis_index("dom")
     half = width // 2
 
-    vec = jnp.concatenate(
-        [edge_bias[0], edge_gain, node_bias[0], node_gain, jnp.zeros((6, width), F32)], axis=0
-    )
     rec_nodes = swap(node_in)
-    rec_edges = swap(edge_in)
-    rec_vec = swap(vec)
-    rec_w1, rec_wm, rec_n1, rec_nm = (
-        swap(w[0]) for w in (w_edge_in, w_edge_mid, w_node_in, w_node_mid)
-    )
 
     hs, gs, ps = halo_send[0], hang_send[0], parent_rows[0]
     idx = jnp.stack([hs[:, 0], hs[:, 1], gs[:, 0], ps[:, 0], ps[:, 1]] + [hs[:, 0]] * 3)
@@ -435,21 +524,27 @@
     ecol = jnp.stack([edge_target, n_rows + source] + [edge_target] * 6, axis=1)
     erow = jnp.stack([n_rows + source, edge_target] + [edge_target] * 6, axis=0)
 
-    outs = pl.pallas_call(
+    rec_nodes, idx = lax.optimization_barrier((rec_nodes, idx))
+    outs, vec = pl.pallas_call(
         pre_kernel,
-        out_shape=jax.ShapeDtypeStruct((5, peers, width), BF),
-        in_specs=[SM, VM, HB, HB, HB],
-        out_specs=VM,
-        scratch_shapes=[
-            pltpu.VMEM((n_rows, width), BF),
-            pltpu.VMEM((n_rows, width), BF),
-            pltpu.VMEM((n_rows, width), BF),
-            pltpu.SemaphoreType.DMA((3,)),
+        out_shape=[
+            jax.ShapeDtypeStruct((peers, 8, width), BF),
+            jax.ShapeDtypeStruct((16, width), F32),
         ],
+        in_specs=[SM] + [VM] * 5 + [HB] * 3,
+        out_specs=[VM] * 2,
+        scratch_shapes=[pltpu.VMEM((n_rows, width), BF)] * 3 + [pltpu.SemaphoreType.DMA((3,))],
         name="pre",
-    )(c.reshape(1), idx, node_in, rec_nodes, cot_node)
-    got = exchange(jnp.swapaxes(outs, 0, 1))
-    got = jnp.swapaxes(got, 0, 1)
+    )(
+        c.reshape(1), idx, edge_bias, edge_gain, node_bias, node_gain,
+        node_in, rec_nodes, cot_node,
+    )
+    rec_vec = swap(vec)
+    bulk = (edge_in, w_edge_in, w_edge_mid, w_node_in, w_node_mid)
+    bulk, _ = lax.optimization_barrier((bulk, rec_nodes))
+    rec_edges = swap(bulk[0])
+    rec_w1, rec_wm, rec_n1, rec_nm = (swap(w[0]) for w in bulk[1:])
+    got = exchange(outs)
 
     shape = jax.ShapeDtypeStruct
     saved = [shape((e_rows, width), BF)] * 3 + [shape((e_rows, width), F32)] * 3
@@ -458,9 +553,12 @@
     saved += [shape((n_rows, 1), F32)]
 
     def results(mode):
-        chunk = shape((peers, 80 if mode == "FB" else 88, half), BF)
+        chunk = shape((peers, 72 if mode == "FB" else 80, half), BF)
         some = [shape((n_rows, width), F32), shape((e_rows, width), BF), chunk, chunk]
-        return some + ([shape((slots, peers, width), BF)] if mode == "FB" else [])
+        if mode == "FB":
+            some += [shape((peers, 8, 128), BF), shape((peers, 128), F32)]
+            some += [shape((slots * peers, width), BF)]
+        return some
 
     stages = [
         shape((n_rows, width), BF),
@@ -481,9 +579,10 @@
         shape((e_rows, width), BF),
         shape((256, width), BF),
         shape((16, width), F32),
+        shape((slots * peers, width), BF),
     ]
 
-    def run(mode, layer, hang_l=None, gout=None, gedge=None, gi=0, kept=()):
+    def run(mode, layer, got, hang_l=None, gout=None, gedge=None, gi=0, kept=(), bias=()):
         own = (c == layer).astype(jnp.int32)
         scal = jnp.stack([own, c, node_count[0], edge_count[0], jnp.int32(gi)]).astype(jnp.int32)
         back = "B" in mode
@@ -492,58 +591,67 @@
         arrays += [node_in, edge_in, w_edge_in, w_edge_mid, w_node_in, w_node_mid, vec]
         arrays += [rec_nodes, rec_edges, rec_w1, rec_wm, rec_n1, rec_nm, rec_vec]
         arrays += ([gout, gedge] if back else []) + list(kept)
+        far = len(arrays)
+        arrays += list(bias)
         outs = (saved if mode == "F" else []) + (results(mode) if back else [])
-        scratch = stages + ([] if mode == "F" else saved) + work
+        scratch = stages + saved + work + (results(mode)[1:4] if back else [])
+        out_specs = [HB] * len(outs)
+        if back:
+            out_specs = [VM, HB, HB, HB] + [VM] * (len(outs) - 4)
         return pl.pallas_call(
-            functools.partial(unit_kernel, mode, layer),
+            functools.partial(unit_kernel, mode),
             out_shape=outs,
-            in_specs=[SM] + [VM] * near + [HB] * (len(arrays) - near - 1),
-            out_specs=[VM] * len(outs),
+            in_specs=[SM] + [VM] * near + [HB] * (far - near - 1) + [VM] * len(bias),
+            out_specs=out_specs,
             scratch_shapes=[pltpu.VMEM(x.shape, x.dtype) for x in scratch]
-            + [pltpu.SemaphoreType.DMA((9 + SAVED,))],
+            + [pltpu.SemaphoreType.DMA((40,))],
             compiler_params=pltpu.CompilerParams(vmem_limit_bytes=56 * 1024 * 1024),
         )(*arrays)
 
     post = pl.pallas_call(
         post_kernel,
-        out_shape=[shape((n_rows, width), BF), shape((2, peers, half), BF)],
+        out_shape=[shape((n_rows, width), BF), shape((peers, 8, 128), BF)],
         in_specs=[VM] * 3,
         out_specs=[VM] * 2,
         name="post",
     )
 
-    def give_back(local, back):
-        came = exchange(jnp.swapaxes(back, 0, 1))
-        return post(idx, local, jnp.swapaxes(came, 0, 1))
-
     def paired(keep, send):
         return (keep.astype(F32) + swap(send).astype(F32)).astype(BF)
 
-    local1, edge1, keep1, send1, back1 = run("FB", 1, None, cot_node, cot_edge, c)
-    kept0 = run("F", 0)
-    node1, hang1 = give_back(local1, back1)
-    hang_in0 = exchange(jnp.swapaxes(hang1, 0, 1))
+    local1, edge1, keep1, send1, back1, bias1, inc0 = run("FB", 1, got, None, cot_node, cot_edge, c)
+    kept0 = run("F", 0, inc0)
+    node1, hang1 = post(idx, local1, exchange(back1))
+    hang_in0 = exchange(hang1)
     mine1, hang_in0 = lax.optimization_barrier((paired(keep1, send1), hang_in0))
-    part1 = jnp.sum(exchange(mine1).astype(F32), axis=0)
+    came1 = exchange(mine1)
     local0, edge0, keep0, send0 = run(
-        "B", 0, jnp.swapaxes(hang_in0, 0, 1), node1[None], edge1[None], 0, kept0
+        "B", 0, inc0, hang_in0, node1[None], edge1[None], 0, kept0, [bias1]
     )
     up = [(0, 1)]
     down = [(1, 0)]
     first = c == 0
-    came = exchange(paired(keep0, send0))
-    part0, node0 = pl.pallas_call(
+    came0 = exchange(paired(keep0, send0))
+    sums_out = [shape((80, half), F32), shape((n_rows + 80, width), BF)]
+    part1, ship1 = pl.pallas_call(
+        first_kernel,
+        out_shape=sums_out,
+        in_specs=[VM] * 2,
+        out_specs=[VM] * 2,
+        name="sums1",
+    )(came1, node1)
+    part0, ship0 = pl.pallas_call(
         sum_kernel,
-        out_shape=[shape((80, half), F32), shape((n_rows, width), BF)],
+        out_shape=sums_out,
         in_specs=[VM] * 3,
         out_specs=[VM] * 2,
-        name="sums",
-    )(idx, local0, came)
+        name="sums0",
+    )(idx, local0, came0)
     lower = lax.ppermute(edge0, "pipe", down)
     upper = lax.ppermute(edge1, "pipe", up)
     edge_final = jnp.where(first, jnp.stack([edge0, lower]), jnp.stack([upper, edge1]))[None]
-    r0, m0 = lax.ppermute((part0, node0), "pipe", down)
-    r1, m1 = lax.ppermute((part1, node1), "pipe", up)
+    r0 = lax.ppermute(ship0, "pipe", down)
+    r1 = lax.ppermute(ship1, "pipe", up)
     node_final, we, wem, wn, wnm = pl.pallas_call(
         end_kernel,
         out_shape=[
@@ -553,13 +661,11 @@
             shape((1, 16, width), F32),
             shape((1, 2, 8, width), F32),
         ],
-        in_specs=[SM] + [VM] * 8,
+        in_specs=[SM] + [VM] * 6,
         out_specs=[VM] * 5,
         name="end",
-    )(c.reshape(1), part0, part1, r0, r1, node0, node1, m0, m1)
-    mine = jnp.where(first, part0[24:32], part1[24:32])
-    bias = jnp.concatenate([mine[:, 0:128], mine[:, 128:256]], axis=0)
-    bias = lax.dynamic_slice_in_dim(bias, (p % 16) * 8, 8, axis=1)
+    )(c.reshape(1), part0, part1, ship0, ship1, r0, r1)
+    bias = jnp.where(first, part0[76, 0:128], part0[76, 128:256]).reshape(16, 8)
     return (
         node_final,
         edge_final,

time: 229 us -> 212 us (0.926)
  local copies, waits for them, and re-layouts: 26 us -> 15.7 us
  waiting for transfers between devices: 77.9 us -> 71.8 us
  Pallas kernels: 56.4 us -> 61.7 us
  starting transfers between devices: 50.5 us -> 45.2 us
    all_to_all x5, waiting for transfers between devices: 74.3 us -> 67.2 us  [exchange(): return lax.all_to_all(x, 'dom', split_axis=0, concat_axis=0, tiled=True)]
    pallas_call x6 -> x7, Pallas kernels: 54.3 us -> 59.6 us  [the longest x3 47 us: run(): pl.pallas_call(functools.partial(unit_kernel, mode), out_shape=outs, in_s...]
    transpose x3 -> x0, local copies, waits for them, and re-layouts: 5.17 us -> none  [the longest x1 1.96 us: body(): got = exchange(jnp.swapaxes(outs, 0, 1))]
    ppermute x4 -> x2, starting transfers between devices: 8 us -> 3.32 us  [the longest x1 2.04 us: body(): r1 = lax.ppermute(ship1, 'pipe', up)]
    concatenate x1 -> x0, local copies, waits for them, and re-layouts: 4.06 us -> none  [body(): jnp.concatenate([edge_bias[0], edge_gain, node_bias[0], node_gain, jnp.ze...]
    all_to_all x2 -> x0, local copies, waits for them, and re-layouts: 2.56 us -> none  [exchange(): return lax.all_to_all(x, 'dom', split_axis=0, concat_axis=0, tiled=True)]
    ppermute x1, waiting for transfers between devices: 0.01 us -> 2.54 us  [body(): lower = lax.ppermute(edge0, 'pipe', down)]
    unnamed x32 -> x24, local copies, waits for them, and re-layouts: 5.91 us -> 7.46 us
  transfers between devices with their start and end apart: 20 -> 18, of which waited for: 7 -> 9; matrix products, arithmetic and copies ran while one was open for 15% -> 10% of each run, Pallas kernels for 9% -> 11%
where the time goes in v1:
time: 212 us; the launch traced here: 209 us
  waiting for transfers between devices  71.8 us (34%)
  Pallas kernels  61.7 us (29%)
  starting transfers between devices  45.2 us (21%)
  local copies, waits for them, and re-layouts  15.7 us (7%)
  other arithmetic  12.3 us (6%)
  between operations  2.19 us (1%)
    all_to_all x5, waiting for transfers between devices, exchange(): return lax.all_to_all(x, 'dom', split_axis=0, concat_axis=0, tiled=True)  67.2 us
    pallas_call x3, Pallas kernels, run(): pl.pallas_call(functools.partial(unit_kernel, mode), out_shape=outs, in_s...  47 us
    all_to_all x5, starting transfers between devices, exchange(): return lax.all_to_all(x, 'dom', split_axis=0, concat_axis=0, tiled=True)  36.6 us
    convert_element_type x2, other arithmetic, paired(): return (keep.astype(F32) + swap(send).astype(F32)).astype(BF)  8.4 us
    unnamed x24, local copies, waits for them, and re-layouts  7.46 us
  transfers between devices with their start and end apart: 18, of which 9 were waited for; matrix products, arithmetic and copies ran while one was open for 10% of the time, Pallas kernels for 11%

profile of v1, /device:TPU:0, one launch (start us, length us, event | category | flops | bytes accessed | tf_op | source)
XLA Modules:
  0.0 208.8 jit_solution(13882197288945419096)
XLA Ops:
  0.6 0.1 collective-permute-start
  0.7 0.7 slice_bitcast_fusion.2
  1.4 0.8 slice_bitcast_fusion
  2.2 0.6 stack.75.idx.refs_1_
  2.8 0.0 collective-permute-done.rec_all.refs_12_.refs_13_
  2.8 0.5 collective-permute-start.2
  3.3 0.1 collective-permute-start.1
  3.4 0.2 copy-done.4
  3.5 3.4 %pre.1 = (bf16[64,8,512]{2,1,0:T(8,128)(2,1)}, f32[16,512]{1,0:T(8,128)}) custom-call(s32[1]{0:T(128)} %bitcast.core, s32[8,64]{1,0:T(8,128)} %stack.75.idx.refs_1_, f32[1,4,512]{2,1,0:T(4,128)} %eb.1, f32[1,512]{1,0:T(1,128)} %eg.1, f32[1,4,512]{2,1,0:T(4,128)} %nb.1, f32[1,512]{1,0:T(1,128)} %ng.1, bf16[1,2,192,512]{3,2,1,0:T(8,128)(2,1)} %refs_6_.5, ...), custom_call_target="tpu_custom_call" | custom-call | tf_op jit(solution)/shard_map/pre/pallas_call | solution.py:528
  6.9 0.6 collective-permute-start.6
  7.5 0.1 collective-permute-start.3
  7.6 0.4 collective-permute-start.4
  8.0 0.8 collective-permute-done.6.refs_18_.refs_19_
  8.8 0.4 collective-permute-start.5
  9.2 11.8 %all-to-all-start = ((bf16[64,8,512]{2,1,0:T(8,128)(2,1)}), bf16[64,8,512]{2,1,0:T(8,128)(2,1)}, u32[]{:S(2)}, u32[]{:S(2)}) async-start(bf16[64,8,512]{2,1,0:T(8,128)(2,1)} %get-tuple-element.59), calls=%async_computation | async-start | bytes 1048576 | tf_op jit(solution)/shard_map/all_to_all | solution.py:503
  21.0 0.7 stack.82
  21.7 0.7 stack.80
  22.4 0.7 fusion.4
  24.4 0.1 stack.84
  24.5 0.9 copy.39.refs_3_
  25.4 0.6 stack.81.refs_2_
  26.0 0.6 stack.87.refs_0_
  26.6 8.0 %all-to-all-done.refs_4_ = bf16[64,8,512]{2,1,0:T(8,128)(2,1)} async-done(((bf16[64,8,512]{2,1,0:T(8,128)(2,1)}), bf16[64,8,512]{2,1,0:T(8,128)(2,1)}, u32[]{:S(2)}, u32[]{:S(2)}) %all-to-all-start) | async-done | bytes 524320 | tf_op jit(solution)/shard_map/all_to_all | solution.py:503
  34.6 1.2 copy-done
  35.8 1.1 copy-done.1
  37.0 19.4 %shard_map.258 = (f32[192,512]{1,0:T(8,128)}, bf16[768,512]{1,0:T(8,128)(2,1)}, bf16[64,72,256]{2,1,0:T(8,128)(2,1)}, bf16[64,72,256]{2,1,0:T(8,128)(2,1)}, bf16...) custom-call(s32[5]{0:T(128)} %stack.87.refs_0_, s32[8,64]{1,0:T(8,128)} %stack.75.idx.refs_1_, ...), custom_call_target="tpu_custom_call" | custom-call | tf_op jit(solution)/shard_map/pallas_call | solution.py:601
  56.4 0.1 collective-permute-start.7
  56.5 4.8 %all-to-all-start.1 = ((bf16[64,8,128]{2,1,0:T(8,128)(2,1)}), bf16[64,8,128]{2,1,0:T(8,128)(2,1)S(1)}, u32[]{:S(2)}, u32[]{:S(2)}) async-start(bf16[64,8,128]{2,1,0:T(8,128)(2,1)} %get-tuple-element.70), calls=%async_computation.1 | async-start | bytes 262144 | tf_op jit(solution)/shard_map/all_to_all | solution.py:503
  61.4 0.6 stack.78.refs_0_
  62.0 9.9 %shard_map.259 = (bf16[768,512]{1,0:T(8,128)(2,1)}, bf16[768,512]{1,0:T(8,128)(2,1)}, bf16[768,512]{1,0:T(8,128)(2,1)}, f32[768,512]{1,0:T(8,128)}, f32[768,512]...) custom-call(s32[5]{0:T(128)} %stack.78.refs_0_, ...), custom_call_target="tpu_custom_call" | custom-call | tf_op jit(solution)/shard_map/pallas_call | solution.py:601
  71.9 0.7 copy-done.8
  72.6 2.7 %post.1 = (bf16[192,512]{1,0:T(8,128)(2,1)}, bf16[64,8,128]{2,1,0:T(8,128)(2,1)}) custom-call(s32[8,64]{1,0:T(8,128)} %stack.75.idx.refs_1_, f32[192,512]{1,0:T(8,128)} %get-tuple-element.69.local, bf16[64,8,128]{2,1,0:T(8,128)(2,1)} %copy-done.8), custom_call_target="tpu_custom_call" | custom-call | tf_op jit(solution)/shard_map/post/pallas_call | solution.py:624
  75.3 10.3 %all-to-all-start.2 = ((bf16[64,8,128]{2,1,0:T(8,128)(2,1)}), bf16[64,8,128]{2,1,0:T(8,128)(2,1)S(1)}, u32[]{:S(2)}, u32[]{:S(2)}) async-start(bf16[64,8,128]{2,1,0:T(8,128)(2,1)} %get-tuple-element.71), calls=%async_computation.2 | async-start | bytes 262144 | tf_op jit(solution)/shard_map/all_to_all | solution.py:503
  85.7 3.7 %add_convert_fusion.1 = bf16[64,72,256]{2,1,0:T(8,128)(2,1)} fusion(bf16[64,72,256]{2,1,0:T(8,128)(2,1)} %collective-permute-done.7, bf16[64,72,256]{2,1,0:T(8,128)(2,1)S(1)} %copy-done.6), kind=kLoop, calls=%fused_computation.1 | loop fusion | flops 4718592 | bytes 7077888 | tf_op jit(solution)/shard_map/convert_element_type | solution.py:620
  89.4 6.2 %all-to-all-done.2.refs_5_ = bf16[64,8,128]{2,1,0:T(8,128)(2,1)S(1)} async-done(((bf16[64,8,128]{2,1,0:T(8,128)(2,1)}), bf16[64,8,128]{2,1,0:T(8,128)(2,1)S(1)}, u32[]{:S(2)}, u32[]{:S(2)}) %all-to-all-start.2) | async-done | bytes 131104 | tf_op jit(solution)/shard_map/all_to_all | solution.py:503
  95.6 0.7 copy-done.7
  96.3 17.6 %shard_map.260 = (f32[192,512]{1,0:T(8,128)}, bf16[768,512]{1,0:T(8,128)(2,1)}, bf16[64,80,256]{2,1,0:T(8,128)(2,1)}, bf16[64,80,256]{2,1,0:T(8,128)(2,1)}) custom-call(s32[5]{0:T(128)} %stack.78.refs_0_, s32[8,64]{1,0:T(8,128)} %stack.75.idx.refs_1_, s32[8,768]{1,0:T(8,128)} %stack.81.refs_2_, s32[768,8]{1,0:T(8,128)} %copy.39.refs_3_, ...), custom_call_target="tpu_custom_call" | custom-call | tf_op jit(solution)/shard_map/pallas_call | solution.py:601
  113.9 0.1 collective-permute-start.8
  114.0 5.0 %all-to-all-start.4 = ((bf16[64,72,256]{2,1,0:T(8,128)(2,1)}), bf16[64,72,256]{2,1,0:T(8,128)(2,1)S(1)}, u32[]{:S(2)}, u32[]{:S(2)}) async-start(bf16[64,72,256]{2,1,0:T(8,128)(2,1)} %add_convert_fusion.1), calls=%async_computation.4 | async-start | bytes 4718592 | tf_op jit(solution)/shard_map/all_to_all | solution.py:503
  119.0 0.3 collective-permute-done.8
  119.2 4.7 %add_convert_fusion = bf16[64,80,256]{2,1,0:T(8,128)(2,1)} fusion(bf16[64,80,256]{2,1,0:T(8,128)(2,1)} %collective-permute-done.8, bf16[64,80,256]{2,1,0:T(8,128)(2,1)} %get-tuple-element.91), kind=kLoop, calls=%fused_computation | loop fusion | flops 5242880 | bytes 7864320 | tf_op jit(solution)/shard_map/convert_element_type | solution.py:620
  123.9 29.8 %all-to-all-done.4.came = bf16[64,72,256]{2,1,0:T(8,128)(2,1)S(1)} async-done(((bf16[64,72,256]{2,1,0:T(8,128)(2,1)}), bf16[64,72,256]{2,1,0:T(8,128)(2,1)S(1)}, u32[]{:S(2)}, u32[]{:S(2)}) %all-to-all-start.4) | async-done | bytes 2359328 | tf_op jit(solution)/shard_map/all_to_all | solution.py:503
  153.8 1.5 copy-done.3
  155.2 4.7 %all-to-all-start.3 = ((bf16[64,80,256]{2,1,0:T(8,128)(2,1)}), bf16[64,80,256]{2,1,0:T(8,128)(2,1)S(1)}, u32[]{:S(2)}, u32[]{:S(2)}) async-start(bf16[64,80,256]{2,1,0:T(8,128)(2,1)} %add_convert_fusion), calls=%async_computation.3 | async-start | bytes 5242880 | tf_op jit(solution)/shard_map/all_to_all | solution.py:503
  160.0 1.6 collective-permute-start.12
  161.6 1.3 collective-permute-start.11
  162.9 0.5 collective-permute-done.12
  163.4 2.5 %collective-permute-done.11 = bf16[768,512]{1,0:T(8,128)(2,1)S(1)} collective-permute-done((bf16[768,512]{1,0:T(8,128)(2,1)}, bf16[768,512]{1,0:T(8,128)(2,1)S(1)}, u32[]{:S(2)}, u32[]{:S(2)}) %collective-permute-start.11) | collective-permute-done | bytes 786464 | tf_op jit(solution)/shard_map/ppermute | solution.py:650
  166.0 2.5 %maximum_select_fusion = bf16[1,2,768,512]{3,2,1,0:T(8,128)(2,1)} fusion(bf16[1,1,768,512]{3,2,1,0:T(8,128)(2,1)S(1)} %bitcast.35, bf16[1,1,768,512]{3,2,1,0:T(8,128)(2,1)} %bitcast.33, bf16[1,1,768,512]{3,2,1,0:T(8,128)(2,1)S(1)} %bitcast.31, bf16[1,1,768,512]{3,2,1,0:T(8,128)(2,1)S(1)} %bitcast.34, pred[]{:T(512)S(6)} %eq.10), kind=kLoop, calls=%fused_computation.2 | loop fusion | flops 2359296 | bytes 4718593 | tf_op jit(solution)/shard_map/jit(_where)/select_n | solution.py:652
  168.5 2.8 %sums1.1 = (f32[80,256]{1,0:T(8,128)}, bf16[272,512]{1,0:T(8,128)(2,1)}) custom-call(bf16[64,72,256]{2,1,0:T(8,128)(2,1)} %copy-done.3, bf16[192,512]{1,0:T(8,128)(2,1)} %get-tuple-element.73.node), custom_call_target="tpu_custom_call" | custom-call | tf_op jit(solution)/shard_map/sums1/pallas_call | solution.py:636
  171.3 2.0 collective-permute-start.10
  173.3 23.2 %all-to-all-done.3.came = bf16[64,80,256]{2,1,0:T(8,128)(2,1)S(1)} async-done(((bf16[64,80,256]{2,1,0:T(8,128)(2,1)}), bf16[64,80,256]{2,1,0:T(8,128)(2,1)S(1)}, u32[]{:S(2)}, u32[]{:S(2)}) %all-to-all-start.3) | async-done | bytes 2621472 | tf_op jit(solution)/shard_map/all_to_all | solution.py:503
  196.6 1.5 copy-done.2
  198.1 3.6 %sums0.1 = (f32[80,256]{1,0:T(8,128)}, bf16[272,512]{1,0:T(8,128)(2,1)}) custom-call(s32[8,64]{1,0:T(8,128)} %stack.75.idx.refs_1_, f32[192,512]{1,0:T(8,128)} %get-tuple-element.90.local, bf16[64,80,256]{2,1,0:T(8,128)(2,1)} %copy-done.2), custom_call_target="tpu_custom_call" | custom-call | tf_op jit(solution)/shard_map/sums0/pallas_call | solution.py:643
  201.7 0.7 broadcast_select_fusion
  202.4 1.3 collective-permute-start.9
  203.6 0.1 slice_reduce_fusion
  203.7 0.7 broadcast_in_dim.13
  204.4 0.7 slice.53
  205.1 0.6 fusion.9
  205.6 0.4 collective-permute-done.9.r0
  206.0 0.3 copy-done.10
  206.3 0.4 copy-done.11
  206.7 2.1 %end.1 = (bf16[1,2,192,512]{3,2,1,0:T(8,128)(2,1)}, f32[1,24,512]{2,1,0:T(8,128)}, f32[1,2,8,512]{3,2,1,0:T(8,128)}, f32[1,16,512]{2,1,0:T(8,128)}, f32[1,2,8,512]{3,2,1,0:T(8,128)}) custom-call(s32[1]{0:T(128)} %bitcast.core, f32[80,256]{1,0:T(8,128)} %get-tuple-element.93.p0, f32[80,256]{1,0:T(8,128)} %get-tuple-element.95.p1, ...), custom_call_target="tpu_custom_call" | custom-call | tf_op jit(solution)/shard_map/end/pallas_call | solution.py:655
  (25 shorter events, 0.1 us)
Async XLA Ops:
  0.6 2.1 %collective-permute-start = (bf16[1,2,192,512]{3,2,1,0:T(8,128)(2,1)}, bf16[1,2,192,512]{3,2,1,0:T(8,128)(2,1)S(1)}, u32[]{:S(2)}, u32[]{:S(2)}) collective-permute-start(bf16[1,2,192,512]{3,2,1,0:T(8,128)(2,1)} %refs_6_.5), channel_id=1, source_target_pairs={{0,64},{64,0},{1,65},{65,1},{2,66},{66,2},{3,67},{67,3},{4,68},{68... | collective-permute-start | bytes 1179656 | tf_op jit(solution)/shard_map/ppermute | solution.py:499
  2.8 0.7 copy-start.4
  2.8 31.8 %collective-permute-start.2 = (bf16[1536,512]{1,0:T(8,128)(2,1)}, bf16[1536,512]{1,0:T(8,128)(2,1)S(1)}, u32[]{:S(2)}, u32[]{:S(2)}) collective-permute-start(bf16[1536,512]{1,0:T(8,128)(2,1)} %bitcast.26), channel_id=1, source_target_pairs={{0,64},{64,0},{1,65},{65,1},{2,66},{66,2},{3,67},{67,3},{4,68},{68... | collective-permute-start | bytes 4718600 | tf_op jit(solution)/shard_map/ppermute | solution.py:499
  3.3 31.3 %collective-permute-start.1 = (bf16[1,2,768,512]{3,2,1,0:T(8,128)(2,1)}, bf16[1,2,768,512]{3,2,1,0:T(8,128)(2,1)S(1)}, u32[]{:S(2)}, u32[]{:S(2)}) collective-permute-start(bf16[1,2,768,512]{3,2,1,0:T(8,128)(2,1)} %refs_7_.5), channel_id=1, source_target_pairs={{0,64},{64,0},{1,65},{65,1},{2,66},{66,2},{3,67},{67,3},{4,68},{68... | collective-permute-start | bytes 4718600 | tf_op jit(solution)/shard_map/ppermute | solution.py:499
  6.9 1.9 collective-permute-start.6
  7.5 27.1 %collective-permute-start.3 = (bf16[2,512,512]{2,1,0:T(8,128)(2,1)}, bf16[2,512,512]{2,1,0:T(8,128)(2,1)}, u32[]{:S(2)}, u32[]{:S(2)}) collective-permute-start(bf16[2,512,512]{2,1,0:T(8,128)(2,1)} %bitcast.27), channel_id=1, source_target_pairs={{0,64},{64,0},{1,65},{65,1},{2,66},{66,2},{3,67},{67,3},{4,68},{68... | collective-permute-start | bytes 3145736 | tf_op jit(solution)/shard_map/ppermute | solution.py:499
  7.6 27.0 %collective-permute-start.4 = (bf16[1024,512]{1,0:T(8,128)(2,1)}, bf16[1024,512]{1,0:T(8,128)(2,1)}, u32[]{:S(2)}, u32[]{:S(2)}) collective-permute-start(bf16[1024,512]{1,0:T(8,128)(2,1)} %bitcast.28), channel_id=1, source_target_pairs={{0,64},{64,0},{1,65},{65,1},{2,66},{66,2},{3,67},{67,3},{4,68},{68... | collective-permute-start | bytes 3145736 | tf_op jit(solution)/shard_map/ppermute | solution.py:499
  8.8 25.8 %copy-start.9 = (f32[16,512]{1,0:T(8,128)}, f32[16,512]{1,0:T(8,128)S(1)}, u32[]{:S(2)}) copy-start(f32[16,512]{1,0:T(8,128)S(1)} %collective-permute-done.6.refs_18_.refs_19_) | copy-start | bytes 98308
  8.8 25.8 %collective-permute-start.5 = (bf16[2,512,512]{2,1,0:T(8,128)(2,1)}, bf16[2,512,512]{2,1,0:T(8,128)(2,1)}, u32[]{:S(2)}, u32[]{:S(2)}) collective-permute-start(bf16[2,512,512]{2,1,0:T(8,128)(2,1)} %bitcast.29), channel_id=1, source_target_pairs={{0,64},{64,0},{1,65},{65,1},{2,66},{66,2},{3,67},{67,3},{4,68},{68... | collective-permute-start | bytes 3145736 | tf_op jit(solution)/shard_map/ppermute | solution.py:499
  9.2 25.4 %all-to-all-start = ((bf16[64,8,512]{2,1,0:T(8,128)(2,1)}), bf16[64,8,512]{2,1,0:T(8,128)(2,1)}, u32[]{:S(2)}, u32[]{:S(2)}) async-start(bf16[64,8,512]{2,1,0:T(8,128)(2,1)} %get-tuple-element.59), calls=%async_computation | async-start | bytes 1048576 | tf_op jit(solution)/shard_map/all_to_all | solution.py:503
  34.6 1.2 copy-start
  35.8 1.1 copy-start.1
  56.4 29.3 %collective-permute-start.7 = (bf16[64,72,256]{2,1,0:T(8,128)(2,1)}, bf16[64,72,256]{2,1,0:T(8,128)(2,1)}, u32[]{:S(2)}, u32[]{:S(2)}) collective-permute-start(bf16[64,72,256]{2,1,0:T(8,128)(2,1)} %get-tuple-element.68), channel_id=1, source_target_pairs={{0,64},{64,0},{1,65},{65,1},{2,66},{66,2},{3,67},{67,3},{4,68},{68... | collective-permute-start | bytes 7077896 | tf_op jit(solution)/shard_map/ppermute | solution.py:499
  56.5 15.4 %all-to-all-start.1 = ((bf16[64,8,128]{2,1,0:T(8,128)(2,1)}), bf16[64,8,128]{2,1,0:T(8,128)(2,1)S(1)}, u32[]{:S(2)}, u32[]{:S(2)}) async-start(bf16[64,8,128]{2,1,0:T(8,128)(2,1)} %get-tuple-element.70), calls=%async_computation.1 | async-start | bytes 262144 | tf_op jit(solution)/shard_map/all_to_all | solution.py:503
  62.0 23.7 %copy-start.6 = (bf16[64,72,256]{2,1,0:T(8,128)(2,1)S(1)}, bf16[64,72,256]{2,1,0:T(8,128)(2,1)}, u32[]{:S(2)}) copy-start(bf16[64,72,256]{2,1,0:T(8,128)(2,1)} %get-tuple-element.67) | copy-start | bytes 7077892
  71.9 0.7 copy-start.8
  75.3 20.3 %all-to-all-start.2 = ((bf16[64,8,128]{2,1,0:T(8,128)(2,1)}), bf16[64,8,128]{2,1,0:T(8,128)(2,1)S(1)}, u32[]{:S(2)}, u32[]{:S(2)}) async-start(bf16[64,8,128]{2,1,0:T(8,128)(2,1)} %get-tuple-element.71), calls=%async_computation.2 | async-start | bytes 262144 | tf_op jit(solution)/shard_map/all_to_all | solution.py:503
  95.6 0.7 copy-start.7
  113.9 5.3 %collective-permute-start.8 = (bf16[64,80,256]{2,1,0:T(8,128)(2,1)}, bf16[64,80,256]{2,1,0:T(8,128)(2,1)}, u32[]{:S(2)}, u32[]{:S(2)}) collective-permute-start(bf16[64,80,256]{2,1,0:T(8,128)(2,1)} %get-tuple-element.92), channel_id=1, source_target_pairs={{0,64},{64,0},{1,65},{65,1},{2,66},{66,2},{3,67},{67,3},{4,68},{68... | collective-permute-start | bytes 7864328 | tf_op jit(solution)/shard_map/ppermute | solution.py:499
  114.0 39.8 %all-to-all-start.4 = ((bf16[64,72,256]{2,1,0:T(8,128)(2,1)}), bf16[64,72,256]{2,1,0:T(8,128)(2,1)S(1)}, u32[]{:S(2)}, u32[]{:S(2)}) async-start(bf16[64,72,256]{2,1,0:T(8,128)(2,1)} %add_convert_fusion.1), calls=%async_computation.4 | async-start | bytes 4718592 | tf_op jit(solution)/shard_map/all_to_all | solution.py:503
  123.9 36.0 %copy-start.5 = (bf16[768,512]{1,0:T(8,128)(2,1)S(1)}, bf16[768,512]{1,0:T(8,128)(2,1)}, u32[]{:S(2)}) copy-start(bf16[768,512]{1,0:T(8,128)(2,1)} %get-tuple-element.74) | copy-start | bytes 2359300
  153.8 1.5 copy-start.3
  155.2 41.4 %all-to-all-start.3 = ((bf16[64,80,256]{2,1,0:T(8,128)(2,1)}), bf16[64,80,256]{2,1,0:T(8,128)(2,1)S(1)}, u32[]{:S(2)}, u32[]{:S(2)}) async-start(bf16[64,80,256]{2,1,0:T(8,128)(2,1)} %add_convert_fusion), calls=%async_computation.3 | async-start | bytes 5242880 | tf_op jit(solution)/shard_map/all_to_all | solution.py:503
  160.0 3.5 %collective-permute-start.12 = (bf16[768,512]{1,0:T(8,128)(2,1)S(1)}, bf16[768,512]{1,0:T(8,128)(2,1)S(1)}, u32[]{:S(2)}, u32[]{:S(2)}) collective-permute-start(bf16[768,512]{1,0:T(8,128)(2,1)S(1)} %copy-done.5), channel_id=1, source_target_pairs={{0,64},{1,65},{2,66},{3,67},{4,68},{5,69},{6,70},{7,71},{8,72},{9,... | collective-permute-start | bytes 2359304 | tf_op jit(solution)/shard_map/ppermute | solution.py:651
  161.6 4.4 %collective-permute-start.11 = (bf16[768,512]{1,0:T(8,128)(2,1)}, bf16[768,512]{1,0:T(8,128)(2,1)S(1)}, u32[]{:S(2)}, u32[]{:S(2)}) collective-permute-start(bf16[768,512]{1,0:T(8,128)(2,1)} %get-tuple-element.99), channel_id=1, source_target_pairs={{64,0},{65,1},{66,2},{67,3},{68,4},{69,5},{70,6},{71,7},{72,8},{73... | collective-permute-start | bytes 2359304 | tf_op jit(solution)/shard_map/ppermute | solution.py:650
  171.3 34.3 %collective-permute-start.10 = (bf16[272,512]{1,0:T(8,128)(2,1)}, bf16[272,512]{1,0:T(8,128)(2,1)S(1)}, u32[]{:S(2)}, u32[]{:S(2)}) collective-permute-start(bf16[272,512]{1,0:T(8,128)(2,1)} %get-tuple-element.97.s1), channel_id=1, source_target_pairs={{0,64},{1,65},{2,66},{3,67},{4,68},{5,69},{6,70},{7,71},{8,72},{9,... | collective-permute-start | bytes 835592 | tf_op jit(solution)/shard_map/ppermute | solution.py:654
  196.6 1.5 copy-start.2
  202.4 3.7 %collective-permute-start.9 = (bf16[272,512]{1,0:T(8,128)(2,1)}, bf16[272,512]{1,0:T(8,128)(2,1)S(1)}, u32[]{:S(2)}, u32[]{:S(2)}) collective-permute-start(bf16[272,512]{1,0:T(8,128)(2,1)} %get-tuple-element.96.s0), channel_id=1, source_target_pairs={{64,0},{65,1},{66,2},{67,3},{68,4},{69,5},{70,6},{71,7},{72,8},{73... | collective-permute-start | bytes 835592 | tf_op jit(solution)/shard_map/ppermute | solution.py:653
  205.6 0.7 copy-start.10
  206.0 0.7 copy-start.11

commit v2 on v1

--- a/solution.py
+++ b/solution.py
@@ -10,7 +10,6 @@
 EPS = 1e-05
 BF = jnp.bfloat16
 F32 = jnp.float32
-BLOCK = 256
 
 
 def dot(a, b):
@@ -211,7 +210,7 @@
         return [next(take) for _ in range(n)]
 
     forward_part, backward_part = "F" in mode, "B" in mode
-    scal, idx, erow, ecol, got = some(5)
+    scal, idx, erow, got = some(4)
     per = idx.shape[1]
     hang_in = next(take) if mode == "B" else None
     own_nodes, own_edges, *own_rest = some(7)
@@ -229,7 +228,7 @@
     oh, a1, a2, s1, s2, nrm, inv, _, _, _, _, _, _, _ = saved
     q, msg, gout, gedge, l1, l2, l3, gag, bsum, inc = some(10)
     if backward_part:
-        edge_ref, keep_ref, send_ref = some(3)
+        edge_ref, left_ref, right_ref = some(3)
     sems = next(take)
     sent = []
 
@@ -274,7 +273,8 @@
     n_rows = nodes.shape[0]
     e_rows = edges.shape[0]
     width = nodes.shape[1]
-    blocks = e_rows // BLOCK
+    block = e_rows // (2 if mode == "F" else 1)
+    blocks = e_rows // block
 
     def live_of(start, size, count):
         return (lax.broadcasted_iota(jnp.int32, (size, 1), 0) + start < count).astype(F32)
@@ -297,14 +297,10 @@
             from_hanging = unfold(from_chunks(hang_in[...], 4), per)
 
     if forward_part:
-        def build(i, _):
-            rows = pl.ds(pl.multiple_of(i * BLOCK, BLOCK), BLOCK)
-            grid = lax.broadcasted_iota(jnp.int32, (BLOCK, width), 1)
-            hit = (grid == ecol[rows, 0:1]) | (grid == ecol[rows, 1:2])
-            oh[rows, :] = jnp.where(hit, 1.0, 0.0).astype(BF)
-            return 0
-
-        lax.fori_loop(0, blocks, build, 0)
+        ecol = jnp.transpose(erow[...])
+        grid = lax.broadcasted_iota(jnp.int32, (e_rows, width), 1)
+        hit = (grid == ecol[:, 0:1]) | (grid == ecol[:, 1:2])
+        oh[...] = jnp.where(hit, 1.0, 0.0).astype(BF)
         ready(0)
         ready(2)
         q[0:n_rows, :] = dot(nodes[...], w1[width : 2 * width, :]).astype(BF)
@@ -318,8 +314,8 @@
             ce.start()
 
         def forward(i, _):
-            start = pl.multiple_of(i * BLOCK, BLOCK)
-            rows = pl.ds(start, BLOCK)
+            start = pl.multiple_of(i * block, block)
+            rows = pl.ds(start, block)
             z = dot(oh[rows, :], q[...]) + dot(edges[rows, :], w1[2 * width :, :]) + eb[0]
             low, slope = act(z)
             a1[rows, :] = low
@@ -329,8 +325,8 @@
             s2[rows, :] = slope
             normed, rstd = norm_rows(dot(low, wm[1]) + eb[2])
             nrm[rows, :] = normed
-            inv[rows, :] = rstd
-            msg[rows, :] = ((normed * eg + eb[3]) * live_of(start, BLOCK, edge_count)).astype(BF)
+            inv[rows, :] = jnp.broadcast_to(rstd, (block, 128))
+            msg[rows, :] = ((normed * eg + eb[3]) * live_of(start, block, edge_count)).astype(BF)
             if mode == "F":
                 for k in range(7):
                     leave(saved[k].at[rows, :], saved_out[k].at[rows, :], 9 + k)
@@ -345,6 +341,7 @@
         na1, ns1 = act(dot(x_n, n1[0:width, :]) + dot(agg, n1[width:, :]) + nb[0])
         na2, ns2 = act(dot(na1, nm[0]) + nb[1])
         nn, nr = norm_rows(dot(na2, nm[1]) + nb[2])
+        nr = jnp.broadcast_to(nr, (n_rows, 128))
         for ref, value in zip(saved[7:], (agg, na1, na2, ns1, ns2, nn, nr)):
             ref[...] = value
 
@@ -367,23 +364,31 @@
     x_n = nodes[...]
     agg, na1, na2, ns1, ns2, nn, nr = (ref[...] for ref in saved[7:])
 
-    def halves(low):
-        half = width // 2
-        f = low.astype(F32)
-        swapped = jnp.concatenate([f[:, half:], f[:, :half]], axis=1)
-        return jnp.where(c == 0, f, swapped).astype(BF)
-
     def put(first, pieces):
         half = width // 2
         tile = jnp.concatenate([x.reshape(64, -1, x.shape[-1]) for x in pieces], axis=1)
         n = tile.shape[1]
-        keep_ref[:, first : first + n, :] = tile[:, :, :half].astype(BF)
-        send_ref[:, first : first + n, :] = tile[:, :, half:].astype(BF)
-        for ref, dst in ((send_ref, send_out), (keep_ref, keep_out)):
-            part = (slice(None), pl.ds(first, n), slice(None))
-            copy = pltpu.make_async_copy(ref.at[part], dst.at[part], sems.at[24 + len(sent)])
-            copy.start()
-            sent.append(copy)
+        left_ref[:, first : first + n, :] = tile[:, :, :half].astype(BF)
+        right_ref[:, first : first + n, :] = tile[:, :, half:].astype(BF)
+        part = (slice(None), pl.ds(first, n), slice(None))
+
+        def copies(one, two):
+            return [
+                pltpu.make_async_copy(ref.at[part], out.at[part], sems.at[24 + len(sent) * 2 + k])
+                for k, (ref, out) in enumerate(((two, send_out), (one, keep_out)))
+            ]
+
+        @pl.when(c == 0)
+        def _():
+            for copy in copies(left_ref, right_ref):
+                copy.start()
+
+        @pl.when(c == 1)
+        def _():
+            for copy in copies(right_ref, left_ref):
+                copy.start()
+
+        sent.append(copies(left_ref, right_ref))
 
     cg.wait()
     hung = jnp.max(
@@ -398,7 +403,7 @@
     gy = grad_new * live_of(0, n_rows, node_count)
     bsum[8:9, :] = col_sum(gy)
     bsum[9:10, :] = col_sum(gy * nn)
-    g3 = norm_back(gy, ng, nn, nr)
+    g3 = norm_back(gy, ng, nn, nr[:, 0:1])
     bsum[7:8, :] = col_sum(g3)
     low3 = g3.astype(BF)
     g2 = dot_t1(low3, nm[1]) * ns2
@@ -410,9 +415,8 @@
     direct = grad_new + dot_t1(low1, n1[0:width, :])
     gag[0:n_rows, :] = dot_t1(low1, n1[width:, :]).astype(BF)
     gag[n_rows:, :] = jnp.zeros((gag.shape[0] - n_rows, width), BF)
-    low1p = halves(low1)
-    put(32, [jnp.concatenate([dot_t0(x_n, low1p), dot_t0(agg, low1p)], axis=0)])
-    put(48, [dot_t0(na1, halves(low2)), dot_t0(na2, halves(low3))])
+    put(32, [jnp.concatenate([dot_t0(x_n, low1), dot_t0(agg, low1)], axis=0)])
+    put(48, [dot_t0(na1, low2), dot_t0(na2, low3)])
 
     if not forward_part:
         ready(1)
@@ -424,18 +428,18 @@
     gk = gag.shape[0]
 
     def backward(i, carry):
-        start = pl.multiple_of(i * BLOCK, BLOCK)
-        rows = pl.ds(start, BLOCK)
+        start = pl.multiple_of(i * block, block)
+        rows = pl.ds(start, block)
         c1, c2, c3, c4, c5 = carry
         ge = gedge[rows, :].astype(F32)
-        gy = (dot(oh[rows, 0:gk], gag[...]) + ge) * live_of(start, BLOCK, edge_count)
+        gy = (dot(oh[rows, 0:gk], gag[...]) + ge) * live_of(start, block, edge_count)
         normed = nrm[rows, :]
-        g3 = norm_back(gy, eg, normed, inv[rows, :])
+        g3 = norm_back(gy, eg, normed, inv[rows, 0:1])
         low = g3.astype(BF)
-        l3[rows, :] = halves(low)
+        l3[rows, :] = low
         g2 = dot_t1(low, wm[1]) * s2[rows, :]
         low = g2.astype(BF)
-        l2[rows, :] = halves(low)
+        l2[rows, :] = low
         g1 = dot_t1(low, wm[0]) * s1[rows, :]
         low = g1.astype(BF)
         l1[rows, :] = low
@@ -472,21 +476,23 @@
         bias_row = jnp.concatenate([bias_row, bias_in[...]], axis=1).astype(BF)
         kept = jnp.concatenate([d_inc[:, :half], d_inc[:, half:], bias_row], axis=0)
         given = jnp.concatenate([jnp.zeros((4 * per, half), BF), bias_row], axis=0)
+        one = jnp.where(c == 0, kept.astype(F32), given.astype(F32)).astype(BF)
+        two = jnp.where(c == 0, given.astype(F32), kept.astype(F32)).astype(BF)
         place = spread_rows(per, 5)
-        extra = [jnp.concatenate([dot(place, kept), dot(place, given)], axis=1)]
+        extra = [jnp.concatenate([dot(place, one), dot(place, two)], axis=1)]
     put(64, [dot_t0(a2[...], l3[...])] + extra)
-    sp, tp = halves(s_sum), halves(t_sum)
     grad_w1 = jnp.concatenate(
         [
-            dot_t0(x_n, sp[0:n_rows, :]) + dot_t0(inc[...], sp[n_rows:, :]),
-            dot_t0(x_n, tp),
-            dot_t0(edges[...], halves(lowv)),
+            dot_t0(x_n, s_sum[0:n_rows, :]) + dot_t0(inc[...], s_sum[n_rows:, :]),
+            dot_t0(x_n, t_sum),
+            dot_t0(edges[...], lowv),
         ],
         axis=0,
     )
     put(0, [grad_w1, dot_t0(a1[...], l2[...])])
-    for copy in sent:
-        copy.wait()
+    for pair in sent:
+        for copy in pair:
+            copy.wait()
     pltpu.make_async_copy(edge_ref, edge_out, sems.at[23]).wait()
 
 
@@ -519,11 +525,6 @@
 
     hs, gs, ps = halo_send[0], hang_send[0], parent_rows[0]
     idx = jnp.stack([hs[:, 0], hs[:, 1], gs[:, 0], ps[:, 0], ps[:, 1]] + [hs[:, 0]] * 3)
-    k = edge_source - n_rows
-    source = jnp.where(k < 0, edge_source, n_rows + (k % slots) * peers + k // slots)
-    ecol = jnp.stack([edge_target, n_rows + source] + [edge_target] * 6, axis=1)
-    erow = jnp.stack([n_rows + source, edge_target] + [edge_target] * 6, axis=0)
-
     rec_nodes, idx = lax.optimization_barrier((rec_nodes, idx))
     outs, vec = pl.pallas_call(
         pre_kernel,
@@ -544,13 +545,20 @@
     bulk, _ = lax.optimization_barrier((bulk, rec_nodes))
     rec_edges = swap(bulk[0])
     rec_w1, rec_wm, rec_n1, rec_nm = (swap(w[0]) for w in bulk[1:])
+    bulk = (rec_edges, rec_w1, rec_wm, rec_n1, rec_nm, edge_source, edge_target)
+    bulk = lax.optimization_barrier(bulk)
+    rec_edges, rec_w1, rec_wm, rec_n1, rec_nm, edge_source, edge_target = bulk
+    k = edge_source - n_rows
+    source = jnp.where(k < 0, edge_source, n_rows + (k % slots) * peers + k // slots)
+    erow = jnp.stack([n_rows + source, edge_target] + [edge_target] * 6, axis=0)
+
     got = exchange(outs)
 
     shape = jax.ShapeDtypeStruct
     saved = [shape((e_rows, width), BF)] * 3 + [shape((e_rows, width), F32)] * 3
-    saved += [shape((e_rows, 1), F32)]
+    saved += [shape((e_rows, 128), F32)]
     saved += [shape((n_rows, width), BF)] * 3 + [shape((n_rows, width), F32)] * 3
-    saved += [shape((n_rows, 1), F32)]
+    saved += [shape((n_rows, 128), F32)]
 
     def results(mode):
         chunk = shape((peers, 72 if mode == "FB" else 80, half), BF)
@@ -586,7 +594,7 @@
         own = (c == layer).astype(jnp.int32)
         scal = jnp.stack([own, c, node_count[0], edge_count[0], jnp.int32(gi)]).astype(jnp.int32)
         back = "B" in mode
-        arrays = [scal, idx, erow, ecol, got] + ([hang_l] if mode == "B" else [])
+        arrays = [scal, idx, erow, got] + ([hang_l] if mode == "B" else [])
         near = len(arrays) - 1
         arrays += [node_in, edge_in, w_edge_in, w_edge_mid, w_node_in, w_node_mid, vec]
         arrays += [rec_nodes, rec_edges, rec_w1, rec_wm, rec_n1, rec_nm, rec_vec]

time: 212 us -> 202 us (0.953)
  Pallas kernels: 61.7 us -> 57.1 us
  local copies, waits for them, and re-layouts: 15.7 us -> 11.6 us
    pallas_call x3, Pallas kernels: 47 us -> 42.4 us  [run(): pl.pallas_call(functools.partial(unit_kernel, mode), out_shape=outs, in_s...]
    unnamed x24, local copies, waits for them, and re-layouts: 7.46 us -> 4.98 us
  transfers between devices with their start and end apart: 18 -> 18, of which waited for: 9 -> 8; matrix products, arithmetic and copies ran while one was open for 10% -> 10% of each run, Pallas kernels for 11% -> 11%
where the time goes in v2:
time: 202 us; the launch traced here: 199 us
  waiting for transfers between devices  72 us (36%)
  Pallas kernels  57.1 us (28%)
  starting transfers between devices  44.2 us (22%)
  other arithmetic  12.4 us (6%)
  local copies, waits for them, and re-layouts  11.6 us (6%)
  between operations  2.19 us (1%)
    all_to_all x5, waiting for transfers between devices, exchange(): return lax.all_to_all(x, 'dom', split_axis=0, concat_axis=0, tiled=True)  68.3 us
    pallas_call x3, Pallas kernels, run(): pl.pallas_call(functools.partial(unit_kernel, mode), out_shape=outs, in_s...  42.4 us
    all_to_all x5, starting transfers between devices, exchange(): return lax.all_to_all(x, 'dom', split_axis=0, concat_axis=0, tiled=True)  36.5 us
    convert_element_type x2, other arithmetic, paired(): return (keep.astype(F32) + swap(send).astype(F32)).astype(BF)  8.4 us
    unnamed x24, local copies, waits for them, and re-layouts  4.98 us
  transfers between devices with their start and end apart: 18, of which 8 were waited for; matrix products, arithmetic and copies ran while one was open for 10% of the time, Pallas kernels for 11%

profile of v2, /device:TPU:0, one launch (start us, length us, event | category | flops | bytes accessed | tf_op | source)
XLA Modules:
  0.0 199.5 jit_solution(11178050948540457609)
XLA Ops:
  0.6 0.1 collective-permute-start
  0.7 0.7 slice_bitcast_fusion.2
  1.4 0.8 slice_bitcast_fusion
  2.2 0.6 stack.60.idx.refs_1_
  2.8 0.0 collective-permute-done.rec_all.refs_11_.refs_12_
  2.8 0.5 collective-permute-start.2
  3.3 0.1 collective-permute-start.1
  3.4 0.4 collective-permute-start.3
  3.8 0.1 collective-permute-start.4
  3.9 0.4 collective-permute-start.5
  4.3 3.4 %pre.1 = (bf16[64,8,512]{2,1,0:T(8,128)(2,1)}, f32[16,512]{1,0:T(8,128)}) custom-call(s32[1]{0:T(128)} %bitcast.core, s32[8,64]{1,0:T(8,128)} %stack.60.idx.refs_1_, f32[1,4,512]{2,1,0:T(4,128)} %eb.1, f32[1,512]{1,0:T(1,128)} %eg.1, f32[1,4,512]{2,1,0:T(4,128)} %nb.1, f32[1,512]{1,0:T(1,128)} %ng.1, bf16[1,2,192,512]{3,2,1,0:T(8,128)(2,1)} %refs_5_.5, ...), custom_call_target="tpu_custom_call" | custom-call | tf_op jit(solution)/shard_map/pre/pallas_call | solution.py:529
  7.7 11.8 %all-to-all-start = ((bf16[64,8,512]{2,1,0:T(8,128)(2,1)}), bf16[64,8,512]{2,1,0:T(8,128)(2,1)}, u32[]{:S(2)}, u32[]{:S(2)}) async-start(bf16[64,8,512]{2,1,0:T(8,128)(2,1)} %get-tuple-element.73), calls=%async_computation | async-start | bytes 1048576 | tf_op jit(solution)/shard_map/all_to_all | solution.py:509
  20.8 0.6 stack.69.refs_0_
  21.4 0.0 collective-permute-done.3.refs_14_.refs_15_
  21.4 0.0 collective-permute-start.6
  21.4 0.0 collective-permute-done.4.refs_15_.refs_16_
  21.4 0.0 collective-permute-done.5.refs_16_.refs_17_
  21.5 0.0 collective-permute-done.2.refs_13_.refs_14_
  21.5 0.0 copy-start.1
  21.5 0.7 fusion.4
  22.2 0.7 stack.65
  23.0 0.7 stack.66.refs_2_
  23.6 9.5 %all-to-all-done.refs_3_ = bf16[64,8,512]{2,1,0:T(8,128)(2,1)} async-done(((bf16[64,8,512]{2,1,0:T(8,128)(2,1)}), bf16[64,8,512]{2,1,0:T(8,128)(2,1)}, u32[]{:S(2)}, u32[]{:S(2)}) %all-to-all-start) | async-done | bytes 524320 | tf_op jit(solution)/shard_map/all_to_all | solution.py:509
  33.1 16.8 %shard_map.258 = (f32[192,512]{1,0:T(8,128)}, bf16[768,512]{1,0:T(8,128)(2,1)}, bf16[64,72,256]{2,1,0:T(8,128)(2,1)}, bf16[64,72,256]{2,1,0:T(8,128)(2,1)}, bf16...) custom-call(s32[5]{0:T(128)} %stack.69.refs_0_, s32[8,64]{1,0:T(8,128)} %stack.60.idx.refs_1_, ...), custom_call_target="tpu_custom_call" | custom-call | tf_op jit(solution)/shard_map/pallas_call | solution.py:609
  49.9 0.1 collective-permute-start.7
  50.0 4.9 %all-to-all-start.1 = ((bf16[64,8,128]{2,1,0:T(8,128)(2,1)}), bf16[64,8,128]{2,1,0:T(8,128)(2,1)S(1)}, u32[]{:S(2)}, u32[]{:S(2)}) async-start(bf16[64,8,128]{2,1,0:T(8,128)(2,1)} %get-tuple-element.84), calls=%async_computation.1 | async-start | bytes 262144 | tf_op jit(solution)/shard_map/all_to_all | solution.py:509
  54.9 0.6 stack.63.refs_0_
  55.5 9.3 %shard_map.259 = (bf16[768,512]{1,0:T(8,128)(2,1)}, bf16[768,512]{1,0:T(8,128)(2,1)}, bf16[768,512]{1,0:T(8,128)(2,1)}, f32[768,512]{1,0:T(8,128)}, f32[768,512]...) custom-call(s32[5]{0:T(128)} %stack.63.refs_0_, ...), custom_call_target="tpu_custom_call" | custom-call | tf_op jit(solution)/shard_map/pallas_call | solution.py:609
  64.9 0.0 all-to-all-done.1.came
  64.9 0.6 copy-done.8
  65.5 2.7 %post.1 = (bf16[192,512]{1,0:T(8,128)(2,1)}, bf16[64,8,128]{2,1,0:T(8,128)(2,1)}) custom-call(s32[8,64]{1,0:T(8,128)} %stack.60.idx.refs_1_, f32[192,512]{1,0:T(8,128)} %get-tuple-element.83.local, bf16[64,8,128]{2,1,0:T(8,128)(2,1)} %copy-done.8), custom_call_target="tpu_custom_call" | custom-call | tf_op jit(solution)/shard_map/post/pallas_call | solution.py:632
  68.3 10.1 %all-to-all-start.2 = ((bf16[64,8,128]{2,1,0:T(8,128)(2,1)}), bf16[64,8,128]{2,1,0:T(8,128)(2,1)S(1)}, u32[]{:S(2)}, u32[]{:S(2)}) async-start(bf16[64,8,128]{2,1,0:T(8,128)(2,1)} %get-tuple-element.85), calls=%async_computation.2 | async-start | bytes 262144 | tf_op jit(solution)/shard_map/all_to_all | solution.py:509
  78.4 3.7 %add_convert_fusion.1 = bf16[64,72,256]{2,1,0:T(8,128)(2,1)} fusion(bf16[64,72,256]{2,1,0:T(8,128)(2,1)} %collective-permute-done.7, bf16[64,72,256]{2,1,0:T(8,128)(2,1)S(1)} %copy-done.6), kind=kLoop, calls=%fused_computation.1 | loop fusion | flops 4718592 | bytes 7077888 | tf_op jit(solution)/shard_map/convert_element_type | solution.py:628
  82.1 6.2 %all-to-all-done.2.refs_4_ = bf16[64,8,128]{2,1,0:T(8,128)(2,1)S(1)} async-done(((bf16[64,8,128]{2,1,0:T(8,128)(2,1)}), bf16[64,8,128]{2,1,0:T(8,128)(2,1)S(1)}, u32[]{:S(2)}, u32[]{:S(2)}) %all-to-all-start.2) | async-done | bytes 131104 | tf_op jit(solution)/shard_map/all_to_all | solution.py:509
  88.3 0.7 copy-done.7
  89.0 16.2 %shard_map.260 = (f32[192,512]{1,0:T(8,128)}, bf16[768,512]{1,0:T(8,128)(2,1)}, bf16[64,80,256]{2,1,0:T(8,128)(2,1)}, bf16[64,80,256]{2,1,0:T(8,128)(2,1)}) custom-call(s32[5]{0:T(128)} %stack.63.refs_0_, s32[8,64]{1,0:T(8,128)} %stack.60.idx.refs_1_, s32[8,768]{1,0:T(8,128)} %stack.66.refs_2_, bf16[128,512]{1,0:T(8,128)(2,1)} %get-tuple-element.80.refs_3_, ...), custom_call_target="tpu_custom_call" | custom-call | tf_op jit(solution)/shard_map/pallas_call | solution.py:609
  105.2 0.1 collective-permute-start.8
  105.3 5.0 %all-to-all-start.4 = ((bf16[64,72,256]{2,1,0:T(8,128)(2,1)}), bf16[64,72,256]{2,1,0:T(8,128)(2,1)S(1)}, u32[]{:S(2)}, u32[]{:S(2)}) async-start(bf16[64,72,256]{2,1,0:T(8,128)(2,1)} %add_convert_fusion.1), calls=%async_computation.4 | async-start | bytes 4718592 | tf_op jit(solution)/shard_map/all_to_all | solution.py:509
  110.2 0.3 collective-permute-done.8
  110.5 4.7 %add_convert_fusion = bf16[64,80,256]{2,1,0:T(8,128)(2,1)} fusion(bf16[64,80,256]{2,1,0:T(8,128)(2,1)} %collective-permute-done.8, bf16[64,80,256]{2,1,0:T(8,128)(2,1)} %get-tuple-element.105), kind=kLoop, calls=%fused_computation | loop fusion | flops 5242880 | bytes 7864320 | tf_op jit(solution)/shard_map/convert_element_type | solution.py:628
  115.2 29.5 %all-to-all-done.4.came = bf16[64,72,256]{2,1,0:T(8,128)(2,1)S(1)} async-done(((bf16[64,72,256]{2,1,0:T(8,128)(2,1)}), bf16[64,72,256]{2,1,0:T(8,128)(2,1)S(1)}, u32[]{:S(2)}, u32[]{:S(2)}) %all-to-all-start.4) | async-done | bytes 2359328 | tf_op jit(solution)/shard_map/all_to_all | solution.py:509
  144.7 1.5 copy-done.3
  146.2 4.7 %all-to-all-start.3 = ((bf16[64,80,256]{2,1,0:T(8,128)(2,1)}), bf16[64,80,256]{2,1,0:T(8,128)(2,1)S(1)}, u32[]{:S(2)}, u32[]{:S(2)}) async-start(bf16[64,80,256]{2,1,0:T(8,128)(2,1)} %add_convert_fusion), calls=%async_computation.3 | async-start | bytes 5242880 | tf_op jit(solution)/shard_map/all_to_all | solution.py:509
  150.9 1.4 collective-permute-start.12
  152.3 1.3 collective-permute-start.11
  153.6 0.5 collective-permute-done.12
  154.1 2.5 %collective-permute-done.11 = bf16[768,512]{1,0:T(8,128)(2,1)S(1)} collective-permute-done((bf16[768,512]{1,0:T(8,128)(2,1)}, bf16[768,512]{1,0:T(8,128)(2,1)S(1)}, u32[]{:S(2)}, u32[]{:S(2)}) %collective-permute-start.11) | collective-permute-done | bytes 786464 | tf_op jit(solution)/shard_map/ppermute | solution.py:658
  156.7 2.5 %maximum_select_fusion = bf16[1,2,768,512]{3,2,1,0:T(8,128)(2,1)} fusion(bf16[1,1,768,512]{3,2,1,0:T(8,128)(2,1)S(1)} %bitcast.35, bf16[1,1,768,512]{3,2,1,0:T(8,128)(2,1)} %bitcast.33, bf16[1,1,768,512]{3,2,1,0:T(8,128)(2,1)S(1)} %bitcast.31, bf16[1,1,768,512]{3,2,1,0:T(8,128)(2,1)S(1)} %bitcast.34, pred[]{:T(512)S(6)} %eq.10), kind=kLoop, calls=%fused_computation.2 | loop fusion | flops 2359296 | bytes 4718593 | tf_op jit(solution)/shard_map/jit(_where)/select_n | solution.py:660
  159.2 2.8 %sums1.1 = (f32[80,256]{1,0:T(8,128)}, bf16[272,512]{1,0:T(8,128)(2,1)}) custom-call(bf16[64,72,256]{2,1,0:T(8,128)(2,1)} %copy-done.3, bf16[192,512]{1,0:T(8,128)(2,1)} %get-tuple-element.87.node), custom_call_target="tpu_custom_call" | custom-call | tf_op jit(solution)/shard_map/sums1/pallas_call | solution.py:644
  162.0 2.0 %collective-permute-start.10 = (bf16[272,512]{1,0:T(8,128)(2,1)}, bf16[272,512]{1,0:T(8,128)(2,1)S(1)}, u32[]{:S(2)}, u32[]{:S(2)}) collective-permute-start(bf16[272,512]{1,0:T(8,128)(2,1)} %get-tuple-element.111.s1), channel_id=1, source_target_pairs={{0,64},{1,65},{2,66},{3,67},{4,68},{5,69},{6,70},{7,71},{8,72},{9,... | collective-permute-start | bytes 835592 | tf_op jit(solution)/shard_map/ppermute | solution.py:662
  164.1 23.1 %all-to-all-done.3.came = bf16[64,80,256]{2,1,0:T(8,128)(2,1)S(1)} async-done(((bf16[64,80,256]{2,1,0:T(8,128)(2,1)}), bf16[64,80,256]{2,1,0:T(8,128)(2,1)S(1)}, u32[]{:S(2)}, u32[]{:S(2)}) %all-to-all-start.3) | async-done | bytes 2621472 | tf_op jit(solution)/shard_map/all_to_all | solution.py:509
  187.2 1.5 copy-done.2
  188.7 3.6 %sums0.1 = (f32[80,256]{1,0:T(8,128)}, bf16[272,512]{1,0:T(8,128)(2,1)}) custom-call(s32[8,64]{1,0:T(8,128)} %stack.60.idx.refs_1_, f32[192,512]{1,0:T(8,128)} %get-tuple-element.104.local, bf16[64,80,256]{2,1,0:T(8,128)(2,1)} %copy-done.2), custom_call_target="tpu_custom_call" | custom-call | tf_op jit(solution)/shard_map/sums0/pallas_call | solution.py:651
  192.3 0.7 broadcast_select_fusion
  193.0 1.3 collective-permute-start.9
  194.3 0.1 slice_reduce_fusion
  194.4 0.7 broadcast_in_dim.13
  195.1 0.7 slice.53
  195.7 0.6 fusion.9
  196.3 0.0 collective-permute-done.10.r1
  196.3 0.4 collective-permute-done.9.r0
  196.7 0.3 copy-done.10
  197.0 0.4 copy-done.11
  197.4 2.1 %end.1 = (bf16[1,2,192,512]{3,2,1,0:T(8,128)(2,1)}, f32[1,24,512]{2,1,0:T(8,128)}, f32[1,2,8,512]{3,2,1,0:T(8,128)}, f32[1,16,512]{2,1,0:T(8,128)}, f32[1,2,8,512]{3,2,1,0:T(8,128)}) custom-call(s32[1]{0:T(128)} %bitcast.core, f32[80,256]{1,0:T(8,128)} %get-tuple-element.107.p0, f32[80,256]{1,0:T(8,128)} %get-tuple-element.109.p1, ...), custom_call_target="tpu_custom_call" | custom-call | tf_op jit(solution)/shard_map/end/pallas_call | solution.py:663
  (21 shorter events, 0.0 us)
Async XLA Ops:
  0.6 2.1 %collective-permute-start = (bf16[1,2,192,512]{3,2,1,0:T(8,128)(2,1)}, bf16[1,2,192,512]{3,2,1,0:T(8,128)(2,1)S(1)}, u32[]{:S(2)}, u32[]{:S(2)}) collective-permute-start(bf16[1,2,192,512]{3,2,1,0:T(8,128)(2,1)} %refs_5_.5), channel_id=1, source_target_pairs={{0,64},{64,0},{1,65},{65,1},{2,66},{66,2},{3,67},{67,3},{4,68},{68... | collective-permute-start | bytes 1179656 | tf_op jit(solution)/shard_map/ppermute | solution.py:505
  2.8 1.5 copy-start.4
  2.8 18.7 %collective-permute-start.2 = (bf16[1536,512]{1,0:T(8,128)(2,1)}, bf16[1536,512]{1,0:T(8,128)(2,1)S(1)}, u32[]{:S(2)}, u32[]{:S(2)}) collective-permute-start(bf16[1536,512]{1,0:T(8,128)(2,1)} %bitcast.26), channel_id=1, source_target_pairs={{0,64},{64,0},{1,65},{65,1},{2,66},{66,2},{3,67},{67,3},{4,68},{68... | collective-permute-start | bytes 4718600 | tf_op jit(solution)/shard_map/ppermute | solution.py:505
  3.3 18.2 %collective-permute-start.1 = (bf16[1,2,768,512]{3,2,1,0:T(8,128)(2,1)}, bf16[1,2,768,512]{3,2,1,0:T(8,128)(2,1)S(1)}, u32[]{:S(2)}, u32[]{:S(2)}) collective-permute-start(bf16[1,2,768,512]{3,2,1,0:T(8,128)(2,1)} %refs_6_.5), channel_id=1, source_target_pairs={{0,64},{64,0},{1,65},{65,1},{2,66},{66,2},{3,67},{67,3},{4,68},{68... | collective-permute-start | bytes 4718600 | tf_op jit(solution)/shard_map/ppermute | solution.py:505
  3.4 18.1 %collective-permute-start.3 = (bf16[2,512,512]{2,1,0:T(8,128)(2,1)}, bf16[2,512,512]{2,1,0:T(8,128)(2,1)}, u32[]{:S(2)}, u32[]{:S(2)}) collective-permute-start(bf16[2,512,512]{2,1,0:T(8,128)(2,1)} %bitcast.27), channel_id=1, source_target_pairs={{0,64},{64,0},{1,65},{65,1},{2,66},{66,2},{3,67},{67,3},{4,68},{68... | collective-permute-start | bytes 3145736 | tf_op jit(solution)/shard_map/ppermute | solution.py:505
  3.8 17.7 %collective-permute-start.4 = (bf16[1024,512]{1,0:T(8,128)(2,1)}, bf16[1024,512]{1,0:T(8,128)(2,1)}, u32[]{:S(2)}, u32[]{:S(2)}) collective-permute-start(bf16[1024,512]{1,0:T(8,128)(2,1)} %bitcast.28), channel_id=1, source_target_pairs={{0,64},{64,0},{1,65},{65,1},{2,66},{66,2},{3,67},{67,3},{4,68},{68... | collective-permute-start | bytes 3145736 | tf_op jit(solution)/shard_map/ppermute | solution.py:505
  3.9 17.6 %collective-permute-start.5 = (bf16[2,512,512]{2,1,0:T(8,128)(2,1)}, bf16[2,512,512]{2,1,0:T(8,128)(2,1)}, u32[]{:S(2)}, u32[]{:S(2)}) collective-permute-start(bf16[2,512,512]{2,1,0:T(8,128)(2,1)} %bitcast.29), channel_id=1, source_target_pairs={{0,64},{64,0},{1,65},{65,1},{2,66},{66,2},{3,67},{67,3},{4,68},{68... | collective-permute-start | bytes 3145736 | tf_op jit(solution)/shard_map/ppermute | solution.py:505
  7.7 25.4 %all-to-all-start = ((bf16[64,8,512]{2,1,0:T(8,128)(2,1)}), bf16[64,8,512]{2,1,0:T(8,128)(2,1)}, u32[]{:S(2)}, u32[]{:S(2)}) async-start(bf16[64,8,512]{2,1,0:T(8,128)(2,1)} %get-tuple-element.73), calls=%async_computation | async-start | bytes 1048576 | tf_op jit(solution)/shard_map/all_to_all | solution.py:509
  21.4 2.2 %collective-permute-start.6 = (f32[16,512]{1,0:T(8,128)}, f32[16,512]{1,0:T(8,128)S(1)}, u32[]{:S(2)}, u32[]{:S(2)}) collective-permute-start(f32[16,512]{1,0:T(8,128)} %get-tuple-element.74.refs_10_.refs_11_), channel_id=1, source_target_pairs={{0,64},{64,0},{1,65},{65,1},{2,66},{66,2},{3,67},{67,3},{4,68},{68... | collective-permute-start | bytes 98312 | tf_op jit(solution)/shard_map/ppermute | solution.py:505
  21.5 11.6 %copy-start = (bf16[1536,512]{1,0:T(8,128)(2,1)}, bf16[1536,512]{1,0:T(8,128)(2,1)S(1)}, u32[]{:S(2)}) copy-start(bf16[1536,512]{1,0:T(8,128)(2,1)S(1)} %collective-permute-done.2.refs_13_.refs_14_) | copy-start | bytes 4718596
  21.5 11.6 %copy-start.1 = (bf16[1,2,768,512]{3,2,1,0:T(8,128)(2,1)}, bf16[1,2,768,512]{3,2,1,0:T(8,128)(2,1)S(1)}, u32[]{:S(2)}) copy-start(bf16[1,2,768,512]{3,2,1,0:T(8,128)(2,1)S(1)} %collective-permute-done.1.refs_12_.refs_13_) | copy-start | bytes 4718596
  23.6 9.5 %copy-start.9 = (f32[16,512]{1,0:T(8,128)}, f32[16,512]{1,0:T(8,128)S(1)}, u32[]{:S(2)}) copy-start(f32[16,512]{1,0:T(8,128)S(1)} %collective-permute-done.6.refs_17_.refs_18_) | copy-start | bytes 98308
  49.9 28.4 %collective-permute-start.7 = (bf16[64,72,256]{2,1,0:T(8,128)(2,1)}, bf16[64,72,256]{2,1,0:T(8,128)(2,1)}, u32[]{:S(2)}, u32[]{:S(2)}) collective-permute-start(bf16[64,72,256]{2,1,0:T(8,128)(2,1)} %get-tuple-element.82), channel_id=1, source_target_pairs={{0,64},{64,0},{1,65},{65,1},{2,66},{66,2},{3,67},{67,3},{4,68},{68... | collective-permute-start | bytes 7077896 | tf_op jit(solution)/shard_map/ppermute | solution.py:505
  50.0 14.8 %all-to-all-start.1 = ((bf16[64,8,128]{2,1,0:T(8,128)(2,1)}), bf16[64,8,128]{2,1,0:T(8,128)(2,1)S(1)}, u32[]{:S(2)}, u32[]{:S(2)}) async-start(bf16[64,8,128]{2,1,0:T(8,128)(2,1)} %get-tuple-element.84), calls=%async_computation.1 | async-start | bytes 262144 | tf_op jit(solution)/shard_map/all_to_all | solution.py:509
  55.5 22.9 %copy-start.6 = (bf16[64,72,256]{2,1,0:T(8,128)(2,1)S(1)}, bf16[64,72,256]{2,1,0:T(8,128)(2,1)}, u32[]{:S(2)}) copy-start(bf16[64,72,256]{2,1,0:T(8,128)(2,1)} %get-tuple-element.81) | copy-start | bytes 7077892
  64.9 0.7 copy-start.8
  68.3 20.1 %all-to-all-start.2 = ((bf16[64,8,128]{2,1,0:T(8,128)(2,1)}), bf16[64,8,128]{2,1,0:T(8,128)(2,1)S(1)}, u32[]{:S(2)}, u32[]{:S(2)}) async-start(bf16[64,8,128]{2,1,0:T(8,128)(2,1)} %get-tuple-element.85), calls=%async_computation.2 | async-start | bytes 262144 | tf_op jit(solution)/shard_map/all_to_all | solution.py:509
  88.3 0.7 copy-start.7
  105.2 5.3 %collective-permute-start.8 = (bf16[64,80,256]{2,1,0:T(8,128)(2,1)}, bf16[64,80,256]{2,1,0:T(8,128)(2,1)}, u32[]{:S(2)}, u32[]{:S(2)}) collective-permute-start(bf16[64,80,256]{2,1,0:T(8,128)(2,1)} %get-tuple-element.106), channel_id=1, source_target_pairs={{0,64},{64,0},{1,65},{65,1},{2,66},{66,2},{3,67},{67,3},{4,68},{68... | collective-permute-start | bytes 7864328 | tf_op jit(solution)/shard_map/ppermute | solution.py:505
  105.3 39.4 %all-to-all-start.4 = ((bf16[64,72,256]{2,1,0:T(8,128)(2,1)}), bf16[64,72,256]{2,1,0:T(8,128)(2,1)S(1)}, u32[]{:S(2)}, u32[]{:S(2)}) async-start(bf16[64,72,256]{2,1,0:T(8,128)(2,1)} %add_convert_fusion.1), calls=%async_computation.4 | async-start | bytes 4718592 | tf_op jit(solution)/shard_map/all_to_all | solution.py:509
  115.2 35.7 %copy-start.5 = (bf16[768,512]{1,0:T(8,128)(2,1)S(1)}, bf16[768,512]{1,0:T(8,128)(2,1)}, u32[]{:S(2)}) copy-start(bf16[768,512]{1,0:T(8,128)(2,1)} %get-tuple-element.88) | copy-start | bytes 2359300
  144.7 1.5 copy-start.3
  146.2 41.1 %all-to-all-start.3 = ((bf16[64,80,256]{2,1,0:T(8,128)(2,1)}), bf16[64,80,256]{2,1,0:T(8,128)(2,1)S(1)}, u32[]{:S(2)}, u32[]{:S(2)}) async-start(bf16[64,80,256]{2,1,0:T(8,128)(2,1)} %add_convert_fusion), calls=%async_computation.3 | async-start | bytes 5242880 | tf_op jit(solution)/shard_map/all_to_all | solution.py:509
  150.9 3.2 %collective-permute-start.12 = (bf16[768,512]{1,0:T(8,128)(2,1)S(1)}, bf16[768,512]{1,0:T(8,128)(2,1)S(1)}, u32[]{:S(2)}, u32[]{:S(2)}) collective-permute-start(bf16[768,512]{1,0:T(8,128)(2,1)S(1)} %copy-done.5), channel_id=1, source_target_pairs={{0,64},{1,65},{2,66},{3,67},{4,68},{5,69},{6,70},{7,71},{8,72},{9,... | collective-permute-start | bytes 2359304 | tf_op jit(solution)/shard_map/ppermute | solution.py:659
  152.3 4.4 %collective-permute-start.11 = (bf16[768,512]{1,0:T(8,128)(2,1)}, bf16[768,512]{1,0:T(8,128)(2,1)S(1)}, u32[]{:S(2)}, u32[]{:S(2)}) collective-permute-start(bf16[768,512]{1,0:T(8,128)(2,1)} %get-tuple-element.113), channel_id=1, source_target_pairs={{64,0},{65,1},{66,2},{67,3},{68,4},{69,5},{70,6},{71,7},{72,8},{73... | collective-permute-start | bytes 2359304 | tf_op jit(solution)/shard_map/ppermute | solution.py:658
  162.0 34.3 %collective-permute-start.10 = (bf16[272,512]{1,0:T(8,128)(2,1)}, bf16[272,512]{1,0:T(8,128)(2,1)S(1)}, u32[]{:S(2)}, u32[]{:S(2)}) collective-permute-start(bf16[272,512]{1,0:T(8,128)(2,1)} %get-tuple-element.111.s1), channel_id=1, source_target_pairs={{0,64},{1,65},{2,66},{3,67},{4,68},{5,69},{6,70},{7,71},{8,72},{9,... | collective-permute-start | bytes 835592 | tf_op jit(solution)/shard_map/ppermute | solution.py:662
  187.2 1.5 copy-start.2
  193.0 3.7 %collective-permute-start.9 = (bf16[272,512]{1,0:T(8,128)(2,1)}, bf16[272,512]{1,0:T(8,128)(2,1)S(1)}, u32[]{:S(2)}, u32[]{:S(2)}) collective-permute-start(bf16[272,512]{1,0:T(8,128)(2,1)} %get-tuple-element.110.s0), channel_id=1, source_target_pairs={{64,0},{65,1},{66,2},{67,3},{68,4},{69,5},{70,6},{71,7},{72,8},{73... | collective-permute-start | bytes 835592 | tf_op jit(solution)/shard_map/ppermute | solution.py:661
  196.3 0.7 copy-start.10
  196.7 0.7 copy-start.11

commit v3 on v2

--- a/solution.py
+++ b/solution.py
@@ -54,6 +54,25 @@
         for b in range(rows.shape[1] // 128):
             parts.append(rows[s * per : (s + 1) * per, b * 128 : (b + 1) * 128])
     return jnp.concatenate(parts, axis=0)
+
+
+def close_rows(pieces, per):
+    rows = fold(pieces, per)
+    rows = jnp.concatenate([rows, jnp.zeros((4 * per, 128), BF)], axis=0)
+    step = 8 * per
+    return jnp.concatenate(
+        [to_chunks(rows[g * step : (g + 1) * step], per) for g in range(3)], axis=2
+    )
+
+
+def open_rows(chunks, count):
+    per = chunks.shape[0]
+    parts = [from_chunks(chunks[:, :, g * 128 : (g + 1) * 128], 8) for g in range(3)]
+    rows = jnp.concatenate(parts, axis=0)
+    step = 4 * per
+    return jnp.concatenate(
+        [unfold(rows[k * step : (k + 1) * step], per) for k in range(count)], axis=0
+    )
 
 
 def unfold(rows, per):
@@ -123,7 +142,7 @@
     top = jnp.where(c == 0, other.astype(F32), own.astype(F32)).astype(BF)
     pairs = ((h0, low), (h1, low), (h0, top), (h1, top), (hg, cotb[...]))
     pieces = jnp.concatenate([dot_t0(hot, src).astype(BF) for hot, src in pairs], axis=0)
-    out[...] = to_chunks(pieces, idx.shape[1])
+    out[...] = close_rows(pieces, idx.shape[1])
 
 
 def post_kernel(idx, local, came, node_out, hang_out):
@@ -200,7 +219,7 @@
         write(part_of(r1), p1[...], r1, s1)
 
 
-SAVED = 14
+SAVED = 7
 
 
 def unit_kernel(mode, *refs):
@@ -209,44 +228,31 @@
     def some(n):
         return [next(take) for _ in range(n)]
 
-    forward_part, backward_part = "F" in mode, "B" in mode
     scal, idx, erow, got = some(4)
     per = idx.shape[1]
-    hang_in = next(take) if mode == "B" else None
+    hang_in = next(take) if mode == 0 else None
     own_nodes, own_edges, *own_rest = some(7)
     recs = some(7)
-    gout_all, gedge_all = some(2) if backward_part else (None, None)
-    kept_in = some(SAVED) if mode == "B" else None
-    bias_in = next(take) if mode == "B" else None
-    saved_out = some(SAVED) if mode == "F" else None
-    if backward_part:
-        local_ref, edge_out, keep_out, send_out = some(4)
-        back_ref, bias_ref, inc_out = some(3) if mode == "FB" else (None, None, None)
+    gout_all, gedge_all = some(2)
+    bias_in = next(take) if mode == 0 else None
+    local_ref, edge_out, keep_out, send_out = some(4)
+    back_ref, bias_ref, inc_out = some(3) if mode == 1 else (None, None, None)
     dsts = some(7)
     nodes, edges, w1, wm, n1, nm, vec = dsts
     saved = some(SAVED)
-    oh, a1, a2, s1, s2, nrm, inv, _, _, _, _, _, _, _ = saved
+    oh, a1, a2, s1, s2, nrm, inv = saved
     q, msg, gout, gedge, l1, l2, l3, gag, bsum, inc = some(10)
-    if backward_part:
-        edge_ref, left_ref, right_ref = some(3)
+    edge_ref, left_ref, right_ref = some(3)
     sems = next(take)
     sent = []
 
-    def leave(src, dst, sem):
-        pltpu.make_async_copy(src, dst, sems.at[sem]).start()
 
     is_own, c, node_count, edge_count, gi = (scal[i] for i in range(5))
     owns = [own_nodes.at[0, c], own_edges.at[0, c]] + [r.at[0] for r in own_rest[:4]]
     owns = owns + [own_rest[4]]
     recs = [recs[0].at[0, c], recs[1].at[0, c]] + recs[2:]
-    if backward_part:
-        cg = pltpu.make_async_copy(gout_all.at[gi], gout, sems.at[7])
-        ce = pltpu.make_async_copy(gedge_all.at[gi], gedge, sems.at[8])
-    loads = []
-    if mode == "B":
-        loads = [
-            pltpu.make_async_copy(kept_in[k], saved[k], sems.at[9 + k]) for k in range(SAVED)
-        ]
+    cg = pltpu.make_async_copy(gout_all.at[gi], gout, sems.at[7])
+    ce = pltpu.make_async_copy(gedge_all.at[gi], gedge, sems.at[8])
 
     def fetch(order):
         @pl.when(is_own == 1)
@@ -259,13 +265,7 @@
             for k in order:
                 pltpu.make_async_copy(recs[k], dsts[k], sems.at[k]).start()
 
-    if mode == "B":
-        cg.start()
-        for k in range(7, SAVED):
-            loads[k].start()
-        fetch([6, 0, 5, 4])
-    else:
-        fetch([6, 0, 2, 1, 3])
+    fetch([6, 0, 2, 1, 3])
 
     def ready(k):
         pltpu.make_async_copy(recs[k], dsts[k], sems.at[k]).wait()
@@ -273,7 +273,7 @@
     n_rows = nodes.shape[0]
     e_rows = edges.shape[0]
     width = nodes.shape[1]
-    block = e_rows // (2 if mode == "F" else 1)
+    block = e_rows
     blocks = e_rows // block
 
     def live_of(start, size, count):
@@ -286,83 +286,57 @@
     ng = vec[9:10, :]
     to_target = hot_rows(erow[1:2, :], n_rows).astype(BF)
 
-    if mode == "FB":
-        pieces = from_chunks(got[...], 5)
+    if mode == 1:
+        pieces = open_rows(got[...], 5)
         inc_out[...] = pieces[0 : 2 * per]
         inc[...] = pieces[2 * per : 4 * per]
         from_hanging = pieces[4 * per :]
     else:
         inc[...] = got[...]
-        if backward_part:
-            from_hanging = unfold(from_chunks(hang_in[...], 4), per)
-
-    if forward_part:
-        ecol = jnp.transpose(erow[...])
-        grid = lax.broadcasted_iota(jnp.int32, (e_rows, width), 1)
-        hit = (grid == ecol[:, 0:1]) | (grid == ecol[:, 1:2])
-        oh[...] = jnp.where(hit, 1.0, 0.0).astype(BF)
-        ready(0)
-        ready(2)
-        q[0:n_rows, :] = dot(nodes[...], w1[width : 2 * width, :]).astype(BF)
-        q[n_rows : 2 * n_rows, :] = dot(nodes[...], w1[0:width, :]).astype(BF)
-        q[2 * n_rows :, :] = dot(inc[...], w1[0:width, :]).astype(BF)
-        ready(1)
-        ready(3)
-        fetch([4, 5])
-        if backward_part:
-            cg.start()
-            ce.start()
-
-        def forward(i, _):
-            start = pl.multiple_of(i * block, block)
-            rows = pl.ds(start, block)
-            z = dot(oh[rows, :], q[...]) + dot(edges[rows, :], w1[2 * width :, :]) + eb[0]
-            low, slope = act(z)
-            a1[rows, :] = low
-            s1[rows, :] = slope
-            low, slope = act(dot(low, wm[0]) + eb[1])
-            a2[rows, :] = low
-            s2[rows, :] = slope
-            normed, rstd = norm_rows(dot(low, wm[1]) + eb[2])
-            nrm[rows, :] = normed
-            inv[rows, :] = jnp.broadcast_to(rstd, (block, 128))
-            msg[rows, :] = ((normed * eg + eb[3]) * live_of(start, block, edge_count)).astype(BF)
-            if mode == "F":
-                for k in range(7):
-                    leave(saved[k].at[rows, :], saved_out[k].at[rows, :], 9 + k)
-            return 0
-
-        lax.fori_loop(0, blocks, forward, 0)
-
-        agg = dot(to_target, msg[...]).astype(BF)
-        ready(4)
-        ready(5)
-        x_n = nodes[...]
-        na1, ns1 = act(dot(x_n, n1[0:width, :]) + dot(agg, n1[width:, :]) + nb[0])
-        na2, ns2 = act(dot(na1, nm[0]) + nb[1])
-        nn, nr = norm_rows(dot(na2, nm[1]) + nb[2])
-        nr = jnp.broadcast_to(nr, (n_rows, 128))
-        for ref, value in zip(saved[7:], (agg, na1, na2, ns1, ns2, nn, nr)):
-            ref[...] = value
-
-    if not backward_part:
-        for k in range(7, SAVED):
-            leave(saved[k], saved_out[k], 9 + k)
-        for k in range(SAVED):
-            pltpu.make_async_copy(saved[k], saved_out[k], sems.at[9 + k]).wait()
-        return
-    if not forward_part:
-        ready(0)
-        ready(4)
-        ready(5)
-        for one in loads[7:]:
-            one.wait()
-        for one in loads[:7]:
-            one.start()
-        fetch([3, 2, 1])
-        ce.start()
+        from_hanging = unfold(from_chunks(hang_in[...], 4), per)
+
+    ecol = jnp.transpose(erow[...])
+    grid = lax.broadcasted_iota(jnp.int32, (e_rows, width), 1)
+    hit = (grid == ecol[:, 0:1]) | (grid == ecol[:, 1:2])
+    oh[...] = jnp.where(hit, 1.0, 0.0).astype(BF)
+    ready(0)
+    ready(2)
+    q[0:n_rows, :] = dot(nodes[...], w1[width : 2 * width, :]).astype(BF)
+    q[n_rows : 2 * n_rows, :] = dot(nodes[...], w1[0:width, :]).astype(BF)
+    q[2 * n_rows :, :] = dot(inc[...], w1[0:width, :]).astype(BF)
+    ready(1)
+    ready(3)
+    fetch([4, 5])
+    cg.start()
+    ce.start()
+
+    def forward(i, _):
+        start = pl.multiple_of(i * block, block)
+        rows = pl.ds(start, block)
+        z = dot(oh[rows, :], q[...]) + dot(edges[rows, :], w1[2 * width :, :]) + eb[0]
+        low, slope = act(z)
+        a1[rows, :] = low
+        s1[rows, :] = slope
+        low, slope = act(dot(low, wm[0]) + eb[1])
+        a2[rows, :] = low
+        s2[rows, :] = slope
+        normed, rstd = norm_rows(dot(low, wm[1]) + eb[2])
+        nrm[rows, :] = normed
+        inv[rows, :] = jnp.broadcast_to(rstd, (block, 128))
+        msg[rows, :] = ((normed * eg + eb[3]) * live_of(start, block, edge_count)).astype(BF)
+        return 0
+
+    lax.fori_loop(0, blocks, forward, 0)
+
+    agg = dot(to_target, msg[...]).astype(BF)
+    ready(4)
+    ready(5)
     x_n = nodes[...]
-    agg, na1, na2, ns1, ns2, nn, nr = (ref[...] for ref in saved[7:])
+    na1, ns1 = act(dot(x_n, n1[0:width, :]) + dot(agg, n1[width:, :]) + nb[0])
+    na2, ns2 = act(dot(na1, nm[0]) + nb[1])
+    nn, nr = norm_rows(dot(na2, nm[1]) + nb[2])
+    nr = jnp.broadcast_to(nr, (n_rows, 128))
+
 
     def put(first, pieces):
         half = width // 2
@@ -418,12 +392,6 @@
     put(32, [jnp.concatenate([dot_t0(x_n, low1), dot_t0(agg, low1)], axis=0)])
     put(48, [dot_t0(na1, low2), dot_t0(na2, low3)])
 
-    if not forward_part:
-        ready(1)
-        ready(2)
-        ready(3)
-        for one in loads[:7]:
-            one.wait()
     ce.wait()
     gk = gag.shape[0]
 
@@ -444,7 +412,7 @@
         low = g1.astype(BF)
         l1[rows, :] = low
         edge_ref[rows, :] = (ge + dot_t1(low, w1[2 * width :, :])).astype(BF)
-        leave(edge_ref.at[rows, :], edge_out.at[rows, :], 23)
+        pltpu.make_async_copy(edge_ref.at[rows, :], edge_out.at[rows, :], sems.at[23]).start()
         return (
             c1 + col_sum(g1),
             c2 + col_sum(g2),
@@ -469,7 +437,7 @@
     bias_row = per_chunk(bsum[...], per)
     half = width // 2
     extra = []
-    if mode == "FB":
+    if mode == 1:
         back_ref[...] = to_chunks(fold(d_inc, per), per)
         bias_ref[...] = bias_row
     else:
@@ -529,7 +497,7 @@
     outs, vec = pl.pallas_call(
         pre_kernel,
         out_shape=[
-            jax.ShapeDtypeStruct((peers, 8, width), BF),
+            jax.ShapeDtypeStruct((peers, 8, 384), BF),
             jax.ShapeDtypeStruct((16, width), F32),
         ],
         in_specs=[SM] + [VM] * 5 + [HB] * 3,
@@ -557,13 +525,11 @@
     shape = jax.ShapeDtypeStruct
     saved = [shape((e_rows, width), BF)] * 3 + [shape((e_rows, width), F32)] * 3
     saved += [shape((e_rows, 128), F32)]
-    saved += [shape((n_rows, width), BF)] * 3 + [shape((n_rows, width), F32)] * 3
-    saved += [shape((n_rows, 128), F32)]
 
     def results(mode):
-        chunk = shape((peers, 72 if mode == "FB" else 80, half), BF)
+        chunk = shape((peers, 72 if mode == 1 else 80, half), BF)
         some = [shape((n_rows, width), F32), shape((e_rows, width), BF), chunk, chunk]
-        if mode == "FB":
+        if mode == 1:
             some += [shape((peers, 8, 128), BF), shape((peers, 128), F32)]
             some += [shape((slots * peers, width), BF)]
         return some
@@ -590,30 +556,25 @@
         shape((slots * peers, width), BF),
     ]
 
-    def run(mode, layer, got, hang_l=None, gout=None, gedge=None, gi=0, kept=(), bias=()):
+    def run(layer, got, gout, gedge, gi, hang_l=(), bias=()):
         own = (c == layer).astype(jnp.int32)
         scal = jnp.stack([own, c, node_count[0], edge_count[0], jnp.int32(gi)]).astype(jnp.int32)
-        back = "B" in mode
-        arrays = [scal, idx, erow, got] + ([hang_l] if mode == "B" else [])
+        arrays = [scal, idx, erow, got] + list(hang_l)
         near = len(arrays) - 1
         arrays += [node_in, edge_in, w_edge_in, w_edge_mid, w_node_in, w_node_mid, vec]
         arrays += [rec_nodes, rec_edges, rec_w1, rec_wm, rec_n1, rec_nm, rec_vec]
-        arrays += ([gout, gedge] if back else []) + list(kept)
+        arrays += [gout, gedge]
         far = len(arrays)
         arrays += list(bias)
-        outs = (saved if mode == "F" else []) + (results(mode) if back else [])
-        scratch = stages + saved + work + (results(mode)[1:4] if back else [])
-        out_specs = [HB] * len(outs)
-        if back:
-            out_specs = [VM, HB, HB, HB] + [VM] * (len(outs) - 4)
+        outs = results(layer)
         return pl.pallas_call(
-            functools.partial(unit_kernel, mode),
+            functools.partial(unit_kernel, layer),
             out_shape=outs,
             in_specs=[SM] + [VM] * near + [HB] * (far - near - 1) + [VM] * len(bias),
-            out_specs=out_specs,
-            scratch_shapes=[pltpu.VMEM(x.shape, x.dtype) for x in scratch]
+            out_specs=[VM, HB, HB, HB] + [VM] * (len(outs) - 4),
+            scratch_shapes=[pltpu.VMEM(x.shape, x.dtype) for x in stages + saved + work + outs[1:4]]
             + [pltpu.SemaphoreType.DMA((40,))],
-            compiler_params=pltpu.CompilerParams(vmem_limit_bytes=56 * 1024 * 1024),
+            compiler_params=pltpu.CompilerParams(vmem_limit_bytes=60 * 1024 * 1024),
         )(*arrays)
 
     post = pl.pallas_call(
@@ -627,14 +588,13 @@
     def paired(keep, send):
         return (keep.astype(F32) + swap(send).astype(F32)).astype(BF)
 
-    local1, edge1, keep1, send1, back1, bias1, inc0 = run("FB", 1, got, None, cot_node, cot_edge, c)
-    kept0 = run("F", 0, inc0)
+    local1, edge1, keep1, send1, back1, bias1, inc0 = run(1, got, cot_node, cot_edge, c)
     node1, hang1 = post(idx, local1, exchange(back1))
     hang_in0 = exchange(hang1)
     mine1, hang_in0 = lax.optimization_barrier((paired(keep1, send1), hang_in0))
     came1 = exchange(mine1)
     local0, edge0, keep0, send0 = run(
-        "B", 0, inc0, hang_in0, node1[None], edge1[None], 0, kept0, [bias1]
+        0, inc0, node1[None], edge1[None], 0, [hang_in0], [bias1]
     )
     up = [(0, 1)]
     down = [(1, 0)]

time: 202 us -> 197 us (0.975)
  Pallas kernels: 57.1 us -> 48.5 us
  waiting for transfers between devices: 72 us -> 79.3 us
  starting transfers between devices: 44.2 us -> 39.2 us
    pallas_call x4 -> x3, Pallas kernels: 45.8 us -> 37.2 us  [the longest x2 33.7 us: run(): pl.pallas_call(functools.partial(unit_kernel, layer), out_shape=outs, in_...]
    all_to_all x5, waiting for transfers between devices: 68.3 us -> 76.1 us  [exchange(): return lax.all_to_all(x, 'dom', split_axis=0, concat_axis=0, tiled=True)]
    all_to_all x5, starting transfers between devices: 36.5 us -> 31.3 us  [exchange(): return lax.all_to_all(x, 'dom', split_axis=0, concat_axis=0, tiled=True)]
    unnamed x24 -> x22, local copies, waits for them, and re-layouts: 4.98 us -> 5.84 us
  transfers between devices with their start and end apart: 18 -> 18, of which waited for: 8 -> 7; matrix products, arithmetic and copies ran while one was open for 10% -> 10% of each run, Pallas kernels for 11% -> 7%
where the time goes in v3:
time: 197 us; the launch traced here: 194 us
  waiting for transfers between devices  79.3 us (40%)
  Pallas kernels  48.5 us (25%)
  starting transfers between devices  39.2 us (20%)
  local copies, waits for them, and re-layouts  12.5 us (6%)
  other arithmetic  12.5 us (6%)
  between operations  2.17 us (1%)
    all_to_all x5, waiting for transfers between devices, exchange(): return lax.all_to_all(x, 'dom', split_axis=0, concat_axis=0, tiled=True)  76.1 us
    pallas_call x2, Pallas kernels, run(): pl.pallas_call(functools.partial(unit_kernel, layer), out_shape=outs, in_...  33.7 us
    all_to_all x5, starting transfers between devices, exchange(): return lax.all_to_all(x, 'dom', split_axis=0, concat_axis=0, tiled=True)  31.3 us
    convert_element_type x2, other arithmetic, paired(): return (keep.astype(F32) + swap(send).astype(F32)).astype(BF)  8.51 us
    unnamed x22, local copies, waits for them, and re-layouts  5.84 us
  transfers between devices with their start and end apart: 18, of which 7 were waited for; matrix products, arithmetic and copies ran while one was open for 10% of the time, Pallas kernels for 7%

profile of v3, /device:TPU:0, one launch (start us, length us, event | category | flops | bytes accessed | tf_op | source)
XLA Modules:
  0.0 194.1 jit_solution(10674294269150106209)
XLA Ops:
  0.6 0.1 collective-permute-start
  0.7 0.7 slice_bitcast_fusion.2
  1.4 0.8 slice_bitcast_fusion
  2.2 0.6 stack.57.idx.refs_1_
  2.8 0.0 collective-permute-done.rec_all.refs_11_.refs_12_
  2.8 0.5 collective-permute-start.1
  3.3 0.1 collective-permute-start.2
  3.4 0.4 collective-permute-start.3
  3.8 0.1 collective-permute-start.4
  3.9 0.4 collective-permute-start.5
  4.3 3.5 %pre.1 = (bf16[64,8,384]{2,1,0:T(8,128)(2,1)}, f32[16,512]{1,0:T(8,128)}) custom-call(s32[1]{0:T(128)} %bitcast.core, s32[8,64]{1,0:T(8,128)} %stack.57.idx.refs_1_, f32[1,4,512]{2,1,0:T(4,128)} %eb.1, f32[1,512]{1,0:T(1,128)} %eg.1, f32[1,4,512]{2,1,0:T(4,128)} %nb.1, f32[1,512]{1,0:T(1,128)} %ng.1, bf16[1,2,192,512]{3,2,1,0:T(8,128)(2,1)} %refs_5_.3, ...), custom_call_target="tpu_custom_call" | custom-call | tf_op jit(solution)/shard_map/pre/pallas_call | solution.py:497
  7.8 11.5 %all-to-all-start = ((bf16[64,8,384]{2,1,0:T(8,128)(2,1)}), bf16[64,8,384]{2,1,0:T(8,128)(2,1)S(1)}, u32[]{:S(2)}, u32[]{:S(2)}) async-start(bf16[64,8,384]{2,1,0:T(8,128)(2,1)} %get-tuple-element.59), calls=%async_computation | async-start | bytes 786432 | tf_op jit(solution)/shard_map/all_to_all | solution.py:477
  20.7 0.6 stack.66.refs_0_
  21.3 0.0 collective-permute-done.3.refs_14_.refs_15_
  21.3 0.0 collective-permute-start.6
  21.3 0.0 collective-permute-done.5.refs_16_.refs_17_
  21.3 0.0 collective-permute-done.1.refs_12_.refs_13_
  21.3 0.0 copy-start.2
  21.3 0.0 collective-permute-done.2.refs_13_.refs_14_
  21.4 0.7 fusion.4
  22.1 0.7 stack.62
  22.8 0.7 stack.63.refs_2_
  23.5 0.0 collective-permute-done.6.refs_17_.refs_18_
  23.5 8.2 %all-to-all-done.refs_3_ = bf16[64,8,384]{2,1,0:T(8,128)(2,1)S(1)} async-done(((bf16[64,8,384]{2,1,0:T(8,128)(2,1)}), bf16[64,8,384]{2,1,0:T(8,128)(2,1)S(1)}, u32[]{:S(2)}, u32[]{:S(2)}) %all-to-all-start) | async-done | bytes 393248 | tf_op jit(solution)/shard_map/all_to_all | solution.py:477
  31.7 0.8 copy-done.6
  32.5 16.9 %shard_map.258 = (f32[192,512]{1,0:T(8,128)}, bf16[768,512]{1,0:T(8,128)(2,1)}, bf16[64,72,256]{2,1,0:T(8,128)(2,1)}, bf16[64,72,256]{2,1,0:T(8,128)(2,1)}, bf16...) custom-call(s32[5]{0:T(128)} %stack.66.refs_0_, s32[8,64]{1,0:T(8,128)} %stack.57.idx.refs_1_, ...), custom_call_target="tpu_custom_call" | custom-call | tf_op jit(solution)/shard_map/pallas_call | solution.py:570
  49.4 0.1 collective-permute-start.7
  49.5 4.7 %all-to-all-start.1 = ((bf16[64,8,128]{2,1,0:T(8,128)(2,1)}), bf16[64,8,128]{2,1,0:T(8,128)(2,1)S(1)}, u32[]{:S(2)}, u32[]{:S(2)}) async-start(bf16[64,8,128]{2,1,0:T(8,128)(2,1)} %get-tuple-element.70), calls=%async_computation.1 | async-start | bytes 262144 | tf_op jit(solution)/shard_map/all_to_all | solution.py:477
  54.3 0.6 stack.60.refs_0_
  54.9 9.4 %all-to-all-done.1.came = bf16[64,8,128]{2,1,0:T(8,128)(2,1)S(1)} async-done(((bf16[64,8,128]{2,1,0:T(8,128)(2,1)}), bf16[64,8,128]{2,1,0:T(8,128)(2,1)S(1)}, u32[]{:S(2)}, u32[]{:S(2)}) %all-to-all-start.1) | async-done | bytes 131104 | tf_op jit(solution)/shard_map/all_to_all | solution.py:477
  64.3 0.7 copy-done.8
  65.0 2.8 %post.1 = (bf16[192,512]{1,0:T(8,128)(2,1)}, bf16[64,8,128]{2,1,0:T(8,128)(2,1)}) custom-call(s32[8,64]{1,0:T(8,128)} %stack.57.idx.refs_1_, f32[192,512]{1,0:T(8,128)} %get-tuple-element.69.local, bf16[64,8,128]{2,1,0:T(8,128)(2,1)} %copy-done.8), custom_call_target="tpu_custom_call" | custom-call | tf_op jit(solution)/shard_map/post/pallas_call | solution.py:592
  67.7 5.1 %all-to-all-start.2 = ((bf16[64,8,128]{2,1,0:T(8,128)(2,1)}), bf16[64,8,128]{2,1,0:T(8,128)(2,1)S(1)}, u32[]{:S(2)}, u32[]{:S(2)}) async-start(bf16[64,8,128]{2,1,0:T(8,128)(2,1)} %get-tuple-element.71), calls=%async_computation.2 | async-start | bytes 262144 | tf_op jit(solution)/shard_map/all_to_all | solution.py:477
  72.9 3.7 %add_convert_fusion.1 = bf16[64,72,256]{2,1,0:T(8,128)(2,1)} fusion(bf16[64,72,256]{2,1,0:T(8,128)(2,1)S(1)} %collective-permute-done.7, bf16[64,72,256]{2,1,0:T(8,128)(2,1)} %get-tuple-element.67), kind=kLoop, calls=%fused_computation.1 | loop fusion | flops 4718592 | bytes 7077888 | tf_op jit(solution)/shard_map/convert_element_type | solution.py:589
  76.6 6.0 %all-to-all-done.2.refs_4_ = bf16[64,8,128]{2,1,0:T(8,128)(2,1)S(1)} async-done(((bf16[64,8,128]{2,1,0:T(8,128)(2,1)}), bf16[64,8,128]{2,1,0:T(8,128)(2,1)S(1)}, u32[]{:S(2)}, u32[]{:S(2)}) %all-to-all-start.2) | async-done | bytes 131104 | tf_op jit(solution)/shard_map/all_to_all | solution.py:477
  82.6 0.7 copy-done.7
  83.2 16.7 %shard_map.259 = (f32[192,512]{1,0:T(8,128)}, bf16[768,512]{1,0:T(8,128)(2,1)}, bf16[64,80,256]{2,1,0:T(8,128)(2,1)}, bf16[64,80,256]{2,1,0:T(8,128)(2,1)}) custom-call(s32[5]{0:T(128)} %stack.60.refs_0_, s32[8,64]{1,0:T(8,128)} %stack.57.idx.refs_1_, s32[8,768]{1,0:T(8,128)} %stack.63.refs_2_, bf16[128,512]{1,0:T(8,128)(2,1)} %get-tuple-element.66.refs_3_, ...), custom_call_target="tpu_custom_call" | custom-call | tf_op jit(solution)/shard_map/pallas_call | solution.py:570
  100.0 0.1 collective-permute-start.8
  100.1 5.2 %all-to-all-start.4 = ((bf16[64,72,256]{2,1,0:T(8,128)(2,1)}), bf16[64,72,256]{2,1,0:T(8,128)(2,1)S(1)}, u32[]{:S(2)}, u32[]{:S(2)}) async-start(bf16[64,72,256]{2,1,0:T(8,128)(2,1)} %add_convert_fusion.1), calls=%async_computation.4 | async-start | bytes 4718592 | tf_op jit(solution)/shard_map/all_to_all | solution.py:477
  105.3 0.0 collective-permute-done.8
  105.3 4.8 %add_convert_fusion = bf16[64,80,256]{2,1,0:T(8,128)(2,1)} fusion(bf16[64,80,256]{2,1,0:T(8,128)(2,1)} %collective-permute-done.8, bf16[64,80,256]{2,1,0:T(8,128)(2,1)} %get-tuple-element.77), kind=kLoop, calls=%fused_computation | loop fusion | flops 5242880 | bytes 7864320 | tf_op jit(solution)/shard_map/convert_element_type | solution.py:589
  110.1 29.4 %all-to-all-done.4.came = bf16[64,72,256]{2,1,0:T(8,128)(2,1)S(1)} async-done(((bf16[64,72,256]{2,1,0:T(8,128)(2,1)}), bf16[64,72,256]{2,1,0:T(8,128)(2,1)S(1)}, u32[]{:S(2)}, u32[]{:S(2)}) %all-to-all-start.4) | async-done | bytes 2359328 | tf_op jit(solution)/shard_map/all_to_all | solution.py:477
  139.5 1.4 copy-done.1
  140.9 4.7 %all-to-all-start.3 = ((bf16[64,80,256]{2,1,0:T(8,128)(2,1)}), bf16[64,80,256]{2,1,0:T(8,128)(2,1)S(1)}, u32[]{:S(2)}, u32[]{:S(2)}) async-start(bf16[64,80,256]{2,1,0:T(8,128)(2,1)} %add_convert_fusion), calls=%async_computation.3 | async-start | bytes 5242880 | tf_op jit(solution)/shard_map/all_to_all | solution.py:477
  145.6 1.4 collective-permute-start.12
  147.1 1.3 collective-permute-start.11
  148.4 0.5 collective-permute-done.12
  148.9 2.5 %collective-permute-done.11 = bf16[768,512]{1,0:T(8,128)(2,1)S(1)} collective-permute-done((bf16[768,512]{1,0:T(8,128)(2,1)}, bf16[768,512]{1,0:T(8,128)(2,1)S(1)}, u32[]{:S(2)}, u32[]{:S(2)}) %collective-permute-start.11) | collective-permute-done | bytes 786464 | tf_op jit(solution)/shard_map/ppermute | solution.py:618
  151.5 2.5 %maximum_select_fusion = bf16[1,2,768,512]{3,2,1,0:T(8,128)(2,1)} fusion(bf16[1,1,768,512]{3,2,1,0:T(8,128)(2,1)S(1)} %bitcast.35, bf16[1,1,768,512]{3,2,1,0:T(8,128)(2,1)} %bitcast.33, bf16[1,1,768,512]{3,2,1,0:T(8,128)(2,1)S(1)} %bitcast.31, bf16[1,1,768,512]{3,2,1,0:T(8,128)(2,1)S(1)} %bitcast.34, pred[]{:T(512)S(6)} %eq.9), kind=kLoop, calls=%fused_computation.2 | loop fusion | flops 2359296 | bytes 4718593 | tf_op jit(solution)/shard_map/jit(_where)/select_n | solution.py:620
  154.0 2.8 %sums1.1 = (f32[80,256]{1,0:T(8,128)}, bf16[272,512]{1,0:T(8,128)(2,1)}) custom-call(bf16[64,72,256]{2,1,0:T(8,128)(2,1)} %copy-done.1, bf16[192,512]{1,0:T(8,128)(2,1)} %get-tuple-element.73.node), custom_call_target="tpu_custom_call" | custom-call | tf_op jit(solution)/shard_map/sums1/pallas_call | solution.py:604
  156.8 2.0 %collective-permute-start.10 = (bf16[272,512]{1,0:T(8,128)(2,1)}, bf16[272,512]{1,0:T(8,128)(2,1)S(1)}, u32[]{:S(2)}, u32[]{:S(2)}) collective-permute-start(bf16[272,512]{1,0:T(8,128)(2,1)} %get-tuple-element.83.s1), channel_id=1, source_target_pairs={{0,64},{1,65},{2,66},{3,67},{4,68},{5,69},{6,70},{7,71},{8,72},{9,... | collective-permute-start | bytes 835592 | tf_op jit(solution)/shard_map/ppermute | solution.py:622
  158.9 23.2 %all-to-all-done.3.came = bf16[64,80,256]{2,1,0:T(8,128)(2,1)S(1)} async-done(((bf16[64,80,256]{2,1,0:T(8,128)(2,1)}), bf16[64,80,256]{2,1,0:T(8,128)(2,1)S(1)}, u32[]{:S(2)}, u32[]{:S(2)}) %all-to-all-start.3) | async-done | bytes 2621472 | tf_op jit(solution)/shard_map/all_to_all | solution.py:477
  182.1 1.5 copy-done
  183.5 3.6 %sums0.1 = (f32[80,256]{1,0:T(8,128)}, bf16[272,512]{1,0:T(8,128)(2,1)}) custom-call(s32[8,64]{1,0:T(8,128)} %stack.57.idx.refs_1_, f32[192,512]{1,0:T(8,128)} %get-tuple-element.76.local, bf16[64,80,256]{2,1,0:T(8,128)(2,1)} %copy-done), custom_call_target="tpu_custom_call" | custom-call | tf_op jit(solution)/shard_map/sums0/pallas_call | solution.py:611
  187.2 1.3 collective-permute-start.9
  188.5 0.7 broadcast_select_fusion
  189.2 0.1 slice_reduce_fusion
  189.2 0.7 broadcast_in_dim.13
  189.9 0.7 slice.53
  190.6 0.6 fusion.9
  191.2 0.0 collective-permute-done.9.r0
  191.2 0.7 copy-done.9
  191.9 0.1 copy-done.10
  192.0 2.1 %end.1 = (bf16[1,2,192,512]{3,2,1,0:T(8,128)(2,1)}, f32[1,24,512]{2,1,0:T(8,128)}, f32[1,2,8,512]{3,2,1,0:T(8,128)}, f32[1,16,512]{2,1,0:T(8,128)}, f32[1,2,8,512]{3,2,1,0:T(8,128)}) custom-call(s32[1]{0:T(128)} %bitcast.core, f32[80,256]{1,0:T(8,128)} %get-tuple-element.79.p0, f32[80,256]{1,0:T(8,128)} %get-tuple-element.81.p1, ...), custom_call_target="tpu_custom_call" | custom-call | tf_op jit(solution)/shard_map/end/pallas_call | solution.py:623
  (18 shorter events, 0.0 us)
Async XLA Ops:
  0.6 2.2 %collective-permute-start = (bf16[1,2,192,512]{3,2,1,0:T(8,128)(2,1)}, bf16[1,2,192,512]{3,2,1,0:T(8,128)(2,1)S(1)}, u32[]{:S(2)}, u32[]{:S(2)}) collective-permute-start(bf16[1,2,192,512]{3,2,1,0:T(8,128)(2,1)} %refs_5_.3), channel_id=1, source_target_pairs={{0,64},{64,0},{1,65},{65,1},{2,66},{66,2},{3,67},{67,3},{4,68},{68... | collective-permute-start | bytes 1179656 | tf_op jit(solution)/shard_map/ppermute | solution.py:473
  2.8 1.5 copy-start.4
  2.8 18.5 %collective-permute-start.1 = (bf16[1,2,768,512]{3,2,1,0:T(8,128)(2,1)}, bf16[1,2,768,512]{3,2,1,0:T(8,128)(2,1)S(1)}, u32[]{:S(2)}, u32[]{:S(2)}) collective-permute-start(bf16[1,2,768,512]{3,2,1,0:T(8,128)(2,1)} %refs_6_.3), channel_id=1, source_target_pairs={{0,64},{64,0},{1,65},{65,1},{2,66},{66,2},{3,67},{67,3},{4,68},{68... | collective-permute-start | bytes 4718600 | tf_op jit(solution)/shard_map/ppermute | solution.py:473
  3.3 18.0 %collective-permute-start.2 = (bf16[1536,512]{1,0:T(8,128)(2,1)}, bf16[1536,512]{1,0:T(8,128)(2,1)S(1)}, u32[]{:S(2)}, u32[]{:S(2)}) collective-permute-start(bf16[1536,512]{1,0:T(8,128)(2,1)} %bitcast.26), channel_id=1, source_target_pairs={{0,64},{64,0},{1,65},{65,1},{2,66},{66,2},{3,67},{67,3},{4,68},{68... | collective-permute-start | bytes 4718600 | tf_op jit(solution)/shard_map/ppermute | solution.py:473
  3.4 17.9 %collective-permute-start.3 = (bf16[2,512,512]{2,1,0:T(8,128)(2,1)}, bf16[2,512,512]{2,1,0:T(8,128)(2,1)}, u32[]{:S(2)}, u32[]{:S(2)}) collective-permute-start(bf16[2,512,512]{2,1,0:T(8,128)(2,1)} %bitcast.27), channel_id=1, source_target_pairs={{0,64},{64,0},{1,65},{65,1},{2,66},{66,2},{3,67},{67,3},{4,68},{68... | collective-permute-start | bytes 3145736 | tf_op jit(solution)/shard_map/ppermute | solution.py:473
  3.8 17.5 %collective-permute-start.4 = (bf16[1024,512]{1,0:T(8,128)(2,1)}, bf16[1024,512]{1,0:T(8,128)(2,1)}, u32[]{:S(2)}, u32[]{:S(2)}) collective-permute-start(bf16[1024,512]{1,0:T(8,128)(2,1)} %bitcast.28), channel_id=1, source_target_pairs={{0,64},{64,0},{1,65},{65,1},{2,66},{66,2},{3,67},{67,3},{4,68},{68... | collective-permute-start | bytes 3145736 | tf_op jit(solution)/shard_map/ppermute | solution.py:473
  3.9 17.4 %collective-permute-start.5 = (bf16[2,512,512]{2,1,0:T(8,128)(2,1)}, bf16[2,512,512]{2,1,0:T(8,128)(2,1)}, u32[]{:S(2)}, u32[]{:S(2)}) collective-permute-start(bf16[2,512,512]{2,1,0:T(8,128)(2,1)} %bitcast.29), channel_id=1, source_target_pairs={{0,64},{64,0},{1,65},{65,1},{2,66},{66,2},{3,67},{67,3},{4,68},{68... | collective-permute-start | bytes 3145736 | tf_op jit(solution)/shard_map/ppermute | solution.py:473
  7.8 23.8 %all-to-all-start = ((bf16[64,8,384]{2,1,0:T(8,128)(2,1)}), bf16[64,8,384]{2,1,0:T(8,128)(2,1)S(1)}, u32[]{:S(2)}, u32[]{:S(2)}) async-start(bf16[64,8,384]{2,1,0:T(8,128)(2,1)} %get-tuple-element.59), calls=%async_computation | async-start | bytes 786432 | tf_op jit(solution)/shard_map/all_to_all | solution.py:477
  21.3 2.2 %collective-permute-start.6 = (f32[16,512]{1,0:T(8,128)}, f32[16,512]{1,0:T(8,128)}, u32[]{:S(2)}, u32[]{:S(2)}) collective-permute-start(f32[16,512]{1,0:T(8,128)} %get-tuple-element.60.refs_10_.refs_11_), channel_id=1, source_target_pairs={{0,64},{64,0},{1,65},{65,1},{2,66},{66,2},{3,67},{67,3},{4,68},{68... | collective-permute-start | bytes 98312 | tf_op jit(solution)/shard_map/ppermute | solution.py:473
  21.3 10.4 %copy-start.2 = (bf16[1,2,768,512]{3,2,1,0:T(8,128)(2,1)}, bf16[1,2,768,512]{3,2,1,0:T(8,128)(2,1)S(1)}, u32[]{:S(2)}) copy-start(bf16[1,2,768,512]{3,2,1,0:T(8,128)(2,1)S(1)} %collective-permute-done.1.refs_12_.refs_13_) | copy-start | bytes 4718596
  21.3 10.4 %copy-start.3 = (bf16[1536,512]{1,0:T(8,128)(2,1)}, bf16[1536,512]{1,0:T(8,128)(2,1)S(1)}, u32[]{:S(2)}) copy-start(bf16[1536,512]{1,0:T(8,128)(2,1)S(1)} %collective-permute-done.2.refs_13_.refs_14_) | copy-start | bytes 4718596
  31.7 0.8 copy-start.6
  49.4 23.4 %collective-permute-start.7 = (bf16[64,72,256]{2,1,0:T(8,128)(2,1)}, bf16[64,72,256]{2,1,0:T(8,128)(2,1)S(1)}, u32[]{:S(2)}, u32[]{:S(2)}) collective-permute-start(bf16[64,72,256]{2,1,0:T(8,128)(2,1)} %get-tuple-element.68), channel_id=1, source_target_pairs={{0,64},{64,0},{1,65},{65,1},{2,66},{66,2},{3,67},{67,3},{4,68},{68... | collective-permute-start | bytes 7077896 | tf_op jit(solution)/shard_map/ppermute | solution.py:473
  49.5 14.8 %all-to-all-start.1 = ((bf16[64,8,128]{2,1,0:T(8,128)(2,1)}), bf16[64,8,128]{2,1,0:T(8,128)(2,1)S(1)}, u32[]{:S(2)}, u32[]{:S(2)}) async-start(bf16[64,8,128]{2,1,0:T(8,128)(2,1)} %get-tuple-element.70), calls=%async_computation.1 | async-start | bytes 262144 | tf_op jit(solution)/shard_map/all_to_all | solution.py:477
  64.3 0.7 copy-start.8
  67.7 14.9 %all-to-all-start.2 = ((bf16[64,8,128]{2,1,0:T(8,128)(2,1)}), bf16[64,8,128]{2,1,0:T(8,128)(2,1)S(1)}, u32[]{:S(2)}, u32[]{:S(2)}) async-start(bf16[64,8,128]{2,1,0:T(8,128)(2,1)} %get-tuple-element.71), calls=%async_computation.2 | async-start | bytes 262144 | tf_op jit(solution)/shard_map/all_to_all | solution.py:477
  82.6 0.7 copy-start.7
  100.0 5.3 %collective-permute-start.8 = (bf16[64,80,256]{2,1,0:T(8,128)(2,1)}, bf16[64,80,256]{2,1,0:T(8,128)(2,1)}, u32[]{:S(2)}, u32[]{:S(2)}) collective-permute-start(bf16[64,80,256]{2,1,0:T(8,128)(2,1)} %get-tuple-element.78), channel_id=1, source_target_pairs={{0,64},{64,0},{1,65},{65,1},{2,66},{66,2},{3,67},{67,3},{4,68},{68... | collective-permute-start | bytes 7864328 | tf_op jit(solution)/shard_map/ppermute | solution.py:473
  100.1 39.4 %all-to-all-start.4 = ((bf16[64,72,256]{2,1,0:T(8,128)(2,1)}), bf16[64,72,256]{2,1,0:T(8,128)(2,1)S(1)}, u32[]{:S(2)}, u32[]{:S(2)}) async-start(bf16[64,72,256]{2,1,0:T(8,128)(2,1)} %add_convert_fusion.1), calls=%async_computation.4 | async-start | bytes 4718592 | tf_op jit(solution)/shard_map/all_to_all | solution.py:477
  110.1 35.5 %copy-start.5 = (bf16[768,512]{1,0:T(8,128)(2,1)S(1)}, bf16[768,512]{1,0:T(8,128)(2,1)}, u32[]{:S(2)}) copy-start(bf16[768,512]{1,0:T(8,128)(2,1)} %get-tuple-element.74) | copy-start | bytes 2359300
  139.5 1.4 copy-start.1
  140.9 41.2 %all-to-all-start.3 = ((bf16[64,80,256]{2,1,0:T(8,128)(2,1)}), bf16[64,80,256]{2,1,0:T(8,128)(2,1)S(1)}, u32[]{:S(2)}, u32[]{:S(2)}) async-start(bf16[64,80,256]{2,1,0:T(8,128)(2,1)} %add_convert_fusion), calls=%async_computation.3 | async-start | bytes 5242880 | tf_op jit(solution)/shard_map/all_to_all | solution.py:477
  145.6 3.3 %collective-permute-start.12 = (bf16[768,512]{1,0:T(8,128)(2,1)S(1)}, bf16[768,512]{1,0:T(8,128)(2,1)S(1)}, u32[]{:S(2)}, u32[]{:S(2)}) collective-permute-start(bf16[768,512]{1,0:T(8,128)(2,1)S(1)} %copy-done.5), channel_id=1, source_target_pairs={{0,64},{1,65},{2,66},{3,67},{4,68},{5,69},{6,70},{7,71},{8,72},{9,... | collective-permute-start | bytes 2359304 | tf_op jit(solution)/shard_map/ppermute | solution.py:619
  147.1 4.4 %collective-permute-start.11 = (bf16[768,512]{1,0:T(8,128)(2,1)}, bf16[768,512]{1,0:T(8,128)(2,1)S(1)}, u32[]{:S(2)}, u32[]{:S(2)}) collective-permute-start(bf16[768,512]{1,0:T(8,128)(2,1)} %get-tuple-element.85), channel_id=1, source_target_pairs={{64,0},{65,1},{66,2},{67,3},{68,4},{69,5},{70,6},{71,7},{72,8},{73... | collective-permute-start | bytes 2359304 | tf_op jit(solution)/shard_map/ppermute | solution.py:618
  156.8 34.3 %collective-permute-start.10 = (bf16[272,512]{1,0:T(8,128)(2,1)}, bf16[272,512]{1,0:T(8,128)(2,1)S(1)}, u32[]{:S(2)}, u32[]{:S(2)}) collective-permute-start(bf16[272,512]{1,0:T(8,128)(2,1)} %get-tuple-element.83.s1), channel_id=1, source_target_pairs={{0,64},{1,65},{2,66},{3,67},{4,68},{5,69},{6,70},{7,71},{8,72},{9,... | collective-permute-start | bytes 835592 | tf_op jit(solution)/shard_map/ppermute | solution.py:622
  182.1 1.5 copy-start
  187.2 4.0 %collective-permute-start.9 = (bf16[272,512]{1,0:T(8,128)(2,1)}, bf16[272,512]{1,0:T(8,128)(2,1)S(1)}, u32[]{:S(2)}, u32[]{:S(2)}) collective-permute-start(bf16[272,512]{1,0:T(8,128)(2,1)} %get-tuple-element.82.s0), channel_id=1, source_target_pairs={{64,0},{65,1},{66,2},{67,3},{68,4},{69,5},{70,6},{71,7},{72,8},{73... | collective-permute-start | bytes 835592 | tf_op jit(solution)/shard_map/ppermute | solution.py:621
  191.2 0.7 copy-start.9
  191.2 0.8 copy-start.10

commit v4 on v3

--- a/solution.py
+++ b/solution.py
@@ -192,13 +192,18 @@
     split_part(part, ship, rows)
 
 
-def end_kernel(core, p0, p1, s0, s1, r0, r1, node_out, we, wem, wn, wnm):
+def end_kernel(core, p0, p1, s0, s1, r0, r1, node_out, we, wem, eb, eg, wn, wnm, nb, ng):
     def part_of(ship):
         rows = node_out.shape[2]
         half = p0.shape[1]
         return ship[rows:, :half].astype(F32) + ship[rows:, half:].astype(F32)
 
-    def write(left, right, first, second):
+    def write(left, right, first, second, sums):
+        for v in range(4):
+            eb[0, v : v + 1, :] = sums[:, v * 8 : v * 8 + 8]
+            nb[0, v : v + 1, :] = sums[:, v * 8 + 40 : v * 8 + 48]
+        eg[...] = sums[:, 32:40]
+        ng[...] = sums[:, 72:80]
         full = jnp.concatenate([left, right], axis=1)
         rows = node_out.shape[2]
         node_out[0, 0] = first[0:rows, :]
@@ -212,11 +217,11 @@
 
     @pl.when(core[0] == 0)
     def _():
-        write(p0[...], part_of(r0), s0, r0)
+        write(p0[...], part_of(r0), s0, r0, p0[76:77, 0:128])
 
     @pl.when(core[0] == 1)
     def _():
-        write(part_of(r1), p1[...], r1, s1)
+        write(part_of(r1), p1[...], r1, s1, p0[76:77, 128:256])
 
 
 SAVED = 7
@@ -620,32 +625,24 @@
     edge_final = jnp.where(first, jnp.stack([edge0, lower]), jnp.stack([upper, edge1]))[None]
     r0 = lax.ppermute(ship0, "pipe", down)
     r1 = lax.ppermute(ship1, "pipe", up)
-    node_final, we, wem, wn, wnm = pl.pallas_call(
+    ends = pl.pallas_call(
         end_kernel,
         out_shape=[
             shape((1, 2, n_rows, width), BF),
             shape((1, 24, width), F32),
             shape((1, 2, 8, width), F32),
+            shape((1, 4, 8), F32),
+            shape((1, 8), F32),
             shape((1, 16, width), F32),
             shape((1, 2, 8, width), F32),
+            shape((1, 4, 8), F32),
+            shape((1, 8), F32),
         ],
         in_specs=[SM] + [VM] * 6,
-        out_specs=[VM] * 5,
+        out_specs=[VM] * 9,
         name="end",
     )(c.reshape(1), part0, part1, ship0, ship1, r0, r1)
-    bias = jnp.where(first, part0[76, 0:128], part0[76, 128:256]).reshape(16, 8)
-    return (
-        node_final,
-        edge_final,
-        we,
-        wem,
-        bias[None, 0:4],
-        bias[4:5],
-        wn,
-        wnm,
-        bias[None, 5:9],
-        bias[9:10],
-    )
+    return (ends[0], edge_final, *ends[1:])
 
 
 def solution(mesh):

time: 197 us -> 198 us (level)
  starting transfers between devices: 39.2 us -> 42.6 us
  local copies, waits for them, and re-layouts: 12.5 us -> 10.4 us
    ppermute x1, starting transfers between devices: 2.04 us -> 4.63 us  [body(): r1 = lax.ppermute(ship1, 'pipe', up)]
    ppermute x1, waiting for transfers between devices: 2.54 us -> 0.01 us  [body(): lower = lax.ppermute(edge0, 'pipe', down)]
    all_to_all x5, waiting for transfers between devices: 76.1 us -> 78.4 us  [exchange(): return lax.all_to_all(x, 'dom', split_axis=0, concat_axis=0, tiled=True)]
    unnamed x22 -> x20, local copies, waits for them, and re-layouts: 5.84 us -> 5.72 us
  transfers between devices with their start and end apart: 18 -> 18, of which waited for: 7 -> 5; matrix products, arithmetic and copies ran while one was open for 10% -> 9% of each run, Pallas kernels for 7% -> 7%
where the time goes in v4:
time: 198 us; the launch traced here: 195 us
  waiting for transfers between devices  78.5 us (40%)
  Pallas kernels  48.4 us (24%)
  starting transfers between devices  42.6 us (22%)
  other arithmetic  12.3 us (6%)
  local copies, waits for them, and re-layouts  10.4 us (5%)
  between operations  2.34 us (1%)
    all_to_all x5, waiting for transfers between devices, exchange(): return lax.all_to_all(x, 'dom', split_axis=0, concat_axis=0, tiled=True)  78.4 us
    pallas_call x2, Pallas kernels, run(): pl.pallas_call(functools.partial(unit_kernel, layer), out_shape=outs, in_...  33.6 us
    all_to_all x5, starting transfers between devices, exchange(): return lax.all_to_all(x, 'dom', split_axis=0, concat_axis=0, tiled=True)  31.3 us
    convert_element_type x2, other arithmetic, paired(): return (keep.astype(F32) + swap(send).astype(F32)).astype(BF)  8.51 us
    unnamed x20, local copies, waits for them, and re-layouts  5.72 us
    ppermute x1, starting transfers between devices, body(): r1 = lax.ppermute(ship1, 'pipe', up)  4.63 us
  transfers between devices with their start and end apart: 18, of which 5 were waited for; matrix products, arithmetic and copies ran while one was open for 9% of the time, Pallas kernels for 7%

profile of v4, /device:TPU:0, one launch (start us, length us, event | category | flops | bytes accessed | tf_op | source)
XLA Modules:
  0.0 194.5 jit_solution(11441415130125155707)
XLA Ops:
  0.6 0.1 collective-permute-start
  0.7 0.7 slice_bitcast_fusion.2
  1.4 0.8 slice_bitcast_fusion
  2.2 0.6 stack.57.idx.refs_1_
  2.8 0.0 collective-permute-done.rec_all.refs_11_.refs_12_
  2.8 0.5 collective-permute-start.1
  3.3 0.1 collective-permute-start.2
  3.4 0.4 collective-permute-start.3
  3.8 0.1 collective-permute-start.4
  3.9 0.4 collective-permute-start.5
  4.3 0.0 copy-done.4
  4.3 3.5 %pre.1 = (bf16[64,8,384]{2,1,0:T(8,128)(2,1)}, f32[16,512]{1,0:T(8,128)}) custom-call(s32[1]{0:T(128)} %bitcast.core, s32[8,64]{1,0:T(8,128)} %stack.57.idx.refs_1_, f32[1,4,512]{2,1,0:T(4,128)} %eb.1, f32[1,512]{1,0:T(1,128)} %eg.1, f32[1,4,512]{2,1,0:T(4,128)} %nb.1, f32[1,512]{1,0:T(1,128)} %ng.1, bf16[1,2,192,512]{3,2,1,0:T(8,128)(2,1)} %refs_5_.3, ...), custom_call_target="tpu_custom_call" | custom-call | tf_op jit(solution)/shard_map/pre/pallas_call | solution.py:502
  7.8 11.5 %all-to-all-start = ((bf16[64,8,384]{2,1,0:T(8,128)(2,1)}), bf16[64,8,384]{2,1,0:T(8,128)(2,1)S(1)}, u32[]{:S(2)}, u32[]{:S(2)}) async-start(bf16[64,8,384]{2,1,0:T(8,128)(2,1)} %get-tuple-element.63), calls=%async_computation | async-start | bytes 786432 | tf_op jit(solution)/shard_map/all_to_all | solution.py:482
  20.7 0.6 stack.66.refs_0_
  21.3 0.0 collective-permute-done.3.refs_14_.refs_15_
  21.3 0.0 collective-permute-start.6
  21.3 0.0 collective-permute-done.4.refs_15_.refs_16_
  21.3 0.0 collective-permute-done.5.refs_16_.refs_17_
  21.3 0.0 collective-permute-done.1.refs_12_.refs_13_
  21.3 0.0 copy-start.2
  21.3 0.0 collective-permute-done.2.refs_13_.refs_14_
  21.3 0.0 copy-start.3
  21.3 0.7 fusion.4
  22.1 0.7 stack.62
  22.8 0.7 stack.63.refs_2_
  23.5 0.0 collective-permute-done.6.refs_17_.refs_18_
  23.5 8.2 %all-to-all-done.refs_3_ = bf16[64,8,384]{2,1,0:T(8,128)(2,1)S(1)} async-done(((bf16[64,8,384]{2,1,0:T(8,128)(2,1)}), bf16[64,8,384]{2,1,0:T(8,128)(2,1)S(1)}, u32[]{:S(2)}, u32[]{:S(2)}) %all-to-all-start) | async-done | bytes 393248 | tf_op jit(solution)/shard_map/all_to_all | solution.py:482
  31.7 0.0 copy-done.2
  31.7 0.8 copy-done.6
  32.5 16.9 %shard_map.258 = (f32[192,512]{1,0:T(8,128)}, bf16[768,512]{1,0:T(8,128)(2,1)}, bf16[64,72,256]{2,1,0:T(8,128)(2,1)}, bf16[64,72,256]{2,1,0:T(8,128)(2,1)}, bf16...) custom-call(s32[5]{0:T(128)} %stack.66.refs_0_, s32[8,64]{1,0:T(8,128)} %stack.57.idx.refs_1_, ...), custom_call_target="tpu_custom_call" | custom-call | tf_op jit(solution)/shard_map/pallas_call | solution.py:575
  49.4 0.1 collective-permute-start.7
  49.5 4.7 %all-to-all-start.1 = ((bf16[64,8,128]{2,1,0:T(8,128)(2,1)}), bf16[64,8,128]{2,1,0:T(8,128)(2,1)S(1)}, u32[]{:S(2)}, u32[]{:S(2)}) async-start(bf16[64,8,128]{2,1,0:T(8,128)(2,1)} %get-tuple-element.74), calls=%async_computation.1 | async-start | bytes 262144 | tf_op jit(solution)/shard_map/all_to_all | solution.py:482
  54.2 0.6 stack.60.refs_0_
  54.8 9.4 %all-to-all-done.1.came = bf16[64,8,128]{2,1,0:T(8,128)(2,1)S(1)} async-done(((bf16[64,8,128]{2,1,0:T(8,128)(2,1)}), bf16[64,8,128]{2,1,0:T(8,128)(2,1)S(1)}, u32[]{:S(2)}, u32[]{:S(2)}) %all-to-all-start.1) | async-done | bytes 131104 | tf_op jit(solution)/shard_map/all_to_all | solution.py:482
  64.2 0.7 copy-done.8
  64.9 2.8 %post.1 = (bf16[192,512]{1,0:T(8,128)(2,1)}, bf16[64,8,128]{2,1,0:T(8,128)(2,1)}) custom-call(s32[8,64]{1,0:T(8,128)} %stack.57.idx.refs_1_, f32[192,512]{1,0:T(8,128)} %get-tuple-element.73.local, bf16[64,8,128]{2,1,0:T(8,128)(2,1)} %copy-done.8), custom_call_target="tpu_custom_call" | custom-call | tf_op jit(solution)/shard_map/post/pallas_call | solution.py:597
  67.6 5.1 %all-to-all-start.2 = ((bf16[64,8,128]{2,1,0:T(8,128)(2,1)}), bf16[64,8,128]{2,1,0:T(8,128)(2,1)S(1)}, u32[]{:S(2)}, u32[]{:S(2)}) async-start(bf16[64,8,128]{2,1,0:T(8,128)(2,1)} %get-tuple-element.75), calls=%async_computation.2 | async-start | bytes 262144 | tf_op jit(solution)/shard_map/all_to_all | solution.py:482
  72.8 0.0 collective-permute-done.7
  72.8 3.7 %add_convert_fusion.1 = bf16[64,72,256]{2,1,0:T(8,128)(2,1)} fusion(bf16[64,72,256]{2,1,0:T(8,128)(2,1)S(1)} %collective-permute-done.7, bf16[64,72,256]{2,1,0:T(8,128)(2,1)} %get-tuple-element.71), kind=kLoop, calls=%fused_computation.1 | loop fusion | flops 4718592 | bytes 7077888 | tf_op jit(solution)/shard_map/convert_element_type | solution.py:594
  76.6 6.0 %all-to-all-done.2.refs_4_ = bf16[64,8,128]{2,1,0:T(8,128)(2,1)S(1)} async-done(((bf16[64,8,128]{2,1,0:T(8,128)(2,1)}), bf16[64,8,128]{2,1,0:T(8,128)(2,1)S(1)}, u32[]{:S(2)}, u32[]{:S(2)}) %all-to-all-start.2) | async-done | bytes 131104 | tf_op jit(solution)/shard_map/all_to_all | solution.py:482
  82.5 0.6 copy-done.7
  83.2 16.7 %shard_map.259 = (f32[192,512]{1,0:T(8,128)}, bf16[768,512]{1,0:T(8,128)(2,1)}, bf16[64,80,256]{2,1,0:T(8,128)(2,1)}, bf16[64,80,256]{2,1,0:T(8,128)(2,1)}) custom-call(s32[5]{0:T(128)} %stack.60.refs_0_, s32[8,64]{1,0:T(8,128)} %stack.57.idx.refs_1_, s32[8,768]{1,0:T(8,128)} %stack.63.refs_2_, bf16[128,512]{1,0:T(8,128)(2,1)} %get-tuple-element.70.refs_3_, ...), custom_call_target="tpu_custom_call" | custom-call | tf_op jit(solution)/shard_map/pallas_call | solution.py:575
  99.9 0.1 collective-permute-start.8
  100.0 5.2 %all-to-all-start.4 = ((bf16[64,72,256]{2,1,0:T(8,128)(2,1)}), bf16[64,72,256]{2,1,0:T(8,128)(2,1)S(1)}, u32[]{:S(2)}, u32[]{:S(2)}) async-start(bf16[64,72,256]{2,1,0:T(8,128)(2,1)} %add_convert_fusion.1), calls=%async_computation.4 | async-start | bytes 4718592 | tf_op jit(solution)/shard_map/all_to_all | solution.py:482
  105.2 0.0 collective-permute-done.8
  105.2 4.8 %add_convert_fusion = bf16[64,80,256]{2,1,0:T(8,128)(2,1)} fusion(bf16[64,80,256]{2,1,0:T(8,128)(2,1)} %collective-permute-done.8, bf16[64,80,256]{2,1,0:T(8,128)(2,1)} %get-tuple-element.81), kind=kLoop, calls=%fused_computation | loop fusion | flops 5242880 | bytes 7864320 | tf_op jit(solution)/shard_map/convert_element_type | solution.py:594
  110.0 29.4 %all-to-all-done.4.came = bf16[64,72,256]{2,1,0:T(8,128)(2,1)S(1)} async-done(((bf16[64,72,256]{2,1,0:T(8,128)(2,1)}), bf16[64,72,256]{2,1,0:T(8,128)(2,1)S(1)}, u32[]{:S(2)}, u32[]{:S(2)}) %all-to-all-start.4) | async-done | bytes 2359328 | tf_op jit(solution)/shard_map/all_to_all | solution.py:482
  139.4 1.4 copy-done.1
  140.8 4.7 %all-to-all-start.3 = ((bf16[64,80,256]{2,1,0:T(8,128)(2,1)}), bf16[64,80,256]{2,1,0:T(8,128)(2,1)S(1)}, u32[]{:S(2)}, u32[]{:S(2)}) async-start(bf16[64,80,256]{2,1,0:T(8,128)(2,1)} %add_convert_fusion), calls=%async_computation.3 | async-start | bytes 5242880 | tf_op jit(solution)/shard_map/all_to_all | solution.py:482
  145.5 2.3 %collective-permute-start.12 = (bf16[768,512]{1,0:T(8,128)(2,1)S(1)}, bf16[768,512]{1,0:T(8,128)(2,1)}, u32[]{:S(2)}, u32[]{:S(2)}) collective-permute-start(bf16[768,512]{1,0:T(8,128)(2,1)S(1)} %copy-done.5), channel_id=1, source_target_pairs={{0,64},{1,65},{2,66},{3,67},{4,68},{5,69},{6,70},{7,71},{8,72},{9,... | collective-permute-start | bytes 2359304 | tf_op jit(solution)/shard_map/ppermute | solution.py:624
  147.8 1.3 collective-permute-start.11
  149.1 2.8 %sums1.1 = (f32[80,256]{1,0:T(8,128)}, bf16[272,512]{1,0:T(8,128)(2,1)}) custom-call(bf16[64,72,256]{2,1,0:T(8,128)(2,1)} %copy-done.1, bf16[192,512]{1,0:T(8,128)(2,1)} %get-tuple-element.77.node), custom_call_target="tpu_custom_call" | custom-call | tf_op jit(solution)/shard_map/sums1/pallas_call | solution.py:609
  151.9 4.6 %collective-permute-start.10 = (bf16[272,512]{1,0:T(8,128)(2,1)}, bf16[272,512]{1,0:T(8,128)(2,1)}, u32[]{:S(2)}, u32[]{:S(2)}) collective-permute-start(bf16[272,512]{1,0:T(8,128)(2,1)} %get-tuple-element.87.s1), channel_id=1, source_target_pairs={{0,64},{1,65},{2,66},{3,67},{4,68},{5,69},{6,70},{7,71},{8,72},{9,... | collective-permute-start | bytes 835592 | tf_op jit(solution)/shard_map/ppermute | solution.py:627
  156.5 25.4 %all-to-all-done.3.came = bf16[64,80,256]{2,1,0:T(8,128)(2,1)S(1)} async-done(((bf16[64,80,256]{2,1,0:T(8,128)(2,1)}), bf16[64,80,256]{2,1,0:T(8,128)(2,1)S(1)}, u32[]{:S(2)}, u32[]{:S(2)}) %all-to-all-start.3) | async-done | bytes 2621472 | tf_op jit(solution)/shard_map/all_to_all | solution.py:482
  182.0 1.5 copy-done
  183.5 3.6 %sums0.1 = (f32[80,256]{1,0:T(8,128)}, bf16[272,512]{1,0:T(8,128)(2,1)}) custom-call(s32[8,64]{1,0:T(8,128)} %stack.57.idx.refs_1_, f32[192,512]{1,0:T(8,128)} %get-tuple-element.80.local, bf16[64,80,256]{2,1,0:T(8,128)(2,1)} %copy-done), custom_call_target="tpu_custom_call" | custom-call | tf_op jit(solution)/shard_map/sums0/pallas_call | solution.py:616
  187.1 1.3 collective-permute-start.9
  188.4 0.0 collective-permute-done.12
  188.4 0.0 collective-permute-done.11
  188.4 3.0 %maximum_select_fusion = bf16[1,2,768,512]{3,2,1,0:T(8,128)(2,1)} fusion(bf16[1,1,768,512]{3,2,1,0:T(8,128)(2,1)} %bitcast.18, bf16[1,1,768,512]{3,2,1,0:T(8,128)(2,1)} %bitcast.33, bf16[1,1,768,512]{3,2,1,0:T(8,128)(2,1)S(1)} %bitcast.31, bf16[1,1,768,512]{3,2,1,0:T(8,128)(2,1)} %bitcast.19, pred[]{:T(512)S(6)} %eq.9), kind=kLoop, calls=%fused_computation.2 | loop fusion | flops 2359296 | bytes 4718593 | tf_op jit(solution)/shard_map/jit(_where)/select_n | solution.py:625
  191.4 0.0 collective-permute-done.10.r1
  191.4 0.0 collective-permute-done.9.r0
  191.4 0.7 copy-done.9
  192.1 2.2 %end.1 = (bf16[1,2,192,512]{3,2,1,0:T(8,128)(2,1)}, f32[1,24,512]{2,1,0:T(8,128)}, f32[1,2,8,512]{3,2,1,0:T(8,128)}, f32[1,4,8]{2,1,0:T(4,128)}, f32[1,8]{1,0:T(...) custom-call(s32[1]{0:T(128)} %bitcast.core, ...), custom_call_target="tpu_custom_call" | custom-call | tf_op jit(solution)/shard_map/end/pallas_call | solution.py:628
  (11 shorter events, 0.0 us)
Async XLA Ops:
  0.6 2.2 %collective-permute-start = (bf16[1,2,192,512]{3,2,1,0:T(8,128)(2,1)}, bf16[1,2,192,512]{3,2,1,0:T(8,128)(2,1)S(1)}, u32[]{:S(2)}, u32[]{:S(2)}) collective-permute-start(bf16[1,2,192,512]{3,2,1,0:T(8,128)(2,1)} %refs_5_.3), channel_id=1, source_target_pairs={{0,64},{64,0},{1,65},{65,1},{2,66},{66,2},{3,67},{67,3},{4,68},{68... | collective-permute-start | bytes 1179656 | tf_op jit(solution)/shard_map/ppermute | solution.py:478
  2.8 1.5 copy-start.4
  2.8 18.5 %collective-permute-start.1 = (bf16[1,2,768,512]{3,2,1,0:T(8,128)(2,1)}, bf16[1,2,768,512]{3,2,1,0:T(8,128)(2,1)S(1)}, u32[]{:S(2)}, u32[]{:S(2)}) collective-permute-start(bf16[1,2,768,512]{3,2,1,0:T(8,128)(2,1)} %refs_6_.3), channel_id=1, source_target_pairs={{0,64},{64,0},{1,65},{65,1},{2,66},{66,2},{3,67},{67,3},{4,68},{68... | collective-permute-start | bytes 4718600 | tf_op jit(solution)/shard_map/ppermute | solution.py:478
  3.3 18.0 %collective-permute-start.2 = (bf16[1536,512]{1,0:T(8,128)(2,1)}, bf16[1536,512]{1,0:T(8,128)(2,1)S(1)}, u32[]{:S(2)}, u32[]{:S(2)}) collective-permute-start(bf16[1536,512]{1,0:T(8,128)(2,1)} %bitcast.26), channel_id=1, source_target_pairs={{0,64},{64,0},{1,65},{65,1},{2,66},{66,2},{3,67},{67,3},{4,68},{68... | collective-permute-start | bytes 4718600 | tf_op jit(solution)/shard_map/ppermute | solution.py:478
  3.4 17.9 %collective-permute-start.3 = (bf16[2,512,512]{2,1,0:T(8,128)(2,1)}, bf16[2,512,512]{2,1,0:T(8,128)(2,1)}, u32[]{:S(2)}, u32[]{:S(2)}) collective-permute-start(bf16[2,512,512]{2,1,0:T(8,128)(2,1)} %bitcast.27), channel_id=1, source_target_pairs={{0,64},{64,0},{1,65},{65,1},{2,66},{66,2},{3,67},{67,3},{4,68},{68... | collective-permute-start | bytes 3145736 | tf_op jit(solution)/shard_map/ppermute | solution.py:478
  3.8 17.5 %collective-permute-start.4 = (bf16[1024,512]{1,0:T(8,128)(2,1)}, bf16[1024,512]{1,0:T(8,128)(2,1)}, u32[]{:S(2)}, u32[]{:S(2)}) collective-permute-start(bf16[1024,512]{1,0:T(8,128)(2,1)} %bitcast.28), channel_id=1, source_target_pairs={{0,64},{64,0},{1,65},{65,1},{2,66},{66,2},{3,67},{67,3},{4,68},{68... | collective-permute-start | bytes 3145736 | tf_op jit(solution)/shard_map/ppermute | solution.py:478
  3.9 17.4 %collective-permute-start.5 = (bf16[2,512,512]{2,1,0:T(8,128)(2,1)}, bf16[2,512,512]{2,1,0:T(8,128)(2,1)}, u32[]{:S(2)}, u32[]{:S(2)}) collective-permute-start(bf16[2,512,512]{2,1,0:T(8,128)(2,1)} %bitcast.29), channel_id=1, source_target_pairs={{0,64},{64,0},{1,65},{65,1},{2,66},{66,2},{3,67},{67,3},{4,68},{68... | collective-permute-start | bytes 3145736 | tf_op jit(solution)/shard_map/ppermute | solution.py:478
  7.8 23.8 %all-to-all-start = ((bf16[64,8,384]{2,1,0:T(8,128)(2,1)}), bf16[64,8,384]{2,1,0:T(8,128)(2,1)S(1)}, u32[]{:S(2)}, u32[]{:S(2)}) async-start(bf16[64,8,384]{2,1,0:T(8,128)(2,1)} %get-tuple-element.63), calls=%async_computation | async-start | bytes 786432 | tf_op jit(solution)/shard_map/all_to_all | solution.py:482
  21.3 2.2 %collective-permute-start.6 = (f32[16,512]{1,0:T(8,128)}, f32[16,512]{1,0:T(8,128)}, u32[]{:S(2)}, u32[]{:S(2)}) collective-permute-start(f32[16,512]{1,0:T(8,128)} %get-tuple-element.64.refs_10_.refs_11_), channel_id=1, source_target_pairs={{0,64},{64,0},{1,65},{65,1},{2,66},{66,2},{3,67},{67,3},{4,68},{68... | collective-permute-start | bytes 98312 | tf_op jit(solution)/shard_map/ppermute | solution.py:478
  21.3 10.4 %copy-start.2 = (bf16[1,2,768,512]{3,2,1,0:T(8,128)(2,1)}, bf16[1,2,768,512]{3,2,1,0:T(8,128)(2,1)S(1)}, u32[]{:S(2)}) copy-start(bf16[1,2,768,512]{3,2,1,0:T(8,128)(2,1)S(1)} %collective-permute-done.1.refs_12_.refs_13_) | copy-start | bytes 4718596
  21.3 10.4 %copy-start.3 = (bf16[1536,512]{1,0:T(8,128)(2,1)}, bf16[1536,512]{1,0:T(8,128)(2,1)S(1)}, u32[]{:S(2)}) copy-start(bf16[1536,512]{1,0:T(8,128)(2,1)S(1)} %collective-permute-done.2.refs_13_.refs_14_) | copy-start | bytes 4718596
  31.7 0.8 copy-start.6
  49.4 23.4 %collective-permute-start.7 = (bf16[64,72,256]{2,1,0:T(8,128)(2,1)}, bf16[64,72,256]{2,1,0:T(8,128)(2,1)S(1)}, u32[]{:S(2)}, u32[]{:S(2)}) collective-permute-start(bf16[64,72,256]{2,1,0:T(8,128)(2,1)} %get-tuple-element.72), channel_id=1, source_target_pairs={{0,64},{64,0},{1,65},{65,1},{2,66},{66,2},{3,67},{67,3},{4,68},{68... | collective-permute-start | bytes 7077896 | tf_op jit(solution)/shard_map/ppermute | solution.py:478
  49.5 14.8 %all-to-all-start.1 = ((bf16[64,8,128]{2,1,0:T(8,128)(2,1)}), bf16[64,8,128]{2,1,0:T(8,128)(2,1)S(1)}, u32[]{:S(2)}, u32[]{:S(2)}) async-start(bf16[64,8,128]{2,1,0:T(8,128)(2,1)} %get-tuple-element.74), calls=%async_computation.1 | async-start | bytes 262144 | tf_op jit(solution)/shard_map/all_to_all | solution.py:482
  64.2 0.7 copy-start.8
  67.6 14.9 %all-to-all-start.2 = ((bf16[64,8,128]{2,1,0:T(8,128)(2,1)}), bf16[64,8,128]{2,1,0:T(8,128)(2,1)S(1)}, u32[]{:S(2)}, u32[]{:S(2)}) async-start(bf16[64,8,128]{2,1,0:T(8,128)(2,1)} %get-tuple-element.75), calls=%async_computation.2 | async-start | bytes 262144 | tf_op jit(solution)/shard_map/all_to_all | solution.py:482
  82.5 0.7 copy-start.7
  99.9 5.3 %collective-permute-start.8 = (bf16[64,80,256]{2,1,0:T(8,128)(2,1)}, bf16[64,80,256]{2,1,0:T(8,128)(2,1)}, u32[]{:S(2)}, u32[]{:S(2)}) collective-permute-start(bf16[64,80,256]{2,1,0:T(8,128)(2,1)} %get-tuple-element.82), channel_id=1, source_target_pairs={{0,64},{64,0},{1,65},{65,1},{2,66},{66,2},{3,67},{67,3},{4,68},{68... | collective-permute-start | bytes 7864328 | tf_op jit(solution)/shard_map/ppermute | solution.py:478
  100.0 39.4 %all-to-all-start.4 = ((bf16[64,72,256]{2,1,0:T(8,128)(2,1)}), bf16[64,72,256]{2,1,0:T(8,128)(2,1)S(1)}, u32[]{:S(2)}, u32[]{:S(2)}) async-start(bf16[64,72,256]{2,1,0:T(8,128)(2,1)} %add_convert_fusion.1), calls=%async_computation.4 | async-start | bytes 4718592 | tf_op jit(solution)/shard_map/all_to_all | solution.py:482
  110.0 35.5 %copy-start.5 = (bf16[768,512]{1,0:T(8,128)(2,1)S(1)}, bf16[768,512]{1,0:T(8,128)(2,1)}, u32[]{:S(2)}) copy-start(bf16[768,512]{1,0:T(8,128)(2,1)} %get-tuple-element.78) | copy-start | bytes 2359300
  139.4 1.4 copy-start.1
  140.8 41.2 %all-to-all-start.3 = ((bf16[64,80,256]{2,1,0:T(8,128)(2,1)}), bf16[64,80,256]{2,1,0:T(8,128)(2,1)S(1)}, u32[]{:S(2)}, u32[]{:S(2)}) async-start(bf16[64,80,256]{2,1,0:T(8,128)(2,1)} %add_convert_fusion), calls=%async_computation.3 | async-start | bytes 5242880 | tf_op jit(solution)/shard_map/all_to_all | solution.py:482
  145.5 42.9 %collective-permute-start.12 = (bf16[768,512]{1,0:T(8,128)(2,1)S(1)}, bf16[768,512]{1,0:T(8,128)(2,1)}, u32[]{:S(2)}, u32[]{:S(2)}) collective-permute-start(bf16[768,512]{1,0:T(8,128)(2,1)S(1)} %copy-done.5), channel_id=1, source_target_pairs={{0,64},{1,65},{2,66},{3,67},{4,68},{5,69},{6,70},{7,71},{8,72},{9,... | collective-permute-start | bytes 2359304 | tf_op jit(solution)/shard_map/ppermute | solution.py:624
  147.8 40.6 %collective-permute-start.11 = (bf16[768,512]{1,0:T(8,128)(2,1)}, bf16[768,512]{1,0:T(8,128)(2,1)}, u32[]{:S(2)}, u32[]{:S(2)}) collective-permute-start(bf16[768,512]{1,0:T(8,128)(2,1)} %get-tuple-element.89), channel_id=1, source_target_pairs={{64,0},{65,1},{66,2},{67,3},{68,4},{69,5},{70,6},{71,7},{72,8},{73... | collective-permute-start | bytes 2359304 | tf_op jit(solution)/shard_map/ppermute | solution.py:623
  151.9 39.5 %collective-permute-start.10 = (bf16[272,512]{1,0:T(8,128)(2,1)}, bf16[272,512]{1,0:T(8,128)(2,1)}, u32[]{:S(2)}, u32[]{:S(2)}) collective-permute-start(bf16[272,512]{1,0:T(8,128)(2,1)} %get-tuple-element.87.s1), channel_id=1, source_target_pairs={{0,64},{1,65},{2,66},{3,67},{4,68},{5,69},{6,70},{7,71},{8,72},{9,... | collective-permute-start | bytes 835592 | tf_op jit(solution)/shard_map/ppermute | solution.py:627
  182.0 1.5 copy-start
  187.1 4.3 %collective-permute-start.9 = (bf16[272,512]{1,0:T(8,128)(2,1)}, bf16[272,512]{1,0:T(8,128)(2,1)S(1)}, u32[]{:S(2)}, u32[]{:S(2)}) collective-permute-start(bf16[272,512]{1,0:T(8,128)(2,1)} %get-tuple-element.86.s0), channel_id=1, source_target_pairs={{64,0},{65,1},{66,2},{67,3},{68,4},{69,5},{70,6},{71,7},{72,8},{73... | collective-permute-start | bytes 835592 | tf_op jit(solution)/shard_map/ppermute | solution.py:626
  191.4 0.7 copy-start.9

commit v5 on v4

--- a/solution.py
+++ b/solution.py
@@ -607,18 +607,10 @@
     came0 = exchange(paired(keep0, send0))
     sums_out = [shape((80, half), F32), shape((n_rows + 80, width), BF)]
     part1, ship1 = pl.pallas_call(
-        first_kernel,
-        out_shape=sums_out,
-        in_specs=[VM] * 2,
-        out_specs=[VM] * 2,
-        name="sums1",
+        first_kernel, out_shape=sums_out, in_specs=[VM] * 2, out_specs=[VM] * 2, name="sums1"
     )(came1, node1)
     part0, ship0 = pl.pallas_call(
-        sum_kernel,
-        out_shape=sums_out,
-        in_specs=[VM] * 3,
-        out_specs=[VM] * 2,
-        name="sums0",
+        sum_kernel, out_shape=sums_out, in_specs=[VM] * 3, out_specs=[VM] * 2, name="sums0"
     )(idx, local0, came0)
     lower = lax.ppermute(edge0, "pipe", down)
     upper = lax.ppermute(edge1, "pipe", up)

time: 198 us -> 198 us (level)
  no operation moved by 1% of the time
where the time goes in v5:
time: 198 us; the launch traced here: 195 us
  waiting for transfers between devices  78.5 us (40%)
  Pallas kernels  48.4 us (24%)
  starting transfers between devices  42.6 us (22%)
  other arithmetic  12.3 us (6%)
  local copies, waits for them, and re-layouts  10.4 us (5%)
  between operations  2.34 us (1%)
    all_to_all x5, waiting for transfers between devices, exchange(): return lax.all_to_all(x, 'dom', split_axis=0, concat_axis=0, tiled=True)  78.4 us
    pallas_call x2, Pallas kernels, run(): pl.pallas_call(functools.partial(unit_kernel, layer), out_shape=outs, in_...  33.6 us
    all_to_all x5, starting transfers between devices, exchange(): return lax.all_to_all(x, 'dom', split_axis=0, concat_axis=0, tiled=True)  31.3 us
    convert_element_type x2, other arithmetic, paired(): return (keep.astype(F32) + swap(send).astype(F32)).astype(BF)  8.51 us
    unnamed x20, local copies, waits for them, and re-layouts  5.72 us
    ppermute x1, starting transfers between devices, body(): r1 = lax.ppermute(ship1, 'pipe', up)  4.63 us
  transfers between devices with their start and end apart: 18, of which 5 were waited for; matrix products, arithmetic and copies ran while one was open for 9% of the time, Pallas kernels for 7%

profile of v5, /device:TPU:0, one launch (start us, length us, event | category | flops | bytes accessed | tf_op | source)
XLA Modules:
  0.0 194.5 jit_solution(11441415130125155707)
XLA Ops:
  0.6 0.1 collective-permute-start
  0.7 0.7 slice_bitcast_fusion.2
  1.4 0.8 slice_bitcast_fusion
  2.2 0.6 stack.57.idx.refs_1_
  2.8 0.0 collective-permute-done.rec_all.refs_11_.refs_12_
  2.8 0.5 collective-permute-start.1
  3.3 0.1 collective-permute-start.2
  3.4 0.4 collective-permute-start.3
  3.8 0.1 collective-permute-start.4
  3.9 0.4 collective-permute-start.5
  4.3 0.0 copy-done.4
  4.3 3.5 %pre.1 = (bf16[64,8,384]{2,1,0:T(8,128)(2,1)}, f32[16,512]{1,0:T(8,128)}) custom-call(s32[1]{0:T(128)} %bitcast.core, s32[8,64]{1,0:T(8,128)} %stack.57.idx.refs_1_, f32[1,4,512]{2,1,0:T(4,128)} %eb.1, f32[1,512]{1,0:T(1,128)} %eg.1, f32[1,4,512]{2,1,0:T(4,128)} %nb.1, f32[1,512]{1,0:T(1,128)} %ng.1, bf16[1,2,192,512]{3,2,1,0:T(8,128)(2,1)} %refs_5_.3, ...), custom_call_target="tpu_custom_call" | custom-call | tf_op jit(solution)/shard_map/pre/pallas_call | solution.py:502
  7.8 11.5 %all-to-all-start = ((bf16[64,8,384]{2,1,0:T(8,128)(2,1)}), bf16[64,8,384]{2,1,0:T(8,128)(2,1)S(1)}, u32[]{:S(2)}, u32[]{:S(2)}) async-start(bf16[64,8,384]{2,1,0:T(8,128)(2,1)} %get-tuple-element.63), calls=%async_computation | async-start | bytes 786432 | tf_op jit(solution)/shard_map/all_to_all | solution.py:482
  20.7 0.6 stack.66.refs_0_
  21.3 0.0 collective-permute-done.3.refs_14_.refs_15_
  21.3 0.0 collective-permute-start.6
  21.3 0.0 collective-permute-done.4.refs_15_.refs_16_
  21.3 0.0 collective-permute-done.5.refs_16_.refs_17_
  21.3 0.0 collective-permute-done.1.refs_12_.refs_13_
  21.3 0.0 copy-start.2
  21.3 0.0 collective-permute-done.2.refs_13_.refs_14_
  21.3 0.0 copy-start.3
  21.3 0.7 fusion.4
  22.1 0.7 stack.62
  22.8 0.7 stack.63.refs_2_
  23.5 0.0 collective-permute-done.6.refs_17_.refs_18_
  23.5 8.2 %all-to-all-done.refs_3_ = bf16[64,8,384]{2,1,0:T(8,128)(2,1)S(1)} async-done(((bf16[64,8,384]{2,1,0:T(8,128)(2,1)}), bf16[64,8,384]{2,1,0:T(8,128)(2,1)S(1)}, u32[]{:S(2)}, u32[]{:S(2)}) %all-to-all-start) | async-done | bytes 393248 | tf_op jit(solution)/shard_map/all_to_all | solution.py:482
  31.7 0.0 copy-done.2
  31.7 0.8 copy-done.6
  32.5 16.9 %shard_map.258 = (f32[192,512]{1,0:T(8,128)}, bf16[768,512]{1,0:T(8,128)(2,1)}, bf16[64,72,256]{2,1,0:T(8,128)(2,1)}, bf16[64,72,256]{2,1,0:T(8,128)(2,1)}, bf16...) custom-call(s32[5]{0:T(128)} %stack.66.refs_0_, s32[8,64]{1,0:T(8,128)} %stack.57.idx.refs_1_, ...), custom_call_target="tpu_custom_call" | custom-call | tf_op jit(solution)/shard_map/pallas_call | solution.py:575
  49.4 0.1 collective-permute-start.7
  49.5 4.7 %all-to-all-start.1 = ((bf16[64,8,128]{2,1,0:T(8,128)(2,1)}), bf16[64,8,128]{2,1,0:T(8,128)(2,1)S(1)}, u32[]{:S(2)}, u32[]{:S(2)}) async-start(bf16[64,8,128]{2,1,0:T(8,128)(2,1)} %get-tuple-element.74), calls=%async_computation.1 | async-start | bytes 262144 | tf_op jit(solution)/shard_map/all_to_all | solution.py:482
  54.2 0.6 stack.60.refs_0_
  54.8 9.4 %all-to-all-done.1.came = bf16[64,8,128]{2,1,0:T(8,128)(2,1)S(1)} async-done(((bf16[64,8,128]{2,1,0:T(8,128)(2,1)}), bf16[64,8,128]{2,1,0:T(8,128)(2,1)S(1)}, u32[]{:S(2)}, u32[]{:S(2)}) %all-to-all-start.1) | async-done | bytes 131104 | tf_op jit(solution)/shard_map/all_to_all | solution.py:482
  64.2 0.7 copy-done.8
  64.9 2.8 %post.1 = (bf16[192,512]{1,0:T(8,128)(2,1)}, bf16[64,8,128]{2,1,0:T(8,128)(2,1)}) custom-call(s32[8,64]{1,0:T(8,128)} %stack.57.idx.refs_1_, f32[192,512]{1,0:T(8,128)} %get-tuple-element.73.local, bf16[64,8,128]{2,1,0:T(8,128)(2,1)} %copy-done.8), custom_call_target="tpu_custom_call" | custom-call | tf_op jit(solution)/shard_map/post/pallas_call | solution.py:597
  67.6 5.1 %all-to-all-start.2 = ((bf16[64,8,128]{2,1,0:T(8,128)(2,1)}), bf16[64,8,128]{2,1,0:T(8,128)(2,1)S(1)}, u32[]{:S(2)}, u32[]{:S(2)}) async-start(bf16[64,8,128]{2,1,0:T(8,128)(2,1)} %get-tuple-element.75), calls=%async_computation.2 | async-start | bytes 262144 | tf_op jit(solution)/shard_map/all_to_all | solution.py:482
  72.8 0.0 collective-permute-done.7
  72.8 3.7 %add_convert_fusion.1 = bf16[64,72,256]{2,1,0:T(8,128)(2,1)} fusion(bf16[64,72,256]{2,1,0:T(8,128)(2,1)S(1)} %collective-permute-done.7, bf16[64,72,256]{2,1,0:T(8,128)(2,1)} %get-tuple-element.71), kind=kLoop, calls=%fused_computation.1 | loop fusion | flops 4718592 | bytes 7077888 | tf_op jit(solution)/shard_map/convert_element_type | solution.py:594
  76.6 6.0 %all-to-all-done.2.refs_4_ = bf16[64,8,128]{2,1,0:T(8,128)(2,1)S(1)} async-done(((bf16[64,8,128]{2,1,0:T(8,128)(2,1)}), bf16[64,8,128]{2,1,0:T(8,128)(2,1)S(1)}, u32[]{:S(2)}, u32[]{:S(2)}) %all-to-all-start.2) | async-done | bytes 131104 | tf_op jit(solution)/shard_map/all_to_all | solution.py:482
  82.5 0.6 copy-done.7
  83.2 16.7 %shard_map.259 = (f32[192,512]{1,0:T(8,128)}, bf16[768,512]{1,0:T(8,128)(2,1)}, bf16[64,80,256]{2,1,0:T(8,128)(2,1)}, bf16[64,80,256]{2,1,0:T(8,128)(2,1)}) custom-call(s32[5]{0:T(128)} %stack.60.refs_0_, s32[8,64]{1,0:T(8,128)} %stack.57.idx.refs_1_, s32[8,768]{1,0:T(8,128)} %stack.63.refs_2_, bf16[128,512]{1,0:T(8,128)(2,1)} %get-tuple-element.70.refs_3_, ...), custom_call_target="tpu_custom_call" | custom-call | tf_op jit(solution)/shard_map/pallas_call | solution.py:575
  99.9 0.1 collective-permute-start.8
  100.0 5.2 %all-to-all-start.4 = ((bf16[64,72,256]{2,1,0:T(8,128)(2,1)}), bf16[64,72,256]{2,1,0:T(8,128)(2,1)S(1)}, u32[]{:S(2)}, u32[]{:S(2)}) async-start(bf16[64,72,256]{2,1,0:T(8,128)(2,1)} %add_convert_fusion.1), calls=%async_computation.4 | async-start | bytes 4718592 | tf_op jit(solution)/shard_map/all_to_all | solution.py:482
  105.2 0.0 collective-permute-done.8
  105.2 4.8 %add_convert_fusion = bf16[64,80,256]{2,1,0:T(8,128)(2,1)} fusion(bf16[64,80,256]{2,1,0:T(8,128)(2,1)} %collective-permute-done.8, bf16[64,80,256]{2,1,0:T(8,128)(2,1)} %get-tuple-element.81), kind=kLoop, calls=%fused_computation | loop fusion | flops 5242880 | bytes 7864320 | tf_op jit(solution)/shard_map/convert_element_type | solution.py:594
  110.0 29.4 %all-to-all-done.4.came = bf16[64,72,256]{2,1,0:T(8,128)(2,1)S(1)} async-done(((bf16[64,72,256]{2,1,0:T(8,128)(2,1)}), bf16[64,72,256]{2,1,0:T(8,128)(2,1)S(1)}, u32[]{:S(2)}, u32[]{:S(2)}) %all-to-all-start.4) | async-done | bytes 2359328 | tf_op jit(solution)/shard_map/all_to_all | solution.py:482
  139.4 1.4 copy-done.1
  140.8 4.7 %all-to-all-start.3 = ((bf16[64,80,256]{2,1,0:T(8,128)(2,1)}), bf16[64,80,256]{2,1,0:T(8,128)(2,1)S(1)}, u32[]{:S(2)}, u32[]{:S(2)}) async-start(bf16[64,80,256]{2,1,0:T(8,128)(2,1)} %add_convert_fusion), calls=%async_computation.3 | async-start | bytes 5242880 | tf_op jit(solution)/shard_map/all_to_all | solution.py:482
  145.5 2.3 %collective-permute-start.12 = (bf16[768,512]{1,0:T(8,128)(2,1)S(1)}, bf16[768,512]{1,0:T(8,128)(2,1)}, u32[]{:S(2)}, u32[]{:S(2)}) collective-permute-start(bf16[768,512]{1,0:T(8,128)(2,1)S(1)} %copy-done.5), channel_id=1, source_target_pairs={{0,64},{1,65},{2,66},{3,67},{4,68},{5,69},{6,70},{7,71},{8,72},{9,... | collective-permute-start | bytes 2359304 | tf_op jit(solution)/shard_map/ppermute | solution.py:616
  147.8 1.3 collective-permute-start.11
  149.1 2.8 %sums1.1 = (f32[80,256]{1,0:T(8,128)}, bf16[272,512]{1,0:T(8,128)(2,1)}) custom-call(bf16[64,72,256]{2,1,0:T(8,128)(2,1)} %copy-done.1, bf16[192,512]{1,0:T(8,128)(2,1)} %get-tuple-element.77.node), custom_call_target="tpu_custom_call" | custom-call | tf_op jit(solution)/shard_map/sums1/pallas_call | solution.py:609
  151.9 4.6 %collective-permute-start.10 = (bf16[272,512]{1,0:T(8,128)(2,1)}, bf16[272,512]{1,0:T(8,128)(2,1)}, u32[]{:S(2)}, u32[]{:S(2)}) collective-permute-start(bf16[272,512]{1,0:T(8,128)(2,1)} %get-tuple-element.87.s1), channel_id=1, source_target_pairs={{0,64},{1,65},{2,66},{3,67},{4,68},{5,69},{6,70},{7,71},{8,72},{9,... | collective-permute-start | bytes 835592 | tf_op jit(solution)/shard_map/ppermute | solution.py:619
  156.5 25.4 %all-to-all-done.3.came = bf16[64,80,256]{2,1,0:T(8,128)(2,1)S(1)} async-done(((bf16[64,80,256]{2,1,0:T(8,128)(2,1)}), bf16[64,80,256]{2,1,0:T(8,128)(2,1)S(1)}, u32[]{:S(2)}, u32[]{:S(2)}) %all-to-all-start.3) | async-done | bytes 2621472 | tf_op jit(solution)/shard_map/all_to_all | solution.py:482
  182.0 1.5 copy-done
  183.5 3.6 %sums0.1 = (f32[80,256]{1,0:T(8,128)}, bf16[272,512]{1,0:T(8,128)(2,1)}) custom-call(s32[8,64]{1,0:T(8,128)} %stack.57.idx.refs_1_, f32[192,512]{1,0:T(8,128)} %get-tuple-element.80.local, bf16[64,80,256]{2,1,0:T(8,128)(2,1)} %copy-done), custom_call_target="tpu_custom_call" | custom-call | tf_op jit(solution)/shard_map/sums0/pallas_call | solution.py:612
  187.1 1.3 collective-permute-start.9
  188.4 0.0 collective-permute-done.12
  188.4 0.0 collective-permute-done.11
  188.4 3.0 %maximum_select_fusion = bf16[1,2,768,512]{3,2,1,0:T(8,128)(2,1)} fusion(bf16[1,1,768,512]{3,2,1,0:T(8,128)(2,1)} %bitcast.18, bf16[1,1,768,512]{3,2,1,0:T(8,128)(2,1)} %bitcast.33, bf16[1,1,768,512]{3,2,1,0:T(8,128)(2,1)S(1)} %bitcast.31, bf16[1,1,768,512]{3,2,1,0:T(8,128)(2,1)} %bitcast.19, pred[]{:T(512)S(6)} %eq.9), kind=kLoop, calls=%fused_computation.2 | loop fusion | flops 2359296 | bytes 4718593 | tf_op jit(solution)/shard_map/jit(_where)/select_n | solution.py:617
  191.4 0.0 collective-permute-done.10.r1
  191.4 0.0 collective-permute-done.9.r0
  191.4 0.7 copy-done.9
  192.1 2.2 %end.1 = (bf16[1,2,192,512]{3,2,1,0:T(8,128)(2,1)}, f32[1,24,512]{2,1,0:T(8,128)}, f32[1,2,8,512]{3,2,1,0:T(8,128)}, f32[1,4,8]{2,1,0:T(4,128)}, f32[1,8]{1,0:T(...) custom-call(s32[1]{0:T(128)} %bitcast.core, ...), custom_call_target="tpu_custom_call" | custom-call | tf_op jit(solution)/shard_map/end/pallas_call | solution.py:620
  (11 shorter events, 0.0 us)
Async XLA Ops:
  0.6 2.2 %collective-permute-start = (bf16[1,2,192,512]{3,2,1,0:T(8,128)(2,1)}, bf16[1,2,192,512]{3,2,1,0:T(8,128)(2,1)S(1)}, u32[]{:S(2)}, u32[]{:S(2)}) collective-permute-start(bf16[1,2,192,512]{3,2,1,0:T(8,128)(2,1)} %refs_5_.3), channel_id=1, source_target_pairs={{0,64},{64,0},{1,65},{65,1},{2,66},{66,2},{3,67},{67,3},{4,68},{68... | collective-permute-start | bytes 1179656 | tf_op jit(solution)/shard_map/ppermute | solution.py:478
  2.8 1.5 copy-start.4
  2.8 18.5 %collective-permute-start.1 = (bf16[1,2,768,512]{3,2,1,0:T(8,128)(2,1)}, bf16[1,2,768,512]{3,2,1,0:T(8,128)(2,1)S(1)}, u32[]{:S(2)}, u32[]{:S(2)}) collective-permute-start(bf16[1,2,768,512]{3,2,1,0:T(8,128)(2,1)} %refs_6_.3), channel_id=1, source_target_pairs={{0,64},{64,0},{1,65},{65,1},{2,66},{66,2},{3,67},{67,3},{4,68},{68... | collective-permute-start | bytes 4718600 | tf_op jit(solution)/shard_map/ppermute | solution.py:478
  3.3 18.0 %collective-permute-start.2 = (bf16[1536,512]{1,0:T(8,128)(2,1)}, bf16[1536,512]{1,0:T(8,128)(2,1)S(1)}, u32[]{:S(2)}, u32[]{:S(2)}) collective-permute-start(bf16[1536,512]{1,0:T(8,128)(2,1)} %bitcast.26), channel_id=1, source_target_pairs={{0,64},{64,0},{1,65},{65,1},{2,66},{66,2},{3,67},{67,3},{4,68},{68... | collective-permute-start | bytes 4718600 | tf_op jit(solution)/shard_map/ppermute | solution.py:478
  3.4 17.9 %collective-permute-start.3 = (bf16[2,512,512]{2,1,0:T(8,128)(2,1)}, bf16[2,512,512]{2,1,0:T(8,128)(2,1)}, u32[]{:S(2)}, u32[]{:S(2)}) collective-permute-start(bf16[2,512,512]{2,1,0:T(8,128)(2,1)} %bitcast.27), channel_id=1, source_target_pairs={{0,64},{64,0},{1,65},{65,1},{2,66},{66,2},{3,67},{67,3},{4,68},{68... | collective-permute-start | bytes 3145736 | tf_op jit(solution)/shard_map/ppermute | solution.py:478
  3.8 17.5 %collective-permute-start.4 = (bf16[1024,512]{1,0:T(8,128)(2,1)}, bf16[1024,512]{1,0:T(8,128)(2,1)}, u32[]{:S(2)}, u32[]{:S(2)}) collective-permute-start(bf16[1024,512]{1,0:T(8,128)(2,1)} %bitcast.28), channel_id=1, source_target_pairs={{0,64},{64,0},{1,65},{65,1},{2,66},{66,2},{3,67},{67,3},{4,68},{68... | collective-permute-start | bytes 3145736 | tf_op jit(solution)/shard_map/ppermute | solution.py:478
  3.9 17.4 %collective-permute-start.5 = (bf16[2,512,512]{2,1,0:T(8,128)(2,1)}, bf16[2,512,512]{2,1,0:T(8,128)(2,1)}, u32[]{:S(2)}, u32[]{:S(2)}) collective-permute-start(bf16[2,512,512]{2,1,0:T(8,128)(2,1)} %bitcast.29), channel_id=1, source_target_pairs={{0,64},{64,0},{1,65},{65,1},{2,66},{66,2},{3,67},{67,3},{4,68},{68... | collective-permute-start | bytes 3145736 | tf_op jit(solution)/shard_map/ppermute | solution.py:478
  7.8 23.8 %all-to-all-start = ((bf16[64,8,384]{2,1,0:T(8,128)(2,1)}), bf16[64,8,384]{2,1,0:T(8,128)(2,1)S(1)}, u32[]{:S(2)}, u32[]{:S(2)}) async-start(bf16[64,8,384]{2,1,0:T(8,128)(2,1)} %get-tuple-element.63), calls=%async_computation | async-start | bytes 786432 | tf_op jit(solution)/shard_map/all_to_all | solution.py:482
  21.3 2.2 %collective-permute-start.6 = (f32[16,512]{1,0:T(8,128)}, f32[16,512]{1,0:T(8,128)}, u32[]{:S(2)}, u32[]{:S(2)}) collective-permute-start(f32[16,512]{1,0:T(8,128)} %get-tuple-element.64.refs_10_.refs_11_), channel_id=1, source_target_pairs={{0,64},{64,0},{1,65},{65,1},{2,66},{66,2},{3,67},{67,3},{4,68},{68... | collective-permute-start | bytes 98312 | tf_op jit(solution)/shard_map/ppermute | solution.py:478
  21.3 10.4 %copy-start.2 = (bf16[1,2,768,512]{3,2,1,0:T(8,128)(2,1)}, bf16[1,2,768,512]{3,2,1,0:T(8,128)(2,1)S(1)}, u32[]{:S(2)}) copy-start(bf16[1,2,768,512]{3,2,1,0:T(8,128)(2,1)S(1)} %collective-permute-done.1.refs_12_.refs_13_) | copy-start | bytes 4718596
  21.3 10.4 %copy-start.3 = (bf16[1536,512]{1,0:T(8,128)(2,1)}, bf16[1536,512]{1,0:T(8,128)(2,1)S(1)}, u32[]{:S(2)}) copy-start(bf16[1536,512]{1,0:T(8,128)(2,1)S(1)} %collective-permute-done.2.refs_13_.refs_14_) | copy-start | bytes 4718596
  31.7 0.8 copy-start.6
  49.4 23.4 %collective-permute-start.7 = (bf16[64,72,256]{2,1,0:T(8,128)(2,1)}, bf16[64,72,256]{2,1,0:T(8,128)(2,1)S(1)}, u32[]{:S(2)}, u32[]{:S(2)}) collective-permute-start(bf16[64,72,256]{2,1,0:T(8,128)(2,1)} %get-tuple-element.72), channel_id=1, source_target_pairs={{0,64},{64,0},{1,65},{65,1},{2,66},{66,2},{3,67},{67,3},{4,68},{68... | collective-permute-start | bytes 7077896 | tf_op jit(solution)/shard_map/ppermute | solution.py:478
  49.5 14.8 %all-to-all-start.1 = ((bf16[64,8,128]{2,1,0:T(8,128)(2,1)}), bf16[64,8,128]{2,1,0:T(8,128)(2,1)S(1)}, u32[]{:S(2)}, u32[]{:S(2)}) async-start(bf16[64,8,128]{2,1,0:T(8,128)(2,1)} %get-tuple-element.74), calls=%async_computation.1 | async-start | bytes 262144 | tf_op jit(solution)/shard_map/all_to_all | solution.py:482
  64.2 0.7 copy-start.8
  67.6 14.9 %all-to-all-start.2 = ((bf16[64,8,128]{2,1,0:T(8,128)(2,1)}), bf16[64,8,128]{2,1,0:T(8,128)(2,1)S(1)}, u32[]{:S(2)}, u32[]{:S(2)}) async-start(bf16[64,8,128]{2,1,0:T(8,128)(2,1)} %get-tuple-element.75), calls=%async_computation.2 | async-start | bytes 262144 | tf_op jit(solution)/shard_map/all_to_all | solution.py:482
  82.5 0.7 copy-start.7
  99.9 5.3 %collective-permute-start.8 = (bf16[64,80,256]{2,1,0:T(8,128)(2,1)}, bf16[64,80,256]{2,1,0:T(8,128)(2,1)}, u32[]{:S(2)}, u32[]{:S(2)}) collective-permute-start(bf16[64,80,256]{2,1,0:T(8,128)(2,1)} %get-tuple-element.82), channel_id=1, source_target_pairs={{0,64},{64,0},{1,65},{65,1},{2,66},{66,2},{3,67},{67,3},{4,68},{68... | collective-permute-start | bytes 7864328 | tf_op jit(solution)/shard_map/ppermute | solution.py:478
  100.0 39.4 %all-to-all-start.4 = ((bf16[64,72,256]{2,1,0:T(8,128)(2,1)}), bf16[64,72,256]{2,1,0:T(8,128)(2,1)S(1)}, u32[]{:S(2)}, u32[]{:S(2)}) async-start(bf16[64,72,256]{2,1,0:T(8,128)(2,1)} %add_convert_fusion.1), calls=%async_computation.4 | async-start | bytes 4718592 | tf_op jit(solution)/shard_map/all_to_all | solution.py:482
  110.0 35.5 %copy-start.5 = (bf16[768,512]{1,0:T(8,128)(2,1)S(1)}, bf16[768,512]{1,0:T(8,128)(2,1)}, u32[]{:S(2)}) copy-start(bf16[768,512]{1,0:T(8,128)(2,1)} %get-tuple-element.78) | copy-start | bytes 2359300
  139.4 1.4 copy-start.1
  140.8 41.2 %all-to-all-start.3 = ((bf16[64,80,256]{2,1,0:T(8,128)(2,1)}), bf16[64,80,256]{2,1,0:T(8,128)(2,1)S(1)}, u32[]{:S(2)}, u32[]{:S(2)}) async-start(bf16[64,80,256]{2,1,0:T(8,128)(2,1)} %add_convert_fusion), calls=%async_computation.3 | async-start | bytes 5242880 | tf_op jit(solution)/shard_map/all_to_all | solution.py:482
  145.5 42.9 %collective-permute-start.12 = (bf16[768,512]{1,0:T(8,128)(2,1)S(1)}, bf16[768,512]{1,0:T(8,128)(2,1)}, u32[]{:S(2)}, u32[]{:S(2)}) collective-permute-start(bf16[768,512]{1,0:T(8,128)(2,1)S(1)} %copy-done.5), channel_id=1, source_target_pairs={{0,64},{1,65},{2,66},{3,67},{4,68},{5,69},{6,70},{7,71},{8,72},{9,... | collective-permute-start | bytes 2359304 | tf_op jit(solution)/shard_map/ppermute | solution.py:616
  147.8 40.6 %collective-permute-start.11 = (bf16[768,512]{1,0:T(8,128)(2,1)}, bf16[768,512]{1,0:T(8,128)(2,1)}, u32[]{:S(2)}, u32[]{:S(2)}) collective-permute-start(bf16[768,512]{1,0:T(8,128)(2,1)} %get-tuple-element.89), channel_id=1, source_target_pairs={{64,0},{65,1},{66,2},{67,3},{68,4},{69,5},{70,6},{71,7},{72,8},{73... | collective-permute-start | bytes 2359304 | tf_op jit(solution)/shard_map/ppermute | solution.py:615
  151.9 39.5 %collective-permute-start.10 = (bf16[272,512]{1,0:T(8,128)(2,1)}, bf16[272,512]{1,0:T(8,128)(2,1)}, u32[]{:S(2)}, u32[]{:S(2)}) collective-permute-start(bf16[272,512]{1,0:T(8,128)(2,1)} %get-tuple-element.87.s1), channel_id=1, source_target_pairs={{0,64},{1,65},{2,66},{3,67},{4,68},{5,69},{6,70},{7,71},{8,72},{9,... | collective-permute-start | bytes 835592 | tf_op jit(solution)/shard_map/ppermute | solution.py:619
  182.0 1.5 copy-start
  187.1 4.3 %collective-permute-start.9 = (bf16[272,512]{1,0:T(8,128)(2,1)}, bf16[272,512]{1,0:T(8,128)(2,1)S(1)}, u32[]{:S(2)}, u32[]{:S(2)}) collective-permute-start(bf16[272,512]{1,0:T(8,128)(2,1)} %get-tuple-element.86.s0), channel_id=1, source_target_pairs={{64,0},{65,1},{66,2},{67,3},{68,4},{69,5},{70,6},{71,7},{72,8},{73... | collective-permute-start | bytes 835592 | tf_op jit(solution)/shard_map/ppermute | solution.py:618
  191.4 0.7 copy-start.9
